TPU v7x, 32 devices: a whole 2x2x4 slice. The times are simulated.
32 devices in a mesh: dp: 4 (over x, core), ctx: 4 (over z), tp: 2 (over y).
Axes of the slice: x: 2, y: 2, z: 4, core: 2. Of those that a mesh axis runs over, the one named last changes fastest.
Arguments:
- tokens: bfloat16 [8192, 2048], P(('dp', 'ctx')), may hold values from -12 to 12, as said below
- gain_one: bfloat16 [2048], P(('dp', 'ctx')), may hold values from 0.099609375 to 1.8984375
- bias_one: bfloat16 [2048], P(('dp', 'ctx')), may hold values from -3 to 3
- w_query: bfloat16 [2048, 2048], P(('dp', 'ctx'), 'tp'), may hold values from -1 to 1, as said below
- w_keyval: bfloat16 [2048, 256], P(('dp', 'ctx')), may hold values from -0.125 to 0.125
- w_out: bfloat16 [2048, 2048], P(('dp', 'ctx'), 'tp'), may hold values from -2 to 2
- gain_two: bfloat16 [2048], P(('dp', 'ctx')), may hold values from 0.099609375 to 1.8984375
- bias_two: bfloat16 [2048], P(('dp', 'ctx')), may hold values from -3 to 3
- w_up: bfloat16 [2048, 8192], P(('dp', 'ctx'), 'tp'), may hold values from -1 to 1, as said below
- w_down: bfloat16 [2048, 8192], P(('dp', 'ctx'), 'tp'), may hold values from -0.0625 to 0.0625
- grad_out: bfloat16 [8192, 2048], P(('dp', 'ctx')), may hold values from -6 to 6
Outputs:
- layer_out: bfloat16 [8192, 2048], P(('dp', 'ctx'))
- input_grad: float32 [8192, 2048], P(('dp', 'ctx'))
- grad_gain_one: float32 [2048], P(('dp', 'ctx'))
- grad_bias_one: float32 [2048], P(('dp', 'ctx'))
- grad_query: float32 [2048, 2048], P(('dp', 'ctx'), 'tp')
- grad_keyval: float32 [2048, 256], P(('dp', 'ctx'))
- grad_out_proj: float32 [2048, 2048], P(('dp', 'ctx'), 'tp')
- grad_gain_two: float32 [2048], P(('dp', 'ctx'))
- grad_bias_two: float32 [2048], P(('dp', 'ctx'))
- grad_up: float32 [2048, 8192], P(('dp', 'ctx'), 'tp')
- grad_down: float32 [2048, 8192], P(('dp', 'ctx'), 'tp')
- rms_values: float32 [3], replicated
Inputs may be any that keep to these rules, and one draw needn't show every extreme that they name: `tokens`: real-valued activations. `w_query`: real-valued projection weights. `w_up`: real-valued projection weights.
All inputs are finite; a program needn't handle non-finite values.
Results may differ from a plain program's by a relative error of at most 0.015.
Values may be sent and summed in bfloat16 or wider, within the bound.
No kernel may reach another device: no remote copies, remote signals or barrier semaphores. Data moves between devices by JAX's collectives and lax.ppermute only.
A program may use at most 256 MiB of HBM per device.

v0:
```python
import jax
import jax.numpy as jnp
from jax import lax
from jax.sharding import PartitionSpec as P

BLOCK = 256


eps_norm = 1e-05
neg_large = -1e30


def layer_norm(values, gain, shift):
    center = values - jnp.mean(values, axis=-1, keepdims=True)
    spread = jnp.mean(center * center, axis=-1, keepdims=True)
    return center * lax.rsqrt(spread + eps_norm) * gain + shift


def gelu_tanh(values):
    return jax.nn.gelu(values, approximate=True)


def last_dot(left, right):
    return lax.dot_general(
        left, right, (((1,), (1,)), ((), ())), preferred_element_type=jnp.float32
    )


def first_dot(left, right):
    return lax.dot_general(
        left, right, (((0,), (0,)), ((), ())), preferred_element_type=jnp.float32
    )


def body(
    tokens, gain_one, bias_one, w_query, w_keyval, w_out, gain_two, bias_two, w_up, w_down, grad_out
):
    rows = tokens.shape[0]
    width = tokens.shape[1]
    head_size = w_keyval.shape[1] // 2
    local_heads = w_query.shape[1] // head_size
    scale = head_size ** (-0.5)
    ctx_index = lax.axis_index("ctx")
    tile_count = ctx_index + 1
    stream = tokens.astype(jnp.float32)
    full_gain_one, full_bias_one, query_full, keyval_full, out_full = (
        lax.all_gather(gain_one, ("dp", "ctx"), axis=0, tiled=True),
        lax.all_gather(bias_one, ("dp", "ctx"), axis=0, tiled=True),
        lax.all_gather(w_query, ("dp", "ctx"), axis=0, tiled=True),
        lax.all_gather(w_keyval, ("dp", "ctx"), axis=0, tiled=True),
        lax.all_gather(w_out, ("dp", "ctx"), axis=0, tiled=True),
    )
    normed_one, norm_one_pull = jax.vjp(
        layer_norm, stream, full_gain_one.astype(jnp.float32), full_bias_one.astype(jnp.float32)
    )
    normed_low = normed_one.astype(jnp.bfloat16)
    queries = jnp.dot(normed_low, query_full, preferred_element_type=jnp.float32).astype(
        jnp.bfloat16
    )
    keyvals = jnp.dot(normed_low, keyval_full, preferred_element_type=jnp.float32).astype(
        jnp.bfloat16
    )
    keyval_all = lax.all_gather(keyvals, "ctx", axis=0, tiled=True)
    keys_all = keyval_all[:, :head_size]
    values_all = keyval_all[:, head_size:]
    query_heads = queries.reshape(rows, local_heads, head_size)
    query_block = (ctx_index * rows + jnp.arange(rows, dtype=jnp.int32)) // BLOCK

    def tile_scores(tile):
        start = tile * rows
        key_tile = lax.dynamic_slice_in_dim(keys_all, start, rows, 0)
        value_tile = lax.dynamic_slice_in_dim(values_all, start, rows, 0)
        scores = (
            jnp.einsum("qhd,kd->hqk", query_heads, key_tile, preferred_element_type=jnp.float32)
            * scale
        )
        key_block = (start + jnp.arange(rows, dtype=jnp.int32)) // BLOCK
        allowed = (key_block[None, :] <= query_block[:, None])[None]
        return (scores, allowed, key_tile, value_tile)

    def max_step(tile, carry):
        run_max, run_sum = carry
        scores, allowed, key_tile, value_tile = tile_scores(tile)
        masked = jnp.where(allowed, scores, neg_large)
        new_max = jnp.maximum(run_max, jnp.max(masked, axis=-1))
        run_sum = run_sum * jnp.exp(run_max - new_max) + jnp.sum(
            jnp.exp(masked - new_max[..., None]), axis=-1
        )
        return (new_max, run_sum)

    start_max = jnp.full((local_heads, rows), neg_large, jnp.float32)
    start_sum = jnp.zeros((local_heads, rows), jnp.float32)
    row_max, row_sum = lax.fori_loop(0, tile_count, max_step, (start_max, start_sum))
    log_total = row_max + jnp.log(row_sum)

    def value_step(tile, accum):
        scores, allowed, key_tile, value_tile = tile_scores(tile)
        probs = jnp.where(allowed, jnp.exp(scores - log_total[..., None]), 0.0)
        return accum + jnp.einsum(
            "hqk,kd->qhd",
            probs.astype(jnp.bfloat16),
            value_tile,
            preferred_element_type=jnp.float32,
        )

    attn_accum = lax.fori_loop(
        0, tile_count, value_step, jnp.zeros((rows, local_heads, head_size), jnp.float32)
    )
    attn_low = attn_accum.reshape(rows, local_heads * head_size).astype(jnp.bfloat16)
    branch_attn = lax.psum(last_dot(attn_low, out_full).astype(jnp.bfloat16), "tp").astype(
        jnp.float32
    )
    hidden = stream + branch_attn
    full_gain_two, full_bias_two, up_full, down_full = (
        lax.all_gather(gain_two, ("dp", "ctx"), axis=0, tiled=True),
        lax.all_gather(bias_two, ("dp", "ctx"), axis=0, tiled=True),
        lax.all_gather(w_up, ("dp", "ctx"), axis=0, tiled=True),
        lax.all_gather(w_down, ("dp", "ctx"), axis=0, tiled=True),
    )
    normed_two, norm_two_pull = jax.vjp(
        layer_norm, hidden, full_gain_two.astype(jnp.float32), full_bias_two.astype(jnp.float32)
    )
    normed_two_low = normed_two.astype(jnp.bfloat16)
    pre_act = jnp.dot(normed_two_low, up_full, preferred_element_type=jnp.float32)
    act_value, gelu_pull = jax.vjp(gelu_tanh, pre_act)
    act_low = act_value.astype(jnp.bfloat16)
    branch_mlp = lax.psum(last_dot(act_low, down_full).astype(jnp.bfloat16), "tp").astype(
        jnp.float32
    )
    result = hidden + branch_mlp
    square_sums = lax.psum(
        jnp.stack(
            [
                jnp.sum(result * result),
                jnp.sum(branch_attn * branch_attn),
                jnp.sum(branch_mlp * branch_mlp),
            ]
        ),
        ("dp", "ctx"),
    )
    entry_count = rows * lax.axis_size("dp") * lax.axis_size("ctx") * width
    rms_values = jnp.sqrt(square_sums / entry_count)
    grad_result = grad_out.astype(jnp.float32)
    grad_act = jnp.dot(grad_out, down_full, preferred_element_type=jnp.float32)
    grad_down = first_dot(grad_out, act_low)
    grad_pre_low = gelu_pull(grad_act)[0].astype(jnp.bfloat16)
    grad_up = first_dot(normed_two_low, grad_pre_low)
    grad_normed_two = lax.psum(last_dot(grad_pre_low, up_full).astype(jnp.bfloat16), "tp").astype(
        jnp.float32
    )
    grad_hidden_norm, grad_gain_two, grad_bias_two = norm_two_pull(grad_normed_two)
    grad_hidden = grad_result + grad_hidden_norm
    grad_gain_two, grad_bias_two, grad_up, grad_down = (
        lax.psum_scatter(grad_gain_two, ("dp", "ctx"), scatter_dimension=0, tiled=True),
        lax.psum_scatter(grad_bias_two, ("dp", "ctx"), scatter_dimension=0, tiled=True),
        lax.psum_scatter(grad_up, ("dp", "ctx"), scatter_dimension=0, tiled=True),
        lax.psum_scatter(grad_down, ("dp", "ctx"), scatter_dimension=0, tiled=True),
    )
    grad_branch_low = grad_hidden.astype(jnp.bfloat16)
    grad_out_proj = first_dot(grad_branch_low, attn_low)
    grad_heads_low = jnp.dot(grad_branch_low, out_full, preferred_element_type=jnp.float32).astype(
        jnp.bfloat16
    )
    grad_heads = grad_heads_low.reshape(rows, local_heads, head_size)
    row_delta = jnp.sum(grad_heads.astype(jnp.float32) * attn_accum, axis=-1).T

    def back_step(tile, carry):
        grad_query_acc, grad_keyval_all = carry
        scores, allowed, key_tile, value_tile = tile_scores(tile)
        probs = jnp.where(allowed, jnp.exp(scores - log_total[..., None]), 0.0)
        grad_probs = jnp.einsum(
            "qhd,kd->hqk", grad_heads, value_tile, preferred_element_type=jnp.float32
        )
        grad_scores = (probs * (grad_probs - row_delta[..., None])).astype(jnp.bfloat16)
        grad_query_acc = grad_query_acc + jnp.einsum(
            "hqk,kd->qhd", grad_scores, key_tile, preferred_element_type=jnp.float32
        )
        grad_key_tile = (
            jnp.einsum("hqk,qhd->kd", grad_scores, query_heads, preferred_element_type=jnp.float32)
            * scale
        )
        grad_value_tile = jnp.einsum(
            "hqk,qhd->kd",
            probs.astype(jnp.bfloat16),
            grad_heads,
            preferred_element_type=jnp.float32,
        )
        grad_keyval_all = lax.dynamic_update_slice_in_dim(
            grad_keyval_all,
            jnp.concatenate([grad_key_tile, grad_value_tile], axis=1),
            tile * rows,
            0,
        )
        return (grad_query_acc, grad_keyval_all)

    start_query = jnp.zeros((rows, local_heads, head_size), jnp.float32)
    start_keyval = jnp.zeros(keyval_all.shape, jnp.float32)
    grad_query_acc, grad_keyval_all = lax.fori_loop(
        0, tile_count, back_step, (start_query, start_keyval)
    )
    grad_query_low = (
        (grad_query_acc * scale).reshape(rows, local_heads * head_size).astype(jnp.bfloat16)
    )
    grad_keyval_mine = lax.psum_scatter(
        grad_keyval_all.astype(jnp.bfloat16), "ctx", scatter_dimension=0, tiled=True
    )
    grad_normed_query = last_dot(grad_query_low, query_full)
    grad_normed_part, grad_keyval_sum = (
        lax.psum(grad_normed_query.astype(jnp.bfloat16), "tp").astype(jnp.float32),
        lax.psum(grad_keyval_mine, "tp").astype(jnp.float32),
    )
    grad_keyval_low = grad_keyval_sum.astype(jnp.bfloat16)
    grad_normed_one = grad_normed_part + last_dot(grad_keyval_low, keyval_full)
    grad_query = first_dot(normed_low, grad_query_low)
    grad_keyval = first_dot(normed_low, grad_keyval_low)
    grad_stream_norm, grad_gain_one, grad_bias_one = norm_one_pull(grad_normed_one)
    input_grad = grad_hidden + grad_stream_norm
    grad_gain_one, grad_bias_one, grad_query, grad_keyval, grad_out_proj = (
        lax.psum_scatter(grad_gain_one, ("dp", "ctx"), scatter_dimension=0, tiled=True),
        lax.psum_scatter(grad_bias_one, ("dp", "ctx"), scatter_dimension=0, tiled=True),
        lax.psum_scatter(grad_query, ("dp", "ctx"), scatter_dimension=0, tiled=True),
        lax.psum_scatter(grad_keyval, ("dp", "ctx"), scatter_dimension=0, tiled=True),
        lax.psum_scatter(grad_out_proj, ("dp", "ctx"), scatter_dimension=0, tiled=True),
    )
    return (
        result.astype(jnp.bfloat16),
        input_grad,
        grad_gain_one,
        grad_bias_one,
        grad_query,
        grad_keyval,
        grad_out_proj,
        grad_gain_two,
        grad_bias_two,
        grad_up,
        grad_down,
        rms_values,
    )


def solution(mesh):
    return jax.shard_map(
        body,
        mesh=mesh,
        in_specs=(
            P(("dp", "ctx"), None),
            P(("dp", "ctx")),
            P(("dp", "ctx")),
            P(("dp", "ctx"), "tp"),
            P(("dp", "ctx"), None),
            P(("dp", "ctx"), "tp"),
            P(("dp", "ctx")),
            P(("dp", "ctx")),
            P(("dp", "ctx"), "tp"),
            P(("dp", "ctx"), "tp"),
            P(("dp", "ctx"), None),
        ),
        out_specs=(
            P(("dp", "ctx"), None),
            P(("dp", "ctx"), None),
            P(("dp", "ctx")),
            P(("dp", "ctx")),
            P(("dp", "ctx"), "tp"),
            P(("dp", "ctx"), None),
            P(("dp", "ctx"), "tp"),
            P(("dp", "ctx")),
            P(("dp", "ctx")),
            P(("dp", "ctx"), "tp"),
            P(("dp", "ctx"), "tp"),
            P(),
        ),
        check_vma=False,
    )
```

profile of v0, /device:TPU:0, one launch (start us, length us, event | category | flops | bytes accessed | tf_op | source)
XLA Modules:
  0.0 1833.9 jit_solution(2962413026030763452)
XLA Ops:
  8.0 33.8 %all-gather.1 = bf16[16,1,128]{2,1,0:T(2,128)(2,1)S(1)} all-gather(bf16[1,1,128]{2,1,0:T(2,128)(2,1)} %bitcast.192), channel_id=1, replica_groups=mesh['dp'=4,'ctx'=4,'tp'=2] {'dp','ctx'}, dimensions={0}, use_global_device_ids=true | all-gather | bytes 4352 | tf_op jit(solution)/shard_map/all_gather | solution.py:48
  41.8 28.4 %all-gather = bf16[16,1,128]{2,1,0:T(2,128)(2,1)S(1)} all-gather(bf16[1,1,128]{2,1,0:T(2,128)(2,1)} %bitcast.193), channel_id=1, replica_groups=mesh['dp'=4,'ctx'=4,'tp'=2] {'dp','ctx'}, dimensions={0}, use_global_device_ids=true | all-gather | bytes 4352 | tf_op jit(solution)/shard_map/all_gather | solution.py:47
  82.6 25.4 %all-gather.13.cloned.1.call-done = bf16[2048,256]{1,0:T(8,128)(2,1)} async-done(((bf16[512,256]{1,0:T(8,128)(2,1)}), bf16[2048,256]{1,0:T(8,128)(2,1)}) %all-gather.13.cloned.1.call-update) | async-done | bytes 1048592 | tf_op jit(solution)/shard_map/all_gather | solution.py:63
  110.3 50.2 %all-gather.15.cloned.1.call-done = bf16[2048,1024]{1,0:T(8,128)(2,1)} async-done(((bf16[128,1024]{1,0:T(8,128)(2,1)}), bf16[2048,1024]{1,0:T(8,128)(2,1)}) %all-gather.15.cloned.1.call-update) | async-done | bytes 4194320 | tf_op jit(solution)/shard_map/all_gather | solution.py:49
  180.7 31.1 %all-gather.17.cloned.1.call-done = bf16[2048,1024]{1,0:T(8,128)(2,1)} async-done(((bf16[128,1024]{1,0:T(8,128)(2,1)}), bf16[2048,1024]{1,0:T(8,128)(2,1)}) %all-gather.17.cloned.1.call-update) | async-done | bytes 4194320 | tf_op jit(solution)/shard_map/all_gather | solution.py:51
  219.2 29.9 %all-gather.3 = bf16[16,1,128]{2,1,0:T(2,128)(2,1)S(1)} all-gather(bf16[1,1,128]{2,1,0:T(2,128)(2,1)S(1)} %bitcast.194), channel_id=1, replica_groups=mesh['dp'=4,'ctx'=4,'tp'=2] {'dp','ctx'}, dimensions={0}, use_global_device_ids=true | all-gather | bytes 4352 | tf_op jit(solution)/shard_map/all_gather | solution.py:116
  249.1 29.0 %all-gather.2 = bf16[16,1,128]{2,1,0:T(2,128)(2,1)S(1)} all-gather(bf16[1,1,128]{2,1,0:T(2,128)(2,1)S(1)} %bitcast.195), channel_id=1, replica_groups=mesh['dp'=4,'ctx'=4,'tp'=2] {'dp','ctx'}, dimensions={0}, use_global_device_ids=true | all-gather | bytes 4352 | tf_op jit(solution)/shard_map/all_gather | solution.py:115
  282.7 125.9 %all-gather.21.cloned.1.call-done = bf16[2048,4096]{1,0:T(8,128)(2,1)} async-done(((bf16[128,4096]{1,0:T(8,128)(2,1)}), bf16[2048,4096]{1,0:T(8,128)(2,1)}) %all-gather.21.cloned.1.call-update) | async-done | bytes 16777232 | tf_op jit(solution)/shard_map/all_gather | solution.py:118
  408.6 14.9 fusion.111
  423.5 112.6 %all-gather.19.cloned.1.call-done = bf16[2048,4096]{1,0:T(8,128)(2,1)} async-done(((bf16[128,4096]{1,0:T(8,128)(2,1)}), bf16[2048,4096]{1,0:T(8,128)(2,1)}) %all-gather.19.cloned.1.call-update) | async-done | bytes 16777232 | tf_op jit(solution)/shard_map/all_gather | solution.py:117
  536.1 21.0 %fusion.81 = (bf16[512,4096]{1,0:T(8,128)(2,1)S(1)}, f32[512,4096]{1,0:T(8,128)}) fusion(f32[512,4096]{1,0:T(8,128)} %fusion.111, bf16[2048,4096]{1,0:T(8,128)(2,1)} %all-gather.19.cloned.1.call-done, bf16[512,2048]{1,0:T(8,128)(2,1)} %all-reduce.11.cloned.1.call-done, bf16[512,2048]{1,0:T(8,128)(2,1)S(1)} %copy-done, f32[2048]{0:T(1024)S(1)} %bitcast.190, ...), kind=kOutput, calls=%fused_computation.119 | convolution fusion | flops 8640266240 | bytes 41963520 | tf_op jit(solution)/shard_map/dot_general | solution.py:124
  557.1 18.5 %convolution_convert_fusion.3 = bf16[512,2048]{1,0:T(8,128)(2,1)} fusion(bf16[2048,4096]{1,0:T(8,128)(2,1)} %all-gather.21.cloned.1.call-done, f32[512,4096]{1,0:T(8,128)} %get-tuple-element.583), kind=kOutput, calls=%fused_computation.160 | convolution fusion | flops 8609857536 | bytes 27262976 | tf_op jit(solution)/shard_map/dot_general | solution.py:24
  575.6 13.4 convolution_convert_fusion.2
  591.0 104.7 %all-reduce.15.cloned.1.call-done = (bf16[512,2048]{1,0:T(8,128)(2,1)}, bf16[512,2048]{1,0:T(8,128)(2,1)}) async-done(((bf16[512,2048]{1,0:T(8,128)(2,1)}, bf16[512,2048]{1,0:T(8,128)(2,1)}), (bf16[512,2048]{1,0:T(8,128)(2,1)}, bf16[512,2048]{1,0:T(8,128)(2,1)})) %all-reduce.15.cloned.1.call-update) | async-done | bytes 4194320 | tf_op jit(solution)/shard_map/psum | solution.py:127
  740.2 56.9 %reduce-scatter.7.cloned.1.call-done = bf16[512,256]{0,1:T(8,128)(2,1)} async-done(((bf16[2048,256]{0,1:T(8,128)(2,1)}), bf16[512,256]{0,1:T(8,128)(2,1)}) %reduce-scatter.7.cloned.1.call-update) | async-done | bytes 262160 | tf_op jit(solution)/shard_map/reduce_scatter | solution.py:204
  797.2 21.1 %convolution_bitcast_fusion.1 = f32[2048,4096]{0,1:T(8,128)} fusion(bf16[512,2048]{1,0:T(8,128)(2,1)} %param.27, f32[512,4096]{1,0:T(8,128)} %get-tuple-element.583), kind=kOutput, calls=%fused_computation.110 | convolution fusion | flops 8608808960 | bytes 44040192 | tf_op jit(solution)/shard_map/dot_general | solution.py:30
  818.4 49.2 %all-reduce.13.cloned.1.call-done = (bf16[512,2048]{1,0:T(8,128)(2,1)}, bf16[512,256]{0,1:T(8,128)(2,1)}) async-done(((bf16[512,2048]{1,0:T(8,128)(2,1)}, bf16[512,256]{0,1:T(8,128)(2,1)}), (bf16[512,2048]{1,0:T(8,128)(2,1)}, bf16[512,256]{0,1:T(8,128)(2,1)})) %all-reduce.13.cloned.1.call-update) | async-done | bytes 2359312 | tf_op jit(solution)/shard_map/psum | solution.py:209
  890.0 25.4 %fusion.106 = f32[2048,4096]{1,0:T(8,128)} fusion(bf16[512,4096]{1,0:T(8,128)(2,1)} %copy-done.33, bf16[512,2048]{1,0:T(8,128)(2,1)} %all-reduce.11.cloned.1.call-done, bf16[512,2048]{1,0:T(8,128)(2,1)S(1)} %copy-done, f32[2048]{0:T(1024)S(1)} %bitcast.191, f32[2048]{0:T(1024)S(1)} %bitcast.187, f32[512]{0:T(512)S(1)} %fusion.104, ...), kind=kOutput, calls=%fused_computation.183 | convolution fusion | flops 8598323200 | bytes 41963520 | tf_op jit(solution)/shard_map/dot_general | solution.py:30
  926.7 66.4 %all-reduce.4 = (f32[2048]{0:T(1024)S(1)}, f32[2048]{0:T(1024)S(1)}, f32[2048]{0:T(1024)S(1)}, f32[2048]{0:T(1024)S(1)}, f32[3]{0:T(128)S(1)}) all-reduce(f32[2048]{0:T(1024)S(1)} %get-tuple-element.498, f32[2048]{0:T(1024)S(1)} %get-tuple-element.503, ...), channel_id=3, replica_groups=mesh['dp'=4,'ctx'=4,'tp'=2] {'dp','ctx'}, use_global_device_ids=true, to_apply=%region_24.25.clone | all-reduce | flops 8195 | bytes 65560
  1002.7 203.6 %reduce-scatter.17.cloned.1.call-done = f32[128,4096]{0,1:T(8,128)} async-done(((f32[2048,4096]{0,1:T(8,128)}), f32[128,4096]{0,1:T(8,128)}) %reduce-scatter.17.cloned.1.call-update) | async-done | bytes 2097168 | tf_op jit(solution)/shard_map/reduce_scatter | solution.py:157
  1209.1 61.9 %reduce-scatter.11.cloned.1.call-done = f32[128,256]{1,0:T(8,128)} async-done(((f32[2048,256]{1,0:T(8,128)}), f32[128,256]{1,0:T(8,128)}) %reduce-scatter.11.cloned.1.call-update) | async-done | bytes 131088 | tf_op jit(solution)/shard_map/reduce_scatter | solution.py:222
  1271.0 108.8 %reduce-scatter.9.cloned.1.call-done = f32[128,1024]{1,0:T(8,128)} async-done(((f32[2048,1024]{1,0:T(8,128)}), f32[128,1024]{1,0:T(8,128)}) %reduce-scatter.9.cloned.1.call-update) | async-done | bytes 524304 | tf_op jit(solution)/shard_map/reduce_scatter | solution.py:221
  1379.8 109.4 %reduce-scatter.13.cloned.1.call-done = f32[128,1024]{1,0:T(8,128)} async-done(((f32[2048,1024]{1,0:T(8,128)}), f32[128,1024]{1,0:T(8,128)}) %reduce-scatter.13.cloned.1.call-update) | async-done | bytes 524304 | tf_op jit(solution)/shard_map/reduce_scatter | solution.py:223
  1489.3 337.7 %reduce-scatter.15.cloned.1.call-done = f32[128,4096]{1,0:T(8,128)} async-done(((f32[2048,4096]{1,0:T(8,128)}), f32[128,4096]{1,0:T(8,128)}) %reduce-scatter.15.cloned.1.call-update) | async-done | bytes 2097168 | tf_op jit(solution)/shard_map/reduce_scatter | solution.py:156
  (174 shorter events, 161.7 us)
Async XLA Ops:
  7.2 68.4 %copy-start = (bf16[512,2048]{1,0:T(8,128)(2,1)S(1)}, bf16[512,2048]{1,0:T(8,128)(2,1)}, u32[]{:S(2)}) copy-start(bf16[512,2048]{1,0:T(8,128)(2,1)} %param.17) | copy-start | bytes 6291460
  7.2 70.6 %all-gather.11.cloned.1.call-start = ((), (), s32[]{:S(2)}) async-start(), calls=%async_computation.6 | async-start | bytes 1114112 | tf_op jit(solution)/shard_map/all_gather | solution.py:50
  7.9 100.2 %all-gather.13.cloned.1.call-start = ((), (), s32[]{:S(2)}) async-start(), calls=%async_computation.7 | async-start | bytes 1310720 | tf_op jit(solution)/shard_map/all_gather | solution.py:63
  81.1 79.5 %all-gather.15.cloned.1.call-start = ((), (), s32[]{:S(2)}) async-start(), calls=%async_computation.8 | async-start | bytes 4456448 | tf_op jit(solution)/shard_map/all_gather | solution.py:49
  81.8 130.1 %all-gather.17.cloned.1.call-start = ((), (), s32[]{:S(2)}) async-start(), calls=%async_computation.9 | async-start | bytes 4456448 | tf_op jit(solution)/shard_map/all_gather | solution.py:51
  82.4 197.0 %all-reduce.11.cloned.1.call-start = ((), (), s32[]{:S(2)}) async-start(), calls=%async_computation.10 | async-start | bytes 4194304 | tf_op jit(solution)/shard_map/psum | solution.py:110
  180.7 37.0 %copy-start.13 = (bf16[512,8,128]{0,2,1:T(8,128)(2,1)}, bf16[512,8,128]{0,2,1:T(8,128)(2,1)S(1)}, u32[]{:S(2)}) copy-start(bf16[512,8,128]{0,2,1:T(8,128)(2,1)S(1)} %convert_element_type.113) | copy-start | bytes 3145732
  217.8 31.4 %copy-start.30 = (bf16[128]{0:T(256)(128)(2,1)S(1)}, bf16[128]{0:T(256)(128)(2,1)}, u32[]{:S(2)}) copy-start(bf16[128]{0:T(256)(128)(2,1)} %param.23) | copy-start | bytes 772
  217.8 190.8 %all-gather.21.cloned.1.call-start = ((), (), s32[]{:S(2)}) async-start(), calls=%async_computation.12 | async-start | bytes 17825792 | tf_op jit(solution)/shard_map/all_gather | solution.py:118
  218.4 317.8 %all-gather.19.cloned.1.call-start = ((), (), s32[]{:S(2)}) async-start(), calls=%async_computation.11 | async-start | bytes 17825792 | tf_op jit(solution)/shard_map/all_gather | solution.py:117
  219.1 476.5 %all-reduce.15.cloned.1.call-start = ((), (), s32[]{:S(2)}) async-start(), calls=%async_computation.20 | async-start | bytes 8388608 | tf_op jit(solution)/shard_map/psum | solution.py:127
  249.1 287.0 %copy-start.27 = (f32[16,1,128]{2,1,0:T(1,128)}, f32[16,1,128]{2,1,0:T(1,128)S(1)}, u32[]{:S(2)}) copy-start(f32[16,1,128]{2,1,0:T(1,128)S(1)} %convert_element_type.139) | copy-start | bytes 24580
  557.1 18.5 %copy-start.33 = (bf16[512,4096]{1,0:T(8,128)(2,1)}, bf16[512,4096]{1,0:T(8,128)(2,1)S(1)}, u32[]{:S(2)}) copy-start(bf16[512,4096]{1,0:T(8,128)(2,1)S(1)} %get-tuple-element.582) | copy-start | bytes 12582916
  589.1 208.1 %reduce-scatter.7.cloned.1.call-start = ((), (), s32[]{:S(2)}) async-start(), calls=%async_computation.13 | async-start | bytes 1310720 | tf_op jit(solution)/shard_map/reduce_scatter | solution.py:204
  695.6 7.0 copy-start.6
  695.6 7.0 copy-start.8
  732.4 135.2 %all-reduce.13.cloned.1.call-start = ((), (), s32[]{:S(2)}) async-start(), calls=%async_computation.19 | async-start | bytes 4718592 | tf_op jit(solution)/shard_map/psum | solution.py:209
  797.2 409.1 %reduce-scatter.17.cloned.1.call-start = ((), (), s32[]{:S(2)}) async-start(), calls=%async_computation.18 | async-start | bytes 35651584 | tf_op jit(solution)/shard_map/reduce_scatter | solution.py:157
  818.3 452.7 %reduce-scatter.11.cloned.1.call-start = ((), (), s32[]{:S(2)}) async-start(), calls=%async_computation.15 | async-start | bytes 2228224 | tf_op jit(solution)/shard_map/reduce_scatter | solution.py:222
  871.3 508.6 %reduce-scatter.9.cloned.1.call-start = ((), (), s32[]{:S(2)}) async-start(), calls=%async_computation.14 | async-start | bytes 8912896 | tf_op jit(solution)/shard_map/reduce_scatter | solution.py:221
  878.9 610.3 %reduce-scatter.13.cloned.1.call-start = ((), (), s32[]{:S(2)}) async-start(), calls=%async_computation.16 | async-start | bytes 8912896 | tf_op jit(solution)/shard_map/reduce_scatter | solution.py:223
  889.3 937.6 %reduce-scatter.15.cloned.1.call-start = ((), (), s32[]{:S(2)}) async-start(), calls=%async_computation.17 | async-start | bytes 35651584 | tf_op jit(solution)/shard_map/reduce_scatter | solution.py:156
  919.4 5.3 copy-start.20
  922.7 73.3 %copy-start.24 = (f32[512]{0:T(512)S(1)}, f32[512]{0:T(512)}, u32[]{:S(2)}) copy-start(f32[512]{0:T(512)} %copy-done.23) | copy-start | bytes 6148
  (25 other events, 64.9 us)
Sparse Core Ops, SparseCore 0:
  10.2 40.6 all-gather.10
  81.2 26.8 all-gather.12
  110.3 50.1 all-gather.14
  162.6 49.2 all-gather.16
  217.9 61.4 all-reduce.10
  281.7 126.8 all-gather.20
  411.1 125.0 all-gather.18
  589.2 106.3 all-reduce.14
  732.5 64.5 reduce-scatter.6
  800.1 67.4 all-reduce.12
  871.8 334.3 reduce-scatter.16
  1210.4 60.5 reduce-scatter.10
  1276.2 103.5 reduce-scatter.8
  1384.9 104.3 reduce-scatter.12
  1494.5 332.3 reduce-scatter.14
where the time goes:
time: 1840 us; the launch traced here: 1830 us
  waiting for transfers between devices  1380 us (75%)
  blocking collectives  188 us (10%)
  matrix products  181 us (10%)
  other arithmetic  39.6 us (2%)
  local copies, waits for them, and re-layouts  27.3 us (1%)
    reduce_scatter x1, waiting for transfers between devices, body(): lax.psum_scatter(grad_up, ('dp', 'ctx'), scatter_dimension=0, tiled=True)  338 us
    reduce_scatter x1, waiting for transfers between devices, body(): lax.psum_scatter(grad_down, ('dp', 'ctx'), scatter_dimension=0, tiled=True)  204 us
    all_gather x1, waiting for transfers between devices, body(): lax.all_gather(w_down, ('dp', 'ctx'), axis=0, tiled=True)  126 us
    all_gather x1, waiting for transfers between devices, body(): lax.all_gather(w_up, ('dp', 'ctx'), axis=0, tiled=True)  113 us
    reduce_scatter x1, waiting for transfers between devices, body(): lax.psum_scatter(grad_out_proj, ('dp', 'ctx'), scatter_dimension=0, tiled...  109 us
    reduce_scatter x1, waiting for transfers between devices, body(): lax.psum_scatter(grad_query, ('dp', 'ctx'), scatter_dimension=0, tiled=True)  109 us
    psum x1, waiting for transfers between devices, body(): lax.psum(last_dot(act_low, down_full).astype(jnp.bfloat16), 'tp')  105 us
    dot_general x5, matrix products, first_dot(): lax.dot_general(left, right, (((0,), (0,)), ((), ())), preferred_element_...  66.7 us
  transfers between devices with their start and end apart: 15, of which 14 were waited for; matrix products, arithmetic and copies ran while one was open for 8% of the time, Pallas kernels for 0%

commit v1 on v0

v1 whole, which is shorter than its diff:
```python
import functools

import jax
import jax.numpy as jnp
from jax import lax
from jax.experimental import pallas as pl
from jax.experimental.pallas import tpu as pltpu
from jax.sharding import PartitionSpec as P

BLOCK = 256
FF_CHUNKS = 4
FF_TILE = 256
EPS = 1e-05
NEG = -1e30
GELU_A = 0.7978845608
GELU_B = 0.044715
F32 = jnp.float32
BF16 = jnp.bfloat16


def layer_norm(values, gain, shift):
    center = values - jnp.mean(values, axis=-1, keepdims=True)
    spread = jnp.mean(center * center, axis=-1, keepdims=True)
    return center * lax.rsqrt(spread + EPS) * gain + shift


def dot_nn(a, b):
    return lax.dot_general(a, b, (((1,), (0,)), ((), ())), preferred_element_type=F32)


def dot_nt(a, b):
    return lax.dot_general(a, b, (((1,), (1,)), ((), ())), preferred_element_type=F32)


def dot_tn(a, b):
    return lax.dot_general(a, b, (((0,), (0,)), ((), ())), preferred_element_type=F32)


class Ring:
    def __init__(self):
        self.nz = lax.axis_size("ctx")
        self.ndp = lax.axis_size("dp")
        self.nx = self.ndp // 2
        self.z_up = [(i, (i + 1) % self.nz) for i in range(self.nz)]
        self.x_up = [(i, (i + 2) % self.ndp) for i in range(self.ndp)]
        self.pair = [(i, i ^ 1) for i in range(self.ndp)]

    def order(self):
        dp, z = lax.axis_index("dp"), lax.axis_index("ctx")
        x, core = dp // 2, dp % 2
        out = []
        for dc in range(2):
            for dx in range(self.nx):
                for dz in range(self.nz):
                    xx = lax.rem(x - dx + self.nx, self.nx)
                    zz = lax.rem(z - dz + self.nz, self.nz)
                    cc = core if dc == 0 else 1 - core
                    out.append((xx * 2 + cc) * self.nz + zz)
        return jnp.stack(out).astype(jnp.int32)

    def gather(self, shard, axis):
        parts = [shard]
        for _ in range(self.nz - 1):
            parts.append(lax.ppermute(parts[-1], "ctx", self.z_up))
        groups = [jnp.concatenate(parts, axis=axis)]
        for _ in range(self.nx - 1):
            groups.append(lax.ppermute(groups[-1], "dp", self.x_up))
        mine = jnp.concatenate(groups, axis=axis)
        return mine, lax.ppermute(mine, "dp", self.pair)

    def scatter(self, mine, other, axis):
        dtype = other.dtype
        got = lax.ppermute(other, "dp", self.pair)
        size = mine.shape[axis] // self.nx

        def part(a, k, n):
            return lax.slice_in_dim(a, k * n, (k + 1) * n, axis=axis).astype(F32)

        xs = [part(mine, k, size) + part(got, k, size) for k in range(self.nx)]
        total = xs[1] if self.nx > 1 else None
        for k in range(1, self.nx):
            if k > 1:
                total = xs[k] + moved.astype(F32)
            moved = lax.ppermute(total.astype(dtype), "dp", self.x_up)
        base = xs[0] if self.nx == 1 else xs[0] + moved.astype(F32)
        size = size // self.nz
        zs = [part(base, k, size) for k in range(self.nz)]
        total = zs[1] if self.nz > 1 else zs[0]
        for k in range(1, self.nz):
            if k > 1:
                total = zs[k] + moved.astype(F32)
            moved = lax.ppermute(total.astype(dtype), "ctx", self.z_up)
        return zs[0] + moved.astype(F32) if self.nz > 1 else zs[0]

    def all_sum(self, value):
        value = value + lax.ppermute(value, "dp", self.pair)
        step = 2
        while step < self.ndp:
            value = value + lax.ppermute(value, "dp", [(i, i ^ step) for i in range(self.ndp)])
            step *= 2
        step = 1
        while step < self.nz:
            value = value + lax.ppermute(value, "ctx", [(i, i ^ step) for i in range(self.nz)])
            step *= 2
        return value


def tp_sum(part):
    n = lax.axis_size("tp")
    total = part.astype(F32)
    moved = part
    for _ in range(n - 1):
        moved = lax.ppermute(moved, "tp", [(i, (i + 1) % n) for i in range(n)])
        total = total + moved.astype(F32)
    return total


def take_blocks(a, order):
    rows, width = a.shape
    count = order.shape[0]
    bw = width // count
    if bw % 128:
        return jnp.take(a.reshape(rows, count, bw), order, axis=1).reshape(rows, width)

    def kernel(order_ref, a_ref, o_ref):
        for k in range(count):
            start = pl.multiple_of(order_ref[k] * bw, 128)
            o_ref[:, k * bw : (k + 1) * bw] = a_ref[:, pl.ds(start, bw)]

    tile = min(rows, 128)
    spec = pl.BlockSpec((tile, width), lambda i, o: (i, 0))
    return pl.pallas_call(
        kernel,
        grid_spec=pltpu.PrefetchScalarGridSpec(
            num_scalar_prefetch=1, grid=(rows // tile,), in_specs=[spec], out_specs=spec
        ),
        out_shape=jax.ShapeDtypeStruct(a.shape, a.dtype),
        cost_estimate=pl.CostEstimate(
            flops=0, transcendentals=0, bytes_accessed=2 * a.size * a.dtype.itemsize
        ),
    )(order, a)


def put_blocks(a, order):
    rows, width = a.shape
    count = order.shape[0]
    bw = width // count
    if bw % 128:
        inverse = jnp.argsort(order)
        return jnp.take(a.reshape(rows, count, bw), inverse, axis=1).reshape(rows, width)

    def kernel(order_ref, a_ref, o_ref):
        for k in range(count):
            start = pl.multiple_of(order_ref[k] * bw, 128)
            o_ref[:, pl.ds(start, bw)] = a_ref[:, k * bw : (k + 1) * bw]

    tile = min(rows, 128)
    spec = pl.BlockSpec((tile, width), lambda i, o: (i, 0))
    return pl.pallas_call(
        kernel,
        grid_spec=pltpu.PrefetchScalarGridSpec(
            num_scalar_prefetch=1, grid=(rows // tile,), in_specs=[spec], out_specs=spec
        ),
        out_shape=jax.ShapeDtypeStruct(a.shape, a.dtype),
        cost_estimate=pl.CostEstimate(
            flops=0, transcendentals=0, bytes_accessed=2 * a.size * a.dtype.itemsize
        ),
    )(order, a)


def ff_kernel(first, *refs):
    if first:
        nt, ntt, go, got, wm, wo, gm, gp, br, dn, acc_b, acc_d = refs
    else:
        nt, ntt, go, got, wm, wo, br_in, dn_in, gm, gp, br, dn, acc_b, acc_d = refs
    step = pl.program_id(0)
    half = nt.shape[1] // 2
    halves = ((wm, gm, 0), (wo, gp, half))

    @pl.when(step == 0)
    def _():
        if first:
            acc_b[...] = jnp.zeros_like(acc_b)
            acc_d[...] = jnp.zeros_like(acc_d)
        else:
            acc_b[...] = br_in[...]
            acc_d[...] = dn_in[...]

    pre = dot_nn(nt[:, :half], wm[0]) + dot_nn(nt[:, half:], wo[0])
    d_act = dot_nn(go[:, :half], wm[1]) + dot_nn(go[:, half:], wo[1])
    square = pre * pre
    th = jnp.tanh(GELU_A * pre * (1.0 + GELU_B * square))
    gate = 0.5 * (1.0 + th)
    act = (pre * gate).astype(BF16)
    slope = gate + pre * (0.5 * GELU_A) * (1.0 - th * th) * (1.0 + 3.0 * GELU_B * square)
    d_pre = (d_act * slope).astype(BF16)
    for w, g, start in halves:
        cols = pl.ds(start, half)
        acc_b[:, cols] += dot_nt(act, w[1])
        acc_d[:, cols] += dot_nt(d_pre, w[0])
        g[0] = dot_nn(ntt[cols, :], d_pre).astype(g.dtype)
        g[1] = dot_nn(got[cols, :], act).astype(g.dtype)

    @pl.when(step == pl.num_programs(0) - 1)
    def _():
        br[...] = acc_b[...].astype(br.dtype)
        dn[...] = acc_d[...].astype(dn.dtype)


def ff_chunk(nt, ntt, go, got, w_mine, w_other, carry, last):
    rows, width = nt.shape
    n = w_mine.shape[2]
    tile = min(FF_TILE, n)
    first = carry is None
    once = pl.Buffered(1)
    full = pl.BlockSpec((rows, width), lambda j: (0, 0), pipeline_mode=once)
    full_t = pl.BlockSpec((width, rows), lambda j: (0, 0), pipeline_mode=once)
    w_spec = pl.BlockSpec((2, width // 2, tile), lambda j: (0, 0, j))
    out_dtype = BF16 if last else F32
    operands = [nt, ntt, go, got, w_mine, w_other]
    specs = [full, full_t, full, full_t, w_spec, w_spec]
    if not first:
        operands += list(carry)
        specs += [full, full]
    shape = jax.ShapeDtypeStruct
    flops = 12 * rows * width * n
    moved = 16 * width * n + 32 * rows * width
    return pl.pallas_call(
        functools.partial(ff_kernel, first),
        grid=(n // tile,),
        in_specs=specs,
        out_specs=[w_spec, w_spec, full, full],
        out_shape=[
            shape(w_mine.shape, BF16),
            shape(w_other.shape, BF16),
            shape((rows, width), out_dtype),
            shape((rows, width), out_dtype),
        ],
        scratch_shapes=[pltpu.VMEM((rows, width), F32), pltpu.VMEM((rows, width), F32)],
        compiler_params=pltpu.CompilerParams(vmem_limit_bytes=60 * 1024 * 1024),
        cost_estimate=pl.CostEstimate(flops=flops, transcendentals=rows * n, bytes_accessed=moved),
    )(*operands)


def body(
    tokens, gain_one, bias_one, w_query, w_keyval, w_out, gain_two, bias_two, w_up, w_down, grad_out
):
    ring = Ring()
    nz = ring.nz
    rows, width = tokens.shape
    half = width // 2
    head_size = w_keyval.shape[1] // 2
    q_cols = w_query.shape[1]
    local_heads = q_cols // head_size
    ff_cols = w_up.shape[1]
    scale = head_size ** (-0.5)
    z = lax.axis_index("ctx")
    order = ring.order()

    small = jnp.stack([gain_one, bias_one, gain_two, bias_two])
    small_full = jnp.concatenate(ring.gather(small, 1), axis=1).astype(F32)
    g1, b1, g2, b2 = (small_full[k][None] for k in range(4))
    qkv_m, qkv_o = ring.gather(jnp.concatenate([w_query, w_keyval], axis=1), 0)
    out_m, out_o = ring.gather(w_out, 0)
    chunk = ff_cols // FF_CHUNKS
    ff_w = []
    for k in range(FF_CHUNKS):
        cols = slice(k * chunk, (k + 1) * chunk)
        ff_w.append(ring.gather(jnp.stack([w_up[:, cols], w_down[:, cols]]), 1))

    tokens_p = take_blocks(tokens, order)
    go = take_blocks(grad_out, order)
    got = go.T
    stream = tokens_p.astype(F32)
    normed_one, pull_one = jax.vjp(layer_norm, stream, g1, b1)
    normed_low = normed_one.astype(BF16)
    qkv = dot_nn(normed_low[:, :half], qkv_m) + dot_nn(normed_low[:, half:], qkv_o)
    qkv = qkv.astype(BF16)
    queries = qkv[:, :q_cols]
    tiles = [qkv[:, q_cols:]]
    for _ in range(nz - 1):
        tiles.append(lax.ppermute(tiles[-1], "ctx", [(i, i + 1) for i in range(nz - 1)]))
    keyval_all = jnp.stack(tiles)
    query_heads = queries.reshape(rows, local_heads, head_size)
    row_block = jnp.arange(rows, dtype=jnp.int32) // BLOCK
    diagonal = row_block[None, :] <= row_block[:, None]

    def tile_scores(tile):
        kv = lax.dynamic_index_in_dim(keyval_all, tile, 0, keepdims=False)
        key_tile, value_tile = kv[:, :head_size], kv[:, head_size:]
        scores = jnp.einsum("qhd,kd->hqk", query_heads, key_tile, preferred_element_type=F32)
        allowed = (diagonal | (tile > 0))[None]
        return scores * scale, allowed, key_tile, value_tile

    def max_step(tile, carry):
        run_max, run_sum = carry
        scores, allowed, _, _ = tile_scores(tile)
        masked = jnp.where(allowed, scores, NEG)
        new_max = jnp.maximum(run_max, jnp.max(masked, axis=-1))
        run_sum = run_sum * jnp.exp(run_max - new_max) + jnp.sum(
            jnp.exp(masked - new_max[..., None]), axis=-1
        )
        return new_max, run_sum

    start = (jnp.full((local_heads, rows), NEG, F32), jnp.zeros((local_heads, rows), F32))
    row_max, row_sum = lax.fori_loop(0, z + 1, max_step, start)
    log_total = row_max + jnp.log(row_sum)

    def value_step(tile, accum):
        scores, allowed, _, value_tile = tile_scores(tile)
        probs = jnp.where(allowed, jnp.exp(scores - log_total[..., None]), 0.0)
        return accum + jnp.einsum(
            "hqk,kd->qhd", probs.astype(BF16), value_tile, preferred_element_type=F32
        )

    attn = lax.fori_loop(0, z + 1, value_step, jnp.zeros((rows, local_heads, head_size), F32))
    attn_low = attn.reshape(rows, q_cols).astype(BF16)
    out_w = jnp.concatenate([out_m, out_o], axis=0)
    branch_attn = tp_sum(dot_nt(attn_low, out_w).astype(BF16))
    hidden = stream + branch_attn
    normed_two, pull_two = jax.vjp(layer_norm, hidden, g2, b2)
    nt = normed_two.astype(BF16)
    ntt = nt.T

    carry = None
    ff_grads = []
    for k in range(FF_CHUNKS):
        last = k == FF_CHUNKS - 1
        gm, gp, *carry = ff_chunk(nt, ntt, go, got, *ff_w[k], carry, last)
        ff_grads.append(ring.scatter(gm, gp, 1))
    branch_part, dn_part = carry
    grad_normed_two = tp_sum(dn_part)
    branch_mlp = tp_sum(branch_part)
    result = hidden + branch_mlp
    squares = jnp.stack(
        [jnp.sum(result * result), jnp.sum(branch_attn * branch_attn), jnp.sum(branch_mlp * branch_mlp)]
    )
    squares = ring.all_sum(jnp.broadcast_to(squares[:, None], (3, 128)))[:, 0]
    entries = rows * ring.ndp * nz * width
    rms_values = jnp.sqrt(squares / entries)
    layer_out = put_blocks(result.astype(BF16), order)

    d_hidden_norm, d_g2, d_b2 = pull_two(grad_normed_two)
    grad_hidden = go.astype(F32) + d_hidden_norm
    d_branch = grad_hidden.astype(BF16)
    d_heads_low = (dot_nn(d_branch, out_w)).astype(BF16)
    g_out = dot_tn(d_branch, attn_low).astype(BF16)
    grad_out_proj = ring.scatter(g_out[:half], g_out[half:], 0)
    grad_heads = d_heads_low.reshape(rows, local_heads, head_size)
    row_delta = jnp.sum(grad_heads.astype(F32) * attn, axis=-1).T

    def back_step(tile, carry):
        dq, dkv_all = carry
        scores, allowed, key_tile, value_tile = tile_scores(tile)
        probs = jnp.where(allowed, jnp.exp(scores - log_total[..., None]), 0.0)
        d_probs = jnp.einsum("qhd,kd->hqk", grad_heads, value_tile, preferred_element_type=F32)
        d_scores = (probs * (d_probs - row_delta[..., None])).astype(BF16)
        dq = dq + jnp.einsum("hqk,kd->qhd", d_scores, key_tile, preferred_element_type=F32)
        dk = jnp.einsum("hqk,qhd->kd", d_scores, query_heads, preferred_element_type=F32) * scale
        dv = jnp.einsum(
            "hqk,qhd->kd", probs.astype(BF16), grad_heads, preferred_element_type=F32
        )
        dkv = jnp.concatenate([dk, dv], axis=1)
        return dq, lax.dynamic_update_index_in_dim(dkv_all, dkv, tile, 0)

    dq, dkv_all = lax.fori_loop(
        0,
        z + 1,
        back_step,
        (jnp.zeros((rows, local_heads, head_size), F32), jnp.zeros(keyval_all.shape, F32)),
    )
    dq_low = (dq * scale).reshape(rows, q_cols).astype(BF16)
    total = dkv_all[0]
    for k in range(1, nz):
        moved = lax.ppermute(
            dkv_all[k].astype(BF16), "ctx", [(i + k, i) for i in range(nz - k)]
        )
        total = total + moved.astype(F32)
    dkv_low = tp_sum(total.astype(BF16)).astype(BF16)

    d_query_part = jnp.concatenate(
        [dot_nt(dq_low, qkv_m[:, :q_cols]), dot_nt(dq_low, qkv_o[:, :q_cols])], axis=1
    )
    g_query = dot_tn(normed_low, dq_low).astype(BF16)
    grad_query = ring.scatter(g_query[:half], g_query[half:], 0)
    g_kv = dot_tn(normed_low, dkv_low).astype(BF16)
    grad_keyval = ring.scatter(g_kv[:half], g_kv[half:], 0)
    d_kv_part = jnp.concatenate(
        [dot_nt(dkv_low, qkv_m[:, q_cols:]), dot_nt(dkv_low, qkv_o[:, q_cols:])], axis=1
    )
    grad_normed_one = tp_sum(d_query_part.astype(BF16)) + d_kv_part
    d_stream, d_g1, d_b1 = pull_one(grad_normed_one)
    input_grad = put_blocks(grad_hidden + d_stream, order)
    gains = jnp.concatenate([d_g1, d_b1, d_g2, d_b2], axis=0)
    gains = ring.scatter(gains[:, :half], gains[:, half:], 1)
    ff_all = jnp.concatenate(ff_grads, axis=2)
    return (
        layer_out,
        input_grad,
        gains[0],
        gains[1],
        grad_query,
        grad_keyval,
        grad_out_proj,
        gains[2],
        gains[3],
        ff_all[0],
        ff_all[1],
        rms_values,
    )


def solution(mesh):
    rows2, vec, split, rows1 = P(("dp", "ctx"), None), P(("dp", "ctx")), P(("dp", "ctx"), "tp"), None
    return jax.shard_map(
        body,
        mesh=mesh,
        in_specs=(rows2, vec, vec, split, rows2, split, vec, vec, split, split, rows2),
        out_specs=(rows2, rows2, vec, vec, split, rows2, split, vec, vec, split, split, P()),
        check_vma=False,
    )
```

time: 1840 us -> 1120 us (0.61)
  waiting for transfers between devices: 1380 us -> 696 us
  blocking collectives: 188 us -> 0 us
  matrix products: 181 us -> 54.2 us
  Pallas kernels: 0 us -> 121 us
  other arithmetic: 39.6 us -> 105 us
  starting transfers between devices: 1.06 us -> 56.9 us
  local copies, waits for them, and re-layouts: 27.3 us -> 74.7 us
    reduce_scatter x6 -> x0, waiting for transfers between devices: 878 us -> none  [the longest x1 338 us: body(): lax.psum_scatter(grad_up, ('dp', 'ctx'), scatter_dimension=0, tiled=True)]
    ppermute x0 -> x90, waiting for transfers between devices: none -> 696 us  [the longest x24 146 us: scatter(): moved = lax.ppermute(total.astype(dtype), 'ctx', self.z_up)]
    all_gather x6 -> x0, waiting for transfers between devices: 345 us -> none  [the longest x1 126 us: body(): lax.all_gather(w_down, ('dp', 'ctx'), axis=0, tiled=True)]
    psum x3 -> x0, waiting for transfers between devices: 155 us -> none  [the longest x1 105 us: body(): lax.psum(last_dot(act_low, down_full).astype(jnp.bfloat16), 'tp')]
    dot_general x21 -> x17, matrix products: 177 us -> 48.6 us  [the longest x5 15.2 us: dot_nt(): lax.dot_general(a, b, (((1,), (1,)), ((), ())), preferred_element_type=F32)]
    pallas_call x0 -> x8, Pallas kernels: none -> 121 us  [the longest x4 102 us: ff_chunk(): pl.pallas_call(functools.partial(ff_kernel, first), grid=(n // tile,), in...]
    all_gather x4 -> x0, blocking collectives: 121 us -> none  [the longest x1 33.8 us: body(): lax.all_gather(bias_one, ('dp', 'ctx'), axis=0, tiled=True)]
    unnamed x1 -> x0, blocking collectives: 66.4 us -> none
  transfers between devices with their start and end apart: 15 -> 90, of which waited for: 14 -> 54; matrix products, arithmetic and copies ran while one was open for 8% -> 20% of each run, Pallas kernels for 0% -> 9%
where the time goes in v1:
time: 1120 us; the launch traced here: 1110 us
  waiting for transfers between devices  696 us (62%)
  Pallas kernels  121 us (11%)
  other arithmetic  105 us (9%)
  local copies, waits for them, and re-layouts  74.7 us (7%)
  starting transfers between devices  56.9 us (5%)
  matrix products  54.2 us (5%)
    ppermute x24, waiting for transfers between devices, scatter(): moved = lax.ppermute(total.astype(dtype), 'ctx', self.z_up)  146 us
    ppermute x21, waiting for transfers between devices, gather(): parts.append(lax.ppermute(parts[-1], 'ctx', self.z_up))  143 us
    ppermute x8, waiting for transfers between devices, scatter(): moved = lax.ppermute(total.astype(dtype), 'dp', self.x_up)  138 us
    pallas_call x4, Pallas kernels, ff_chunk(): pl.pallas_call(functools.partial(ff_kernel, first), grid=(n // tile,), in...  102 us
    ppermute x5, waiting for transfers between devices, tp_sum(): moved = lax.ppermute(moved, 'tp', [(i, (i + 1) % n) for i in range(n)])  101 us
    ppermute x7, waiting for transfers between devices, gather(): groups.append(lax.ppermute(groups[-1], 'dp', self.x_up))  96.1 us
    ppermute x3, waiting for transfers between devices, body(): lax.ppermute(dkv_all[k].astype(BF16), 'ctx', [(i + k, i) for i in range(n...  59.1 us
    unnamed x190, local copies, waits for them, and re-layouts  36.3 us
  transfers between devices with their start and end apart: 90, of which 54 were waited for; matrix products, arithmetic and copies ran while one was open for 20% of the time, Pallas kernels for 9%

profile of v1, /device:TPU:0, one launch (start us, length us, event | category | flops | bytes accessed | tf_op | source)
XLA Modules:
  0.0 1111.0 jit_solution(3297234994946063092)
XLA Ops:
  25.7 28.4 %collective-permute-done.6 = bf16[128,1280]{1,0:T(8,128)(2,1)S(1)} collective-permute-done((bf16[128,1280]{1,0:T(8,128)(2,1)}, bf16[128,1280]{1,0:T(8,128)(2,1)S(1)}, u32[]{:S(2)}, u32[]{:S(2)}) %collective-permute-start.6) | collective-permute-done | bytes 327712 | tf_op jit(solution)/shard_map/ppermute | solution.py:64
  77.5 16.2 %collective-permute-done.8 = bf16[512,1280]{1,0:T(8,128)(2,1)S(1)} collective-permute-done((bf16[512,1280]{1,0:T(8,128)(2,1)S(1)}, bf16[512,1280]{1,0:T(8,128)(2,1)S(1)}, u32[]{:S(2)}, u32[]{:S(2)}) %collective-permute-start.8) | collective-permute-done | bytes 1310752 | tf_op jit(solution)/shard_map/ppermute | solution.py:67
  118.9 11.2 %collective-permute-done.19 = bf16[2,128,1024]{2,1,0:T(8,128)(2,1)S(1)} collective-permute-done((bf16[2,128,1024]{2,1,0:T(8,128)(2,1)}, bf16[2,128,1024]{2,1,0:T(8,128)(2,1)S(1)}, u32[]{:S(2)}, u32[]{:S(2)}) %collective-permute-start.19) | collective-permute-done | bytes 524320 | tf_op jit(solution)/shard_map/ppermute | solution.py:64
  169.5 11.2 %collective-permute-done.20 = bf16[2,128,1024]{2,1,0:T(8,128)(2,1)S(1)} collective-permute-done((bf16[2,128,1024]{2,1,0:T(8,128)(2,1)S(1)}, bf16[2,128,1024]{2,1,0:T(8,128)(2,1)S(1)}, u32[]{:S(2)}, u32[]{:S(2)}) %collective-permute-start.20) | collective-permute-done | bytes 524320 | tf_op jit(solution)/shard_map/ppermute | solution.py:64
  296.7 36.6 %collective-permute-done.27 = bf16[2,512,1024]{2,1,0:T(8,128)(2,1)} collective-permute-done((bf16[2,512,1024]{2,1,0:T(8,128)(2,1)}, bf16[2,512,1024]{2,1,0:T(8,128)(2,1)}, u32[]{:S(2)}, u32[]{:S(2)}) %collective-permute-start.27) | collective-permute-done | bytes 2097184 | tf_op jit(solution)/shard_map/ppermute | solution.py:67
  336.4 41.2 %collective-permute-done.22 = bf16[2,512,1024]{2,1,0:T(8,128)(2,1)} collective-permute-done((bf16[2,512,1024]{2,1,0:T(8,128)(2,1)}, bf16[2,512,1024]{2,1,0:T(8,128)(2,1)}, u32[]{:S(2)}, u32[]{:S(2)}) %collective-permute-start.22) | collective-permute-done | bytes 2097184 | tf_op jit(solution)/shard_map/ppermute | solution.py:67
  395.0 23.8 %shard_map.204 = (bf16[2,1024,1024]{2,1,0:T(8,128)(2,1)}, bf16[2,1024,1024]{2,1,0:T(8,128)(2,1)}, f32[512,2048]{1,0:T(8,128)}, f32[512,2048]{1,0:T(8,128)}) custom-call(bf16[512,2048]{1,0:T(8,128)(2,1)} %add_convert_fusion.4.refs_0_, bf16[2048,512]{1,0:T(8,128)(2,1)} %copy.35.refs_1_, bf16[512,2048]{1,0:T(8,128)(2,1)} %shard_map.203.refs_2_, ...), custom_call_target="tpu_custom_call" | custom-call | flops 12884901888 | bytes 67108864 | tf_op jit(solution)/shard_map/pallas_call | solution.py:228
  418.9 26.5 %shard_map.205 = (bf16[2,1024,1024]{2,1,0:T(8,128)(2,1)}, bf16[2,1024,1024]{2,1,0:T(8,128)(2,1)}, f32[512,2048]{1,0:T(8,128)}, f32[512,2048]{1,0:T(8,128)}) custom-call(bf16[512,2048]{1,0:T(8,128)(2,1)} %add_convert_fusion.4.refs_0_, bf16[2048,512]{1,0:T(8,128)(2,1)} %copy.35.refs_1_, bf16[512,2048]{1,0:T(8,128)(2,1)} %shard_map.203.refs_2_, ...), custom_call_target="tpu_custom_call" | custom-call | flops 12884901888 | bytes 67108864 | tf_op jit(solution)/shard_map/pallas_call | solution.py:228
  445.4 26.3 %shard_map.206 = (bf16[2,1024,1024]{2,1,0:T(8,128)(2,1)}, bf16[2,1024,1024]{2,1,0:T(8,128)(2,1)}, f32[512,2048]{1,0:T(8,128)}, f32[512,2048]{1,0:T(8,128)}) custom-call(bf16[512,2048]{1,0:T(8,128)(2,1)} %add_convert_fusion.4.refs_0_, bf16[2048,512]{1,0:T(8,128)(2,1)} %copy.35.refs_1_, bf16[512,2048]{1,0:T(8,128)(2,1)} %shard_map.203.refs_2_, ...), custom_call_target="tpu_custom_call" | custom-call | flops 12884901888 | bytes 67108864 | tf_op jit(solution)/shard_map/pallas_call | solution.py:228
  471.8 25.1 %shard_map.207 = (bf16[2,1024,1024]{2,1,0:T(8,128)(2,1)}, bf16[2,1024,1024]{2,1,0:T(8,128)(2,1)}, bf16[512,2048]{1,0:T(8,128)(2,1)}, bf16[512,2048]{1,0:T(8,128)(2,1)}) custom-call(bf16[512,2048]{1,0:T(8,128)(2,1)} %add_convert_fusion.4.refs_0_, bf16[2048,512]{1,0:T(8,128)(2,1)} %copy.35.refs_1_, bf16[512,2048]{1,0:T(8,128)(2,1)} %shard_map.203.refs_2_, ...), custom_call_target="tpu_custom_call" | custom-call | flops 12884901888 | bytes 67108864 | tf_op jit(solution)/shard_map/pallas_call | solution.py:228
  501.2 44.5 %collective-permute-done.39 = bf16[512,2048]{1,0:T(8,128)(2,1)} collective-permute-done((bf16[512,2048]{1,0:T(8,128)(2,1)}, bf16[512,2048]{1,0:T(8,128)(2,1)}, u32[]{:S(2)}, u32[]{:S(2)}) %collective-permute-start.39) | collective-permute-done | bytes 2097184 | tf_op jit(solution)/shard_map/ppermute | solution.py:113
  545.7 44.4 %collective-permute-done.40 = bf16[512,2048]{1,0:T(8,128)(2,1)S(1)} collective-permute-done((bf16[512,2048]{1,0:T(8,128)(2,1)}, bf16[512,2048]{1,0:T(8,128)(2,1)S(1)}, u32[]{:S(2)}, u32[]{:S(2)}) %collective-permute-start.40) | collective-permute-done | bytes 2097184 | tf_op jit(solution)/shard_map/ppermute | solution.py:113
  615.4 16.7 %while.39 = (s32[]{:T(128)}, f32[512,8,128]{0,2,1:T(8,128)S(1)}, f32[4,512,256]{1,2,0:T(8,128)}, s32[]{:T(128)}, bf16[4,512,256]{2,1,0:T(8,128)(2,1)}, /*index=5...) while((s32[]{:T(128)}, f32[512,8,128]{0,2,1:T(8,128)S(1)}, ...), condition=%wide.region_14.15_spmd.clone, body=%wide.region_13.14_spmd.clone.sunk | while | flops 2706571264 | bytes 78825728 | solution.py:366
  643.2 13.7 %collective-permute-done.42 = bf16[512,256]{0,1:T(8,128)(2,1)S(1)} collective-permute-done((bf16[512,256]{0,1:T(8,128)(2,1)S(1)}, bf16[512,256]{0,1:T(8,128)(2,1)S(1)}, u32[]{:S(2)}, u32[]{:S(2)}) %collective-permute-start.42) | collective-permute-done | bytes 262176 | tf_op jit(solution)/shard_map/ppermute | solution.py:375
  656.9 21.4 %collective-permute-done.43 = bf16[512,256]{0,1:T(8,128)(2,1)S(1)} collective-permute-done((bf16[512,256]{0,1:T(8,128)(2,1)S(1)}, bf16[512,256]{0,1:T(8,128)(2,1)S(1)}, u32[]{:S(2)}, u32[]{:S(2)}) %collective-permute-start.43) | collective-permute-done | bytes 262176 | tf_op jit(solution)/shard_map/ppermute | solution.py:375
  678.3 24.0 %collective-permute-done.44 = bf16[512,256]{0,1:T(8,128)(2,1)S(1)} collective-permute-done((bf16[512,256]{0,1:T(8,128)(2,1)S(1)}, bf16[512,256]{0,1:T(8,128)(2,1)S(1)}, u32[]{:S(2)}, u32[]{:S(2)}) %collective-permute-start.44) | collective-permute-done | bytes 262176 | tf_op jit(solution)/shard_map/ppermute | solution.py:375
  793.0 93.1 %collective-permute-done.47 = f32[4,512]{1,0:T(4,128)S(1)} collective-permute-done((f32[4,512]{1,0:T(4,128)S(1)}, f32[4,512]{1,0:T(4,128)S(1)}, u32[]{:S(2)}, u32[]{:S(2)}) %collective-permute-start.47) | collective-permute-done | bytes 8224 | tf_op jit(solution)/shard_map/ppermute | solution.py:84
  900.3 12.3 %collective-permute-done.52 = bf16[512,1024]{1,0:T(8,128)(2,1)} collective-permute-done((bf16[512,1024]{1,0:T(8,128)(2,1)}, bf16[512,1024]{1,0:T(8,128)(2,1)}, u32[]{:S(2)}, u32[]{:S(2)}) %collective-permute-start.52) | collective-permute-done | bytes 1048608 | tf_op jit(solution)/shard_map/ppermute | solution.py:84
  967.9 32.7 %collective-permute-done.82 = bf16[2,512,1024]{2,1,0:T(8,128)(2,1)} collective-permute-done((bf16[2,512,1024]{2,1,0:T(8,128)(2,1)S(1)}, bf16[2,512,1024]{2,1,0:T(8,128)(2,1)}, u32[]{:S(2)}, u32[]{:S(2)}) %collective-permute-start.82) | collective-permute-done | bytes 2097184 | tf_op jit(solution)/shard_map/ppermute | solution.py:84
  1009.3 11.1 collective-permute-done.83
  1020.6 11.0 collective-permute-done.69
  1043.1 11.0 collective-permute-done.79
  1076.7 11.0 collective-permute-done.75
  1088.0 11.0 collective-permute-done.80
  (521 shorter events, 531.5 us)
Async XLA Ops:
  1.4 67.5 %collective-permute-start = (bf16[4,128]{1,0:T(4,128)(2,1)S(1)}, bf16[4,128]{1,0:T(4,128)(2,1)S(1)}, u32[]{:S(2)}, u32[]{:S(2)}) collective-permute-start(bf16[4,128]{1,0:T(4,128)(2,1)S(1)} %get-tuple-element.329), channel_id=1, source_target_pairs={{0,2},{2,4},{4,6},{6,0},{1,3},{3,5},{5,7},{7,1},{8,10},{10,12},{12... | collective-permute-start | bytes 3080 | tf_op jit(solution)/shard_map/ppermute | solution.py:64
  9.4 87.2 %collective-permute-start.13 = (bf16[128,1024]{1,0:T(8,128)(2,1)}, bf16[128,1024]{1,0:T(8,128)(2,1)}, u32[]{:S(2)}, u32[]{:S(2)}) collective-permute-start(bf16[128,1024]{1,0:T(8,128)(2,1)} %param.22), channel_id=1, source_target_pairs={{0,2},{2,4},{4,6},{6,0},{1,3},{3,5},{5,7},{7,1},{8,10},{10,12},{12... | collective-permute-start | bytes 786440 | tf_op jit(solution)/shard_map/ppermute | solution.py:64
  13.9 93.9 %collective-permute-start.34 = (bf16[2,128,1024]{2,1,0:T(8,128)(2,1)}, bf16[2,128,1024]{2,1,0:T(8,128)(2,1)}, u32[]{:S(2)}, u32[]{:S(2)}) collective-permute-start(bf16[2,128,1024]{2,1,0:T(8,128)(2,1)} %get-tuple-element.353), channel_id=1, source_target_pairs={{0,2},{2,4},{4,6},{6,0},{1,3},{3,5},{5,7},{7,1},{8,10},{10,12},{12... | collective-permute-start | bytes 1572872 | tf_op jit(solution)/shard_map/ppermute | solution.py:64
  15.1 92.8 %collective-permute-start.29 = (bf16[2,128,1024]{2,1,0:T(8,128)(2,1)}, bf16[2,128,1024]{2,1,0:T(8,128)(2,1)}, u32[]{:S(2)}, u32[]{:S(2)}) collective-permute-start(bf16[2,128,1024]{2,1,0:T(8,128)(2,1)} %get-tuple-element.355), channel_id=1, source_target_pairs={{0,2},{2,4},{4,6},{6,0},{1,3},{3,5},{5,7},{7,1},{8,10},{10,12},{12... | collective-permute-start | bytes 1572872 | tf_op jit(solution)/shard_map/ppermute | solution.py:64
  94.9 99.7 %collective-permute-start.9 = (bf16[1024,1280]{1,0:T(8,128)(2,1)}, bf16[1024,1280]{1,0:T(8,128)(2,1)}, u32[]{:S(2)}, u32[]{:S(2)}) collective-permute-start(bf16[1024,1280]{1,0:T(8,128)(2,1)} %constant_dynamic-update-slice_fusion.13), channel_id=1, source_target_pairs={{0,8},{8,0},{16,24},{24,16},{1,9},{9,1},{17,25},{25,17},{2,10},{10... | collective-permute-start | bytes 7864328 | tf_op jit(solution)/shard_map/ppermute | solution.py:69
  194.6 76.4 %collective-permute-start.37 = (bf16[2,512,1024]{2,1,0:T(8,128)(2,1)}, bf16[2,512,1024]{2,1,0:T(8,128)(2,1)}, u32[]{:S(2)}, u32[]{:S(2)}) collective-permute-start(bf16[2,512,1024]{2,1,0:T(8,128)(2,1)} %pad_maximum_fusion.4), channel_id=1, source_target_pairs={{0,16},{8,24},{16,0},{24,8},{1,17},{9,25},{17,1},{25,9},{2,18},{10... | collective-permute-start | bytes 6291464 | tf_op jit(solution)/shard_map/ppermute | solution.py:67
  214.4 77.1 %collective-permute-start.32 = (bf16[2,512,1024]{2,1,0:T(8,128)(2,1)}, bf16[2,512,1024]{2,1,0:T(8,128)(2,1)}, u32[]{:S(2)}, u32[]{:S(2)}) collective-permute-start(bf16[2,512,1024]{2,1,0:T(8,128)(2,1)} %pad_maximum_fusion.3), channel_id=1, source_target_pairs={{0,16},{8,24},{16,0},{24,8},{1,17},{9,25},{17,1},{25,9},{2,18},{10... | collective-permute-start | bytes 6291464 | tf_op jit(solution)/shard_map/ppermute | solution.py:67
  225.0 108.3 %collective-permute-start.27 = (bf16[2,512,1024]{2,1,0:T(8,128)(2,1)}, bf16[2,512,1024]{2,1,0:T(8,128)(2,1)}, u32[]{:S(2)}, u32[]{:S(2)}) collective-permute-start(bf16[2,512,1024]{2,1,0:T(8,128)(2,1)} %pad_maximum_fusion.2), channel_id=1, source_target_pairs={{0,16},{8,24},{16,0},{24,8},{1,17},{9,25},{17,1},{25,9},{2,18},{10... | collective-permute-start | bytes 6291464 | tf_op jit(solution)/shard_map/ppermute | solution.py:67
  232.5 145.1 %collective-permute-start.22 = (bf16[2,512,1024]{2,1,0:T(8,128)(2,1)}, bf16[2,512,1024]{2,1,0:T(8,128)(2,1)}, u32[]{:S(2)}, u32[]{:S(2)}) collective-permute-start(bf16[2,512,1024]{2,1,0:T(8,128)(2,1)} %pad_maximum_fusion.1), channel_id=1, source_target_pairs={{0,16},{8,24},{16,0},{24,8},{1,17},{9,25},{17,1},{25,9},{2,18},{10... | collective-permute-start | bytes 6291464 | tf_op jit(solution)/shard_map/ppermute | solution.py:67
  267.8 113.0 %collective-permute-start.18 = (bf16[512,2048]{1,0:T(8,128)(2,1)}, bf16[512,2048]{1,0:T(8,128)(2,1)}, u32[]{:S(2)}, u32[]{:S(2)}) collective-permute-start(bf16[512,2048]{1,0:T(8,128)(2,1)} %convolution_convert_fusion.2), channel_id=1, source_target_pairs={{0,1},{1,0},{2,3},{3,2},{4,5},{5,4},{6,7},{7,6},{8,9},{9,8},{10,11... | collective-permute-start | bytes 6291464 | tf_op jit(solution)/shard_map/ppermute | solution.py:113
  274.1 120.9 %collective-permute-start.38 = (bf16[2,1024,1024]{2,1,0:T(8,128)(2,1)}, bf16[2,1024,1024]{2,1,0:T(8,128)(2,1)}, u32[]{:S(2)}, u32[]{:S(2)}) collective-permute-start(bf16[2,1024,1024]{2,1,0:T(8,128)(2,1)} %constant_dynamic-update-slice_fusion.45.refs_4_), channel_id=1, source_target_pairs={{0,8},{8,0},{16,24},{24,16},{1,9},{9,1},{17,25},{25,17},{2,10},{10... | collective-permute-start | bytes 12582920 | tf_op jit(solution)/shard_map/ppermute | solution.py:69
  294.7 124.2 %collective-permute-start.33 = (bf16[2,1024,1024]{2,1,0:T(8,128)(2,1)}, bf16[2,1024,1024]{2,1,0:T(8,128)(2,1)}, u32[]{:S(2)}, u32[]{:S(2)}) collective-permute-start(bf16[2,1024,1024]{2,1,0:T(8,128)(2,1)} %constant_dynamic-update-slice_fusion.40.refs_4_), channel_id=1, source_target_pairs={{0,8},{8,0},{16,24},{24,16},{1,9},{9,1},{17,25},{25,17},{2,10},{10... | collective-permute-start | bytes 12582920 | tf_op jit(solution)/shard_map/ppermute | solution.py:69
  336.4 109.0 %collective-permute-start.28 = (bf16[2,1024,1024]{2,1,0:T(8,128)(2,1)}, bf16[2,1024,1024]{2,1,0:T(8,128)(2,1)}, u32[]{:S(2)}, u32[]{:S(2)}) collective-permute-start(bf16[2,1024,1024]{2,1,0:T(8,128)(2,1)} %constant_dynamic-update-slice_fusion.35.refs_4_), channel_id=1, source_target_pairs={{0,8},{8,0},{16,24},{24,16},{1,9},{9,1},{17,25},{25,17},{2,10},{10... | collective-permute-start | bytes 12582920 | tf_op jit(solution)/shard_map/ppermute | solution.py:69
  380.8 91.0 %collective-permute-start.23 = (bf16[2,1024,1024]{2,1,0:T(8,128)(2,1)}, bf16[2,1024,1024]{2,1,0:T(8,128)(2,1)}, u32[]{:S(2)}, u32[]{:S(2)}) collective-permute-start(bf16[2,1024,1024]{2,1,0:T(8,128)(2,1)} %constant_dynamic-update-slice_fusion.30.refs_4_), channel_id=1, source_target_pairs={{0,8},{8,0},{16,24},{24,16},{1,9},{9,1},{17,25},{25,17},{2,10},{10... | collective-permute-start | bytes 12582920 | tf_op jit(solution)/shard_map/ppermute | solution.py:69
  498.5 91.7 %collective-permute-start.40 = (bf16[512,2048]{1,0:T(8,128)(2,1)}, bf16[512,2048]{1,0:T(8,128)(2,1)S(1)}, u32[]{:S(2)}, u32[]{:S(2)}) collective-permute-start(bf16[512,2048]{1,0:T(8,128)(2,1)} %get-tuple-element.169), channel_id=1, source_target_pairs={{0,1},{1,0},{2,3},{3,2},{4,5},{5,4},{6,7},{7,6},{8,9},{9,8},{10,11... | collective-permute-start | bytes 6291464 | tf_op jit(solution)/shard_map/ppermute | solution.py:113
  500.6 265.0 %collective-permute-start.66 = (bf16[2,1024,1024]{2,1,0:T(8,128)(2,1)}, bf16[2,1024,1024]{2,1,0:T(8,128)(2,1)}, u32[]{:S(2)}, u32[]{:S(2)}) collective-permute-start(bf16[2,1024,1024]{2,1,0:T(8,128)(2,1)} %get-tuple-element.173), channel_id=1, source_target_pairs={{0,8},{8,0},{16,24},{24,16},{1,9},{9,1},{17,25},{25,17},{2,10},{10... | collective-permute-start | bytes 12582920 | tf_op jit(solution)/shard_map/ppermute | solution.py:73
  500.7 270.2 %collective-permute-start.71 = (bf16[2,1024,1024]{2,1,0:T(8,128)(2,1)}, bf16[2,1024,1024]{2,1,0:T(8,128)(2,1)}, u32[]{:S(2)}, u32[]{:S(2)}) collective-permute-start(bf16[2,1024,1024]{2,1,0:T(8,128)(2,1)} %get-tuple-element.175), channel_id=1, source_target_pairs={{0,8},{8,0},{16,24},{24,16},{1,9},{9,1},{17,25},{25,17},{2,10},{10... | collective-permute-start | bytes 12582920 | tf_op jit(solution)/shard_map/ppermute | solution.py:73
  636.5 65.8 %collective-permute-start.44 = (bf16[512,256]{0,1:T(8,128)(2,1)S(1)}, bf16[512,256]{0,1:T(8,128)(2,1)S(1)}, u32[]{:S(2)}, u32[]{:S(2)}) collective-permute-start(bf16[512,256]{0,1:T(8,128)(2,1)S(1)} %get-tuple-element.341), channel_id=1, source_target_pairs={{6,0},{7,1},{14,8},{15,9},{22,16},{23,17},{30,24},{31,25}} | collective-permute-start | bytes 786440 | tf_op jit(solution)/shard_map/ppermute | solution.py:375
  753.1 134.5 %collective-permute-start.81 = (bf16[2,1024,1024]{2,1,0:T(8,128)(2,1)}, bf16[2,1024,1024]{2,1,0:T(8,128)(2,1)S(1)}, u32[]{:S(2)}, u32[]{:S(2)}) collective-permute-start(bf16[2,1024,1024]{2,1,0:T(8,128)(2,1)} %get-tuple-element.179), channel_id=1, source_target_pairs={{0,8},{8,0},{16,24},{24,16},{1,9},{9,1},{17,25},{25,17},{2,10},{10... | collective-permute-start | bytes 12582920 | tf_op jit(solution)/shard_map/ppermute | solution.py:73
  770.9 185.0 %collective-permute-start.67 = (bf16[2,512,1024]{2,1,0:T(8,128)(2,1)S(1)}, bf16[2,512,1024]{2,1,0:T(8,128)(2,1)}, u32[]{:S(2)}, u32[]{:S(2)}) collective-permute-start(bf16[2,512,1024]{2,1,0:T(8,128)(2,1)S(1)} %add_convert_fusion.3), channel_id=1, source_target_pairs={{0,16},{8,24},{16,0},{24,8},{1,17},{9,25},{17,1},{25,9},{2,18},{10... | collective-permute-start | bytes 6291464 | tf_op jit(solution)/shard_map/ppermute | solution.py:84
  776.5 183.3 %collective-permute-start.72 = (bf16[2,512,1024]{2,1,0:T(8,128)(2,1)}, bf16[2,512,1024]{2,1,0:T(8,128)(2,1)}, u32[]{:S(2)}, u32[]{:S(2)}) collective-permute-start(bf16[2,512,1024]{2,1,0:T(8,128)(2,1)} %add_convert_fusion.2), channel_id=1, source_target_pairs={{0,16},{8,24},{16,0},{24,8},{1,17},{9,25},{17,1},{25,9},{2,18},{10... | collective-permute-start | bytes 6291464 | tf_op jit(solution)/shard_map/ppermute | solution.py:84
  788.3 109.7 %collective-permute-start.62 = (bf16[512,1024]{1,0:T(8,128)(2,1)}, bf16[512,1024]{1,0:T(8,128)(2,1)S(1)}, u32[]{:S(2)}, u32[]{:S(2)}) collective-permute-start(bf16[512,1024]{1,0:T(8,128)(2,1)} %add_convert_fusion.5), channel_id=1, source_target_pairs={{0,16},{8,24},{16,0},{24,8},{1,17},{9,25},{17,1},{25,9},{2,18},{10... | collective-permute-start | bytes 3145736 | tf_op jit(solution)/shard_map/ppermute | solution.py:84
  789.2 96.9 %collective-permute-start.47 = (f32[4,512]{1,0:T(4,128)S(1)}, f32[4,512]{1,0:T(4,128)S(1)}, u32[]{:S(2)}, u32[]{:S(2)}) collective-permute-start(f32[4,512]{1,0:T(4,128)S(1)} %slice_add_fusion.21), channel_id=1, source_target_pairs={{0,16},{8,24},{16,0},{24,8},{1,17},{9,25},{17,1},{25,9},{2,18},{10... | collective-permute-start | bytes 24584 | tf_op jit(solution)/shard_map/ppermute | solution.py:84
  897.4 66.3 %collective-permute-start.77 = (bf16[2,512,1024]{2,1,0:T(8,128)(2,1)}, bf16[2,512,1024]{2,1,0:T(8,128)(2,1)}, u32[]{:S(2)}, u32[]{:S(2)}) collective-permute-start(bf16[2,512,1024]{2,1,0:T(8,128)(2,1)} %add_convert_fusion.1), channel_id=1, source_target_pairs={{0,16},{8,24},{16,0},{24,8},{1,17},{9,25},{17,1},{25,9},{2,18},{10... | collective-permute-start | bytes 6291464 | tf_op jit(solution)/shard_map/ppermute | solution.py:84
  (150 other events, 3910.3 us)

commit v2 on v1

v2 whole, which is shorter than its diff:
```python
import functools

import jax
import jax.numpy as jnp
from jax import lax
from jax.experimental import pallas as pl
from jax.experimental.pallas import tpu as pltpu
from jax.sharding import PartitionSpec as P

BLOCK = 256
FF_SPLIT = (2048, 2048)
FF_TILE = 256
EPS = 1e-05
NEG = -1e30
GELU_A = 0.7978845608
GELU_B = 0.044715
LOG2E = 1.4426950408889634
F32 = jnp.float32
SMALL = pl.CostEstimate(flops=1000, transcendentals=0, bytes_accessed=1000)
BF16 = jnp.bfloat16


def dot_nn(a, b):
    return lax.dot_general(a, b, (((1,), (0,)), ((), ())), preferred_element_type=F32)


def dot_nt(a, b):
    return lax.dot_general(a, b, (((1,), (1,)), ((), ())), preferred_element_type=F32)


def dot_tn(a, b):
    return lax.dot_general(a, b, (((0,), (0,)), ((), ())), preferred_element_type=F32)


def after(value, *others):
    return lax.optimization_barrier((value, *others))[0]


class Order:
    def __init__(self):
        self.token = []

    def run(self, function, *args, wait=()):
        leaves, tree = jax.tree.flatten(args)
        held = lax.optimization_barrier((*leaves, *self.token, *jax.tree.leaves(wait)))
        out = function(*jax.tree.unflatten(tree, held[: len(leaves)]))
        self.token = jax.tree.leaves(out)[:1]
        return out


def join(axis):
    return lambda *parts: jnp.concatenate(parts, axis=axis)


class Ring:
    def __init__(self):
        self.nz = lax.axis_size("ctx")
        self.ndp = lax.axis_size("dp")
        self.nx = self.ndp // 2

    def z(self, value, k):
        return lax.ppermute(value, "ctx", [(i, (i + k) % self.nz) for i in range(self.nz)])

    def x(self, value, k):
        return lax.ppermute(value, "dp", [(i, (i + 2 * k) % self.ndp) for i in range(self.ndp)])

    def core(self, value):
        return lax.ppermute(value, "dp", [(i, i ^ 1) for i in range(self.ndp)])

    def z_all(self, value):
        far = self.nz // 2
        ups, downs = [], []
        for _ in range(far):
            ups.append(self.z(ups[-1] if ups else value, 1))
        for _ in range(self.nz - 1 - far):
            downs.append(self.z(downs[-1] if downs else value, -1))
        return ups + downs[::-1]

    def x_all(self, value):
        return [self.x(value, k) for k in range(1, self.nx)]

    def order(self):
        dp, z = lax.axis_index("dp"), lax.axis_index("ctx")
        x, core = dp // 2, dp % 2
        out = []
        for dc in range(2):
            for dx in range(self.nx):
                for dz in range(self.nz):
                    xx = lax.rem(x - dx + self.nx, self.nx)
                    zz = lax.rem(z - dz + self.nz, self.nz)
                    cc = core if dc == 0 else 1 - core
                    out.append((xx * 2 + cc) * self.nz + zz)
        return jnp.stack(out).astype(jnp.int32)

    def side_parts(self, mine, other, axis):
        width = mine.shape[axis] // self.nx
        return [
            (cut(mine, k * width, width, axis) + cut(other, k * width, width, axis)).astype(BF16)
            for k in range(1, self.nx)
        ]

    def block_parts(self, mine, other, crossed, axis):
        size = mine.shape[axis] // self.nx // self.nz
        out = []
        for k in range(self.nz):
            part = cut(mine, k * size, size, axis) + cut(other, k * size, size, axis)
            for c in crossed:
                part = part + cut(c, k * size, size, axis)
            out.append(part.astype(BF16) if k else part)
        return out

    def small_sum(self, value):
        value = value + self.core(value)
        step = 2
        while step < self.ndp:
            value = value + lax.ppermute(value, "dp", [(i, i ^ step) for i in range(self.ndp)])
            step *= 2
        step = 1
        while step < self.nz:
            value = value + lax.ppermute(value, "ctx", [(i, i ^ step) for i in range(self.nz)])
            step *= 2
        return value

    def small_scatter(self, full):
        half = full.shape[1] // 2
        base = full[:, :half] + self.core(full[:, half:])
        size = half // self.nx
        base = added([base[:, :size]] + [self.x(base[:, k * size : (k + 1) * size], -k) for k in range(1, self.nx)])
        size = size // self.nz
        return added([base[:, :size]] + [self.z(base[:, k * size : (k + 1) * size], -k) for k in range(1, self.nz)])


def cut(a, start, length, axis):
    return lax.slice_in_dim(a, start, start + length, axis=axis).astype(F32)


def added(parts):
    out = parts[0].astype(F32)
    for p in parts[1:]:
        out = out + p.astype(F32)
    return out


def tp_others(part):
    n = lax.axis_size("tp")
    return [lax.ppermute(part, "tp", [(i, (i + k) % n) for i in range(n)]) for k in range(1, n)]


def gathered(a, order):
    rows, width = a.shape
    count = order.shape[0]
    return jnp.take(a.reshape(rows, count, width // count), order, axis=1).reshape(rows, width)


def row_call(kernel, order, ins, outs, scratch=()):
    rows = max(a.shape[0] for kind, a in ins if kind == "row")
    tile = min(rows, 128)

    def spec(kind, shape):
        if kind == "row":
            return pl.BlockSpec((tile, shape[1]), lambda i, o: (i, 0))
        if kind == "col":
            return pl.BlockSpec((shape[0], tile), lambda i, o: (0, i))
        return pl.BlockSpec(shape, lambda i, o: (0,) * len(shape))

    return pl.pallas_call(
        kernel,
        grid_spec=pltpu.PrefetchScalarGridSpec(
            num_scalar_prefetch=1,
            grid=(rows // tile,),
            in_specs=[spec(kind, a.shape) for kind, a in ins],
            out_specs=[spec(kind, shape) for kind, shape, _ in outs],
            scratch_shapes=[pltpu.VMEM((tile, w), d) for w, d in scratch],
        ),
        out_shape=[jax.ShapeDtypeStruct(shape, dtype) for _, shape, dtype in outs],
        cost_estimate=SMALL,
    )(order, *[a for _, a in ins])


def columns(order_ref, width):
    count = order_ref.shape[0]
    bw = width // count
    if bw % 128:
        return [(slice(0, width), slice(0, width))]
    return [
        (slice(k * bw, (k + 1) * bw), pl.ds(pl.multiple_of(order_ref[k] * bw, 128), bw))
        for k in range(count)
    ]


def aligned(order, width):
    return (width // order.shape[0]) % 128 == 0


def into(a, order):
    return a if aligned(order, a.shape[1]) else gathered(a, order)


def outof(a, order):
    return a if aligned(order, a.shape[1]) else gathered(a, jnp.argsort(order))


def turn_kernel(order_ref, a_ref, t_ref):
    for there, here in columns(order_ref, a_ref.shape[1]):
        t_ref[there, :] = a_ref[:, here].T


def turned(a, order):
    out = row_call(turn_kernel, order, [("row", a)], [("col", a.shape[::-1], a.dtype)])[0]
    return out if aligned(order, a.shape[1]) else gathered(out.T, order).T


def norm_stats(values):
    mean = jnp.mean(values, axis=-1, keepdims=True)
    center = values - mean
    rate = lax.rsqrt(jnp.mean(center * center, axis=-1, keepdims=True) + EPS)
    return mean, rate, center * rate


def first_kernel(order_ref, tok_ref, gain_ref, out_ref, mean_ref, rate_ref, keep_ref):
    mean, rate, unit = norm_stats(tok_ref[...].astype(F32))
    keep_ref[...] = (unit * gain_ref[0:1] + gain_ref[1:2]).astype(BF16)
    for there, here in columns(order_ref, tok_ref.shape[1]):
        out_ref[:, there] = keep_ref[:, here]
    mean_ref[...] = mean
    rate_ref[...] = rate


def first_norm(tokens, gains, order):
    rows, width = tokens.shape
    out, mean, rate = row_call(
        first_kernel,
        order,
        [("row", tokens), ("all", gains)],
        [("row", (rows, width), BF16), ("row", (rows, 1), F32), ("row", (rows, 1), F32)],
        [(width, BF16)],
    )
    return into(out, order), mean, rate


def second_kernel(order_ref, tok_ref, *refs):
    *parts, gain_ref, nt_ref, ntt_ref, hid_ref, mean_ref, rate_ref, square_ref, keep_ref = refs
    width = tok_ref.shape[1]
    square = 0.0
    for there, here in columns(order_ref, width):
        branch = added([p[:, there] for p in parts])
        hid_ref[:, here] = tok_ref[:, here].astype(F32) + branch
        square = square + jnp.sum(branch * branch, axis=-1, keepdims=True)
    mean, rate, unit = norm_stats(hid_ref[...])
    keep_ref[...] = (unit * gain_ref[0:1] + gain_ref[1:2]).astype(BF16)
    nt_ref[...] = keep_ref[...]
    for there, here in columns(order_ref, width):
        ntt_ref[there, :] = keep_ref[:, here].T
    mean_ref[...] = mean
    rate_ref[...] = rate
    square_ref[...] = square


def second_norm(tokens, parts, gains, order):
    rows, width = tokens.shape
    parts = [outof(p, order) for p in parts]
    out = row_call(
        second_kernel,
        order,
        [("row", tokens), *[("row", p) for p in parts], ("all", gains)],
        [
            ("row", (rows, width), BF16),
            ("col", (width, rows), BF16),
            ("row", (rows, width), F32),
            ("row", (rows, 1), F32),
            ("row", (rows, 1), F32),
            ("row", (rows, 1), F32),
        ],
        [(width, BF16)],
    )
    if not aligned(order, width):
        out = [out[0], into(out[0], order).T, *out[2:]]
    return out


def norm_pull(d_normed, unit, rate, gain):
    scaled = d_normed * gain
    pull = scaled - jnp.mean(scaled, axis=-1, keepdims=True)
    return rate * (pull - unit * jnp.mean(scaled * unit, axis=-1, keepdims=True))


def gain_sums(grad_ref, d_normed, unit):
    @pl.when(pl.program_id(0) == 0)
    def _():
        grad_ref[...] = jnp.zeros_like(grad_ref)

    grad_ref[0:1] += jnp.sum(d_normed * unit, axis=0, keepdims=True)
    grad_ref[1:2] += jnp.sum(d_normed, axis=0, keepdims=True)


def second_back_kernel(order_ref, hid_ref, go_ref, mean_ref, rate_ref, gain_ref, *refs):
    *parts, low_ref, full_ref, grad_ref, keep_ref = refs
    rate = rate_ref[...]
    unit = (hid_ref[...] - mean_ref[...]) * rate
    d_normed = added([p[...] for p in parts])
    full = go_ref[...].astype(F32) + norm_pull(d_normed, unit, rate, gain_ref[0:1])
    full_ref[...] = full
    keep_ref[...] = full.astype(BF16)
    for there, here in columns(order_ref, hid_ref.shape[1]):
        low_ref[:, there] = keep_ref[:, here]
    gain_sums(grad_ref, d_normed, unit)


def second_back(hidden, go, mean, rate, gains, parts, order):
    rows, width = hidden.shape
    low, full, grad = row_call(
        second_back_kernel,
        order,
        [("row", hidden), ("row", go), ("row", mean), ("row", rate), ("all", gains)]
        + [("row", p) for p in parts],
        [("row", (rows, width), BF16), ("row", (rows, width), F32), ("all", (2, width), F32)],
        [(width, BF16)],
    )
    return into(low, order), full, grad


def first_back_kernel(order_ref, tok_ref, gh_ref, mean_ref, rate_ref, gain_ref, *refs):
    *parts, out_ref, grad_ref, keep_ref = refs
    rate = rate_ref[...]
    unit = (tok_ref[...].astype(F32) - mean_ref[...]) * rate
    for there, here in columns(order_ref, tok_ref.shape[1]):
        keep_ref[:, here] = added([p[:, there] for p in parts])
    d_normed = keep_ref[...]
    out_ref[...] = gh_ref[...] + norm_pull(d_normed, unit, rate, gain_ref[0:1])
    gain_sums(grad_ref, d_normed, unit)


def first_back(tokens, grad_hidden, mean, rate, gains, parts, order):
    rows, width = tokens.shape
    parts = [outof(p, order) for p in parts]
    return row_call(
        first_back_kernel,
        order,
        [("row", tokens), ("row", grad_hidden), ("row", mean), ("row", rate), ("all", gains)]
        + [("row", p) for p in parts],
        [("row", (rows, width), F32), ("all", (2, width), F32)],
        [(width, F32)],
    )


def ff_hidden(nt, go, up, down):
    pre = dot_nn(nt[...], up[...])
    d_act = dot_nn(go[...], down[...])
    square = pre * pre
    th = jnp.tanh(GELU_A * pre * (1.0 + GELU_B * square))
    gate = 0.5 * (1.0 + th)
    act = (pre * gate).astype(BF16)
    slope = gate + pre * (0.5 * GELU_A) * (1.0 - th * th) * (1.0 + 3.0 * GELU_B * square)
    return act, (d_act * slope).astype(BF16)


def ff_grads(act, d_pre, ntt, got, gm, gp):
    half = gm.shape[1]
    for g, rows in ((gm, slice(0, half)), (gp, slice(half, 2 * half))):
        g[0] = dot_nn(ntt[rows, :], d_pre).astype(g.dtype)
        g[1] = dot_nn(got[rows, :], act).astype(g.dtype)


def ff_first_kernel(nt, ntt, go, got, up, down, gm, gp, br, dn):
    @pl.when(pl.program_id(0) == 0)
    def _():
        br[...] = jnp.zeros_like(br)
        dn[...] = jnp.zeros_like(dn)

    act, d_pre = ff_hidden(nt, go, up, down)
    dn[...] += dot_nt(d_pre, up[...])
    br[...] += dot_nt(act, down[...])
    ff_grads(act, d_pre, ntt, got, gm, gp)


def ff_hidden_kernel(nt, go, up, down, dn_in, act_out, d_pre_out, dn, acc):
    @pl.when(pl.program_id(0) == 0)
    def _():
        acc[...] = dn_in[...]

    act, d_pre = ff_hidden(nt, go, up, down)
    act_out[...] = act
    d_pre_out[...] = d_pre
    acc[...] += dot_nt(d_pre, up[...])

    @pl.when(pl.program_id(0) == pl.num_programs(0) - 1)
    def _():
        dn[...] = acc[...].astype(dn.dtype)


def ff_grad_kernel(act, d_pre, ntt, got, down, br_in, gm, gp, br, acc):
    @pl.when(pl.program_id(0) == 0)
    def _():
        acc[...] = br_in[...]

    acc[...] += dot_nt(act[...], down[...])
    ff_grads(act[...], d_pre[...], ntt, got, gm, gp)

    @pl.when(pl.program_id(0) == pl.num_programs(0) - 1)
    def _():
        br[...] = acc[...].astype(br.dtype)


class FeedForward:
    def __init__(self, rows, width, n):
        self.rows, self.width, self.n = rows, width, n
        self.tile = min(FF_TILE, n)
        once = pl.Buffered(1)
        steps = n // self.tile
        self.full = pl.BlockSpec((rows, width), lambda j: (0, 0), pipeline_mode=once)
        self.full_t = pl.BlockSpec((width, rows), lambda j: (0, 0), pipeline_mode=once)
        self.up = pl.BlockSpec((width, self.tile), lambda j: (0, j))
        self.down = pl.BlockSpec((width, self.tile), lambda j: (0, steps + j))
        self.act = pl.BlockSpec((rows, self.tile), lambda j: (0, j))
        self.grad = pl.BlockSpec((2, width // 2, self.tile), lambda j: (0, 0, j))
        shape = jax.ShapeDtypeStruct
        self.grad_shape = shape((2, width // 2, n), BF16)
        self.act_shape = shape((rows, n), BF16)
        self.high = shape((rows, width), F32)
        self.low = shape((rows, width), BF16)

    def call(self, kernel, in_specs, out_specs, out_shape, args, scratch=1):
        return pl.pallas_call(
            kernel,
            grid=(self.n // self.tile,),
            in_specs=in_specs,
            out_specs=out_specs,
            out_shape=out_shape,
            scratch_shapes=[pltpu.VMEM((self.rows, self.width), F32)] * scratch,
            compiler_params=pltpu.CompilerParams(vmem_limit_bytes=56 * 1024 * 1024),
            cost_estimate=SMALL,
        )(*args)

    def first(self, nt, ntt, go, got, w):
        return self.call(
            ff_first_kernel,
            [self.full, self.full_t, self.full, self.full_t, self.up, self.down],
            [self.grad, self.grad, self.full, self.full],
            [self.grad_shape, self.grad_shape, self.high, self.high],
            (nt, ntt, go, got, w, w),
            0,
        )

    def hidden(self, nt, go, w, dn):
        return self.call(
            ff_hidden_kernel,
            [self.full, self.full, self.up, self.down, self.full],
            [self.act, self.act, self.full],
            [self.act_shape, self.act_shape, self.low],
            (nt, go, w, w, dn),
        )

    def grads(self, act, d_pre, ntt, got, w, br):
        return self.call(
            ff_grad_kernel,
            [self.act, self.act, self.full_t, self.full_t, self.down, self.full],
            [self.grad, self.grad, self.full],
            [self.grad_shape, self.grad_shape, self.low],
            (act, d_pre, ntt, got, w, br),
        )


def diagonal_mask(rows):
    keys = lax.broadcasted_iota(jnp.int32, (rows, rows), 0) // BLOCK
    queries = lax.broadcasted_iota(jnp.int32, (rows, rows), 1) // BLOCK
    return keys <= queries


def attn_kernel(scale, z_ref, q_ref, kv_ref, out_ref, low_ref, lse_ref, vt_ref):
    rows, size = q_ref.shape
    factor = scale * LOG2E
    tiles = z_ref[0] + 1

    @pl.when(pl.program_id(0) == 0)
    def _():
        def turn(t, _):
            vt_ref[t] = kv_ref[t, :, size:].T
            return 0

        lax.fori_loop(0, tiles, turn, 0)

    q = q_ref[...]
    scores = jnp.where(diagonal_mask(rows), dot_nt(kv_ref[0, :, :size], q), NEG)
    top = jnp.max(scores, axis=0, keepdims=True)
    probs = jnp.exp2(scores * factor - top * factor)
    total = jnp.sum(probs, axis=0, keepdims=True)
    acc = dot_nn(vt_ref[0], probs.astype(BF16))

    def step(t, carry):
        top, total, acc = carry
        scores = dot_nt(kv_ref[t, :, :size], q)
        new = jnp.maximum(top, jnp.max(scores, axis=0, keepdims=True))
        fade = jnp.exp2((top - new) * factor)
        probs = jnp.exp2(scores * factor - new * factor)
        total = total * fade + jnp.sum(probs, axis=0, keepdims=True)
        acc = acc * fade + dot_nn(vt_ref[t], probs.astype(BF16))
        return new, total, acc

    top, total, acc = lax.fori_loop(1, tiles, step, (top, total, acc))
    heads = acc / total
    out_ref[0] = heads
    low_ref[...] = heads.T.astype(BF16)
    lse_ref[0] = top * factor + jnp.log2(total)


def attn_call(scale, z, queries, kv):
    rows, cols = queries.shape
    tiles, _, two = kv.shape
    size = two // 2
    heads = cols // size
    shape = jax.ShapeDtypeStruct
    pairs = heads * rows * rows * tiles
    return pl.pallas_call(
        functools.partial(attn_kernel, scale),
        grid_spec=pltpu.PrefetchScalarGridSpec(
            num_scalar_prefetch=1,
            grid=(heads,),
            in_specs=[
                pl.BlockSpec((rows, size), lambda h, s: (0, h)),
                pl.BlockSpec(kv.shape, lambda h, s: (0, 0, 0)),
            ],
            out_specs=[
                pl.BlockSpec((1, size, rows), lambda h, s: (h, 0, 0)),
                pl.BlockSpec((rows, size), lambda h, s: (0, h)),
                pl.BlockSpec((1, 1, rows), lambda h, s: (h, 0, 0)),
            ],
            scratch_shapes=[pltpu.VMEM((tiles, size, rows), BF16)],
        ),
        out_shape=[
            shape((heads, size, rows), F32),
            shape((rows, cols), BF16),
            shape((heads, 1, rows), F32),
        ],
        compiler_params=pltpu.CompilerParams(vmem_limit_bytes=32 * 1024 * 1024),
        cost_estimate=SMALL,
    )(z, queries, kv)


def attn_back_kernel(scale, z_ref, q_ref, kv_ref, d_ref, out_ref, lse_ref, dq_ref, dkv_ref, kt_ref):
    rows, size = q_ref.shape
    factor = scale * LOG2E
    tiles = z_ref[0] + 1

    @pl.when(pl.program_id(0) == 0)
    def _():
        dkv_ref[...] = jnp.zeros_like(dkv_ref)

        def turn(t, _):
            kt_ref[t] = kv_ref[t, :, :size].T
            return 0

        lax.fori_loop(0, tiles, turn, 0)

    q, d_heads, lse = q_ref[...], d_ref[...], lse_ref[0]
    delta = jnp.sum(d_heads.astype(F32).T * out_ref[0], axis=0, keepdims=True)

    def tile(t, masked):
        scores = dot_nt(kv_ref[t, :, :size], q)
        probs = jnp.exp2(scores * factor - lse)
        if masked:
            probs = jnp.where(diagonal_mask(rows), probs, 0.0)
        d_probs = dot_nt(kv_ref[t, :, size:], d_heads)
        d_scores = (probs * (d_probs - delta)).astype(BF16)
        dkv_ref[t, :, :size] += dot_nn(d_scores, q)
        dkv_ref[t, :, size:] += dot_nn(probs.astype(BF16), d_heads)
        return dot_nn(kt_ref[t], d_scores)

    dqt = tile(0, True)
    dqt = lax.fori_loop(1, tiles, lambda t, total: total + tile(t, False), dqt)
    dq_ref[...] = (dqt * scale).T.astype(BF16)

    @pl.when(pl.program_id(0) == pl.num_programs(0) - 1)
    def _():
        dkv_ref[:, :, :size] = dkv_ref[:, :, :size] * scale


def attn_back_call(scale, z, queries, kv, d_heads, out, lse):
    rows, cols = queries.shape
    tiles, _, two = kv.shape
    size = two // 2
    heads = cols // size
    shape = jax.ShapeDtypeStruct
    pairs = heads * rows * rows * tiles
    row_spec = pl.BlockSpec((rows, size), lambda h, s: (0, h))
    kv_spec = pl.BlockSpec(kv.shape, lambda h, s: (0, 0, 0))
    return pl.pallas_call(
        functools.partial(attn_back_kernel, scale),
        grid_spec=pltpu.PrefetchScalarGridSpec(
            num_scalar_prefetch=1,
            grid=(heads,),
            in_specs=[
                row_spec,
                kv_spec,
                row_spec,
                pl.BlockSpec((1, size, rows), lambda h, s: (h, 0, 0)),
                pl.BlockSpec((1, 1, rows), lambda h, s: (h, 0, 0)),
            ],
            out_specs=[row_spec, kv_spec],
            scratch_shapes=[pltpu.VMEM((tiles, size, rows), BF16)],
        ),
        out_shape=[shape((rows, cols), BF16), shape(kv.shape, F32)],
        compiler_params=pltpu.CompilerParams(vmem_limit_bytes=32 * 1024 * 1024),
        cost_estimate=SMALL,
    )(z, queries, kv, d_heads, out, lse)


def body(
    tokens, gain_one, bias_one, w_query, w_keyval, w_out, gain_two, bias_two, w_up, w_down, grad_out
):
    ring, todo = Ring(), Order()
    run = todo.run
    nz = ring.nz
    rows, width = tokens.shape
    half = width // 2
    own_d = w_keyval.shape[0]
    head_size = w_keyval.shape[1] // 2
    ff_cols = w_up.shape[1]
    scale = head_size ** (-0.5)
    z = lax.axis_index("ctx").astype(jnp.int32)[None]
    order = ring.order()
    entries = rows * ring.ndp * nz * width
    split = FF_SPLIT if sum(FF_SPLIT) == ff_cols else (ff_cols // 2, ff_cols - ff_cols // 2)

    small = jnp.stack([gain_one, bias_one, gain_two, bias_two])
    small = jnp.pad(small, ((0, 12), (0, w_keyval.shape[1] - own_d)))
    kv_shard = jnp.concatenate([w_keyval, small], axis=0)

    def sides(parts):
        across = [ring.x_all(p) for p in parts]
        return parts + [s[k] for k in range(ring.nx - 1) for s in across]

    kv_blocks = sides([kv_shard, *ring.z_all(kv_shard)])
    q_parts = [w_query, *ring.z_all(w_query)]
    got = run(turned, grad_out, order)
    kv_mine = run(join(0), *kv_blocks, wait=(q_parts[1], q_parts[-1]))
    kv_other = ring.core(kv_mine)
    q_blocks = sides(q_parts)

    cols_a, cols_b = slice(0, split[0]), slice(split[0], ff_cols)
    both = ("dp", "ctx")

    def ff_shard(cols, *others):
        return after(jnp.concatenate([w_up[:, cols], w_down[:, cols]], axis=1), *others)

    ff_a = lax.all_gather(ff_shard(cols_a, q_parts[1]), both, axis=0, tiled=True)
    ff_b = lax.all_gather(ff_shard(cols_b, q_parts[1]), both, axis=0, tiled=True)

    def split_rows(*kv_rows):
        parts = [r.reshape(-1, own_d + 16, r.shape[1]) for r in kv_rows]
        weights = [p[:, :own_d].reshape(half, -1) for p in parts]
        small = jnp.concatenate([p[:, own_d : own_d + 4, :own_d] for p in parts], axis=0)
        small = small.transpose(1, 0, 2).reshape(4, width)
        return weights, gathered(small, jnp.argsort(order)).astype(F32)

    w_kv, gains = run(split_rows, kv_mine, kv_other)
    normed, mean1, rate1 = run(first_norm, tokens, gains[0:2], order)

    def project(normed, mine, other):
        return (dot_nn(normed[:, :half], mine) + dot_nn(normed[:, half:], other)).astype(BF16)

    keyval = run(project, normed, *w_kv)
    tiles = [keyval, *ring.z_all(keyval)]
    q_mine = run(join(0), *q_blocks)
    q_other = ring.core(q_mine)
    o_parts = [w_out, *ring.z_all(after(w_out, q_mine))]
    o_blocks = sides(o_parts)
    queries = run(project, normed, q_mine, q_other)
    keyval_all = run(lambda *t: jnp.stack(t), *tiles, wait=(o_parts[1], o_parts[-1]))
    attn_t, attn_low, lse = run(lambda q, kv: attn_call(scale, z, q, kv), queries, keyval_all)
    o_mine = run(join(0), *o_blocks)
    o_other = ring.core(o_mine)

    def widened(a, mine, other):
        return jnp.concatenate([dot_nt(a, mine), dot_nt(a, other)], axis=1).astype(BF16)

    part = run(widened, attn_low, o_mine, o_other)
    parts = [part, *tp_others(part)]
    nt, ntt, hidden, mean2, rate2, attn_square = run(
        lambda *a: second_norm(a[0], a[2:], a[1], order), tokens, gains[2:4], *parts
    )

    def scatter_core(pieces):
        return [(m, ring.core(o)) for m, o in pieces]

    def scatter_x(pair, axis):
        mine, other = pair
        across = run(lambda m, o: ring.side_parts(m, o, axis), mine, other)
        return mine, other, [ring.x(p, -k - 1) for k, p in enumerate(across)]

    far = nz // 2

    def scatter_z(triple, axis):
        blocks = run(lambda m, o, c: ring.block_parts(m, o, c, axis), *triple)
        downs = ring.z(blocks[far], -1) if far else None
        ups = ring.z(blocks[far + 1], 1) if far + 1 < nz else None
        return blocks, downs, ups

    def plus(a, b):
        return (a.astype(F32) + b.astype(F32)).astype(BF16)

    def scatter_mid(state):
        blocks, downs, ups = state
        for k in range(far - 1, 0, -1):
            downs = ring.z(run(plus, blocks[k], downs), -1)
        for k in range(far + 2, nz):
            ups = ring.z(run(plus, blocks[k], ups), 1)
        return [blocks[0]] + [m for m in (downs, ups) if m is not None]

    def scatter_end(parts):
        return run(lambda *p: added(p), *parts)

    def halves(gm, gp):
        return [(gm[k : k + 1], gp[k : k + 1]) for k in (1, 0)]

    ff1 = FeedForward(rows, width, split[0])
    ff2 = FeedForward(rows, width, split[1])
    gm, gp, br, dn = run(ff1.first, nt, ntt, grad_out, got, ff_a)
    a_c = scatter_core(halves(gm, gp))
    a0 = scatter_x(a_c[0], 1)
    a1 = scatter_x(a_c[1], 1)
    act, d_pre, dn = run(ff2.hidden, nt, grad_out, ff_b, dn)
    dn_parts = [dn, *tp_others(dn)]
    gm, gp, br = run(ff2.grads, act, d_pre, ntt, got, ff_b, br)
    b_c = scatter_core(halves(gm, gp))
    a0 = scatter_z(a0, 1)
    b0 = scatter_x(b_c[0], 1)
    b1 = scatter_x(b_c[1], 1)
    a0 = scatter_mid(a0)
    d_branch, grad_hidden, d_two = run(
        lambda *a: second_back(*a[:5], a[5:], order),
        hidden, grad_out, mean2, rate2, gains[2:3], *dn_parts,
    )
    br_parts = [br, *tp_others(after(br, dn_parts[-1]))]
    d_heads = run(project, d_branch, o_mine, o_other)
    a1 = scatter_z(a1, 1)
    dq, dkv = run(
        lambda *a: attn_back_call(scale, z, *a), queries, keyval_all, d_heads, attn_t, lse,
        wait=a0,
    )
    sends = run(lambda d: [d[k].astype(BF16) for k in range(1, nz)], dkv)
    got_kv = [ring.z(s, -k - 1) for k, s in enumerate(sends)]
    dq_part = run(widened, dq, q_mine, q_other)
    dq_parts = [dq_part, *tp_others(after(dq_part, br_parts[-1]))]
    a1 = scatter_mid(a1)

    def outer(a, b):
        full = dot_tn(a, b).astype(BF16)
        return full[:half], full[half:]

    b0 = scatter_z(b0, 1)
    g_out = run(outer, d_branch, attn_low)
    g_q = run(outer, normed, dq)
    o_c, q_c = scatter_core([g_out, g_q])
    mine_kv = run(lambda d, *g: added([d[0], *g]).astype(BF16), dkv, *got_kv)
    kv_parts = [mine_kv, *tp_others(mine_kv)]

    def finish(hidden, *parts):
        branch = added(parts)
        result = hidden + branch
        return result.astype(BF16), jnp.sum(result * result), jnp.sum(branch * branch)

    layer_out, square_r, square_m = run(finish, hidden, *br_parts)
    squares = jnp.stack([square_r, jnp.sum(attn_square), square_m])
    rms_values = jnp.sqrt(ring.small_sum(jnp.broadcast_to(squares[:, None], (3, 128)))[:, 0] / entries)
    o_s = scatter_x(o_c, 0)
    q_s = scatter_x(q_c, 0)
    dkv_low = run(lambda *p: added(p).astype(BF16), *kv_parts)
    g_kv = run(outer, normed, dkv_low)
    kv_c = scatter_core([g_kv])[0]
    dkv_part = run(widened, dkv_low, *w_kv)
    b0 = scatter_mid(b0)
    kv_s = scatter_x(kv_c, 0)
    a1_end = scatter_end(a1)
    a0_end = scatter_end(a0)
    input_grad, d_one = run(
        lambda *a: first_back(*a[:5], a[5:], order),
        tokens, grad_hidden, mean1, rate1, gains[0:1], *dq_parts, dkv_part,
    )
    small = ring.small_scatter(gathered(jnp.concatenate([d_one, d_two], axis=0), order))
    b1 = scatter_z(b1, 1)
    o_s = scatter_z(o_s, 0)
    b0_end = scatter_end(b0)
    b1 = scatter_mid(b1)
    q_s = scatter_z(q_s, 0)
    o_s = scatter_mid(o_s)
    kv_s = scatter_z(kv_s, 0)
    q_s = scatter_mid(q_s)
    kv_s = scatter_mid(kv_s)
    b1_end = scatter_end(b1)
    grad_out_proj, grad_query, grad_keyval = (scatter_end(e) for e in (o_s, q_s, kv_s))
    grad_down = jnp.concatenate([a0_end[0], b0_end[0]], axis=1)
    grad_up = jnp.concatenate([a1_end[0], b1_end[0]], axis=1)
    return (
        layer_out, input_grad, small[0], small[1], grad_query, grad_keyval, grad_out_proj,
        small[2], small[3], grad_up, grad_down, rms_values,
    )


def solution(mesh):
    rows2, vec, split = P(("dp", "ctx"), None), P(("dp", "ctx")), P(("dp", "ctx"), "tp")
    return jax.shard_map(
        body,
        mesh=mesh,
        in_specs=(rows2, vec, vec, split, rows2, split, vec, vec, split, split, rows2),
        out_specs=(rows2, rows2, vec, vec, split, rows2, split, vec, vec, split, split, P()),
        check_vma=False,
    )
```

time: 1120 us -> 780 us (0.70)
  waiting for transfers between devices: 696 us -> 382 us
  starting transfers between devices: 56.9 us -> 112 us
  other arithmetic: 105 us -> 67.6 us
  local copies, waits for them, and re-layouts: 74.7 us -> 38.9 us
  matrix products: 54.2 us -> 21 us
  Pallas kernels: 121 us -> 136 us
  between operations: 2.86 us -> 15.7 us
    ppermute x90 -> x79, waiting for transfers between devices: 696 us -> 350 us  [the longest x39 158 us: z(): lax.ppermute(value, 'ctx', [(i, (i + k) % self.nz) for i in range(self.nz)])]
    ppermute x90 -> x79, starting transfers between devices: 56.9 us -> 112 us  [the longest x39 79.2 us: z(): lax.ppermute(value, 'ctx', [(i, (i + k) % self.nz) for i in range(self.nz)])]
    all_gather x0 -> x2, waiting for transfers between devices: none -> 31.8 us  [the longest x1 31.8 us: body(): lax.all_gather(ff_shard(cols_b, q_parts[1]), both, axis=0, tiled=True)]
    unnamed x190 -> x161, local copies, waits for them, and re-layouts: 36.3 us -> 13.9 us
    dot_general x7 -> x0, matrix products: 21.5 us -> none  [the longest x2 6.15 us: tile_scores(): jnp.einsum('qhd,kd->hqk', query_heads, key_tile, preferred_element_type=F32)]
    slice x13 -> x18, local copies, waits for them, and re-layouts: 3.74 us -> 22 us  [the longest x4 15 us: halves(): return [(gm[k:k + 1], gp[k:k + 1]) for k in (1, 0)]]
    reduce_sum x10 -> x2, other arithmetic: 25.6 us -> 7.52 us  [the longest x1 6.85 us: finish(): jnp.sum(result * result)]
    add x25 -> x13, other arithmetic: 25.8 us -> 7.83 us  [the longest x9 6.33 us: added(): out = out + p.astype(F32)]
  transfers between devices with their start and end apart: 90 -> 81, of which waited for: 54 -> 33; matrix products, arithmetic and copies ran while one was open for 20% -> 14% of each run, Pallas kernels for 9% -> 12%
where the time goes in v2:
time: 780 us; the launch traced here: 774 us
  waiting for transfers between devices  382 us (49%)
  Pallas kernels  136 us (17%)
  starting transfers between devices  112 us (14%)
  other arithmetic  67.6 us (9%)
  local copies, waits for them, and re-layouts  38.9 us (5%)
  matrix products  21 us (3%)
  between operations  15.7 us (2%)
    ppermute x39, waiting for transfers between devices, z(): lax.ppermute(value, 'ctx', [(i, (i + k) % self.nz) for i in range(self.nz)])  158 us
    ppermute x5, waiting for transfers between devices, tp_others(): lax.ppermute(part, 'tp', [(i, (i + k) % n) for i in range(n)])  131 us
    pallas_call x3, Pallas kernels, call(): pl.pallas_call(kernel, grid=(self.n // self.tile,), in_specs=in_specs, ou...  82.3 us
    ppermute x39, starting transfers between devices, z(): lax.ppermute(value, 'ctx', [(i, (i + k) % self.nz) for i in range(self.nz)])  79.2 us
    pallas_call x5, Pallas kernels, row_call(): pl.pallas_call(kernel, grid_spec=pltpu.PrefetchScalarGridSpec(num_scalar_...  38.2 us
    all_gather x1, waiting for transfers between devices, body(): lax.all_gather(ff_shard(cols_b, q_parts[1]), both, axis=0, tiled=True)  31.8 us
    ppermute x20, waiting for transfers between devices, x(): lax.ppermute(value, 'dp', [(i, (i + 2 * k) % self.ndp) for i in range(sel...  31.8 us
    convert_element_type x7, other arithmetic, block_parts(): out.append(part.astype(BF16) if k else part)  20.3 us
  transfers between devices with their start and end apart: 81, of which 33 were waited for; matrix products, arithmetic and copies ran while one was open for 14% of the time, Pallas kernels for 12%

profile of v2, /device:TPU:0, one launch (start us, length us, event | category | flops | bytes accessed | tf_op | source)
XLA Modules:
  0.0 773.6 jit_solution(2234857778269241845)
XLA Ops:
  50.0 14.3 %collective-permute-done.10 = bf16[128,1024]{1,0:T(8,128)(2,1)S(1)} collective-permute-done((bf16[128,1024]{1,0:T(8,128)(2,1)S(1)}, bf16[128,1024]{1,0:T(8,128)(2,1)S(1)}, u32[]{:S(2)}, u32[]{:S(2)}) %collective-permute-start.10) | collective-permute-done | bytes 262176 | tf_op jit(solution)/shard_map/ppermute | solution.py:62
  87.5 10.3 %collective-permute-start.20 = (bf16[128,1024]{1,0:T(8,128)(2,1)S(1)}, bf16[128,1024]{1,0:T(8,128)(2,1)S(1)}, u32[]{:S(2)}, u32[]{:S(2)}) collective-permute-start(bf16[128,1024]{1,0:T(8,128)(2,1)S(1)} %copy-done.43), channel_id=1, source_target_pairs={{0,6},{2,0},{4,2},{6,4},{1,7},{3,1},{5,3},{7,5},{8,14},{10,8},{12,... | collective-permute-start | bytes 786440 | tf_op jit(solution)/shard_map/ppermute | solution.py:62
  99.1 7.8 %collective-permute-done.18 = bf16[512,256]{1,0:T(8,128)(2,1)S(1)} collective-permute-done((bf16[512,256]{1,0:T(8,128)(2,1)S(1)}, bf16[512,256]{1,0:T(8,128)(2,1)S(1)}, u32[]{:S(2)}, u32[]{:S(2)}) %collective-permute-start.18) | collective-permute-done | bytes 262176 | tf_op jit(solution)/shard_map/ppermute | solution.py:62
  117.0 11.1 %collective-permute-done.20 = bf16[128,1024]{1,0:T(8,128)(2,1)S(1)} collective-permute-done((bf16[128,1024]{1,0:T(8,128)(2,1)S(1)}, bf16[128,1024]{1,0:T(8,128)(2,1)S(1)}, u32[]{:S(2)}, u32[]{:S(2)}) %collective-permute-start.20) | collective-permute-done | bytes 262176 | tf_op jit(solution)/shard_map/ppermute | solution.py:62
  161.8 46.1 %collective-permute-done.27.refs_1_ = bf16[512,2048]{1,0:T(8,128)(2,1)S(1)} collective-permute-done((bf16[512,2048]{1,0:T(8,128)(2,1)S(1)}, bf16[512,2048]{1,0:T(8,128)(2,1)S(1)}, u32[]{:S(2)}, u32[]{:S(2)}) %collective-permute-start.27) | collective-permute-done | bytes 2097184 | tf_op jit(solution)/shard_map/ppermute | solution.py:146
  209.2 9.0 %shard_map.205 = (bf16[512,2048]{1,0:T(8,128)(2,1)}, bf16[2048,512]{1,0:T(8,128)(2,1)}, f32[512,2048]{1,0:T(8,128)}, f32[512,1]{1,0:T(8,128)}, f32[512,1]{1,0:T(8,128)}, /*index=5*/f32[512,1]{1,0:T(8,128)}) custom-call(s32[16]{0:T(128)} %copy-done.52, bf16[512,2048]{1,0:T(8,128)(2,1)} %tok_ref.2, bf16[512,2048]{1,0:T(8,128)(2,1)} %copy-done.10, ...), custom_call_target="tpu_custom_call" | custom-call | flops 1000 | bytes 1000 | tf_op jit(solution)/shard_map/pallas_call | solution.py:166
  218.3 36.8 %shard_map.206 = (bf16[2,1024,2048]{2,1,0:T(8,128)(2,1)}, bf16[2,1024,2048]{2,1,0:T(8,128)(2,1)}, f32[512,2048]{1,0:T(8,128)}, f32[512,2048]{1,0:T(8,128)}) custom-call(bf16[512,2048]{1,0:T(8,128)(2,1)} %get-tuple-element.299.nt, bf16[2048,512]{1,0:T(8,128)(2,1)} %get-tuple-element.308.ntt, bf16[512,2048]{1,0:T(8,128)(2,1)} %go_ref, ...), custom_call_target="tpu_custom_call" | custom-call | flops 1000 | bytes 1000 | tf_op jit(solution)/shard_map/pallas_call | solution.py:423
  263.7 10.2 %collective-permute-done.29 = bf16[1,1024,2048]{2,1,0:T(8,128)(2,1)S(1)} collective-permute-done((bf16[1,1024,2048]{2,1,0:T(8,128)(2,1)}, bf16[1,1024,2048]{2,1,0:T(8,128)(2,1)S(1)}, u32[]{:S(2)}, u32[]{:S(2)}) %collective-permute-start.29) | collective-permute-done | bytes 4194336 | tf_op jit(solution)/shard_map/ppermute | solution.py:68
  280.9 31.8 %all-gather.3.cloned.1.call-done.up.down = bf16[2048,4096]{1,0:T(8,128)(2,1)} async-done(((bf16[128,4096]{1,0:T(8,128)(2,1)}), bf16[2048,4096]{1,0:T(8,128)(2,1)}) %all-gather.3.cloned.1.call-update) | async-done | bytes 16777232 | tf_op jit(solution)/shard_map/all_gather | solution.py:646
  312.7 23.1 %shard_map.207 = (bf16[512,2048]{1,0:T(8,128)(2,1)}, bf16[512,2048]{1,0:T(8,128)(2,1)}, bf16[512,2048]{1,0:T(8,128)(2,1)}) custom-call(bf16[512,2048]{1,0:T(8,128)(2,1)} %get-tuple-element.299.nt, bf16[512,2048]{1,0:T(8,128)(2,1)} %go_ref, bf16[2048,4096]{1,0:T(8,128)(2,1)} %all-gather.3.cloned.1.call-done.up.down, ...), custom_call_target="tpu_custom_call" | custom-call | flops 1000 | bytes 1000 | tf_op jit(solution)/shard_map/pallas_call | solution.py:423
  335.8 22.5 %shard_map.208 = (bf16[2,1024,2048]{2,1,0:T(8,128)(2,1)}, bf16[2,1024,2048]{2,1,0:T(8,128)(2,1)}, bf16[512,2048]{1,0:T(8,128)(2,1)}) custom-call(bf16[512,2048]{1,0:T(8,128)(2,1)} %get-tuple-element.306.act, bf16[512,2048]{1,0:T(8,128)(2,1)} %get-tuple-element.307.d_pre, bf16[2048,512]{1,0:T(8,128)(2,1)} %get-tuple-element.308.ntt, ...), custom_call_target="tpu_custom_call" | custom-call | flops 1000 | bytes 1000 | tf_op jit(solution)/shard_map/pallas_call | solution.py:423
  371.3 42.5 %collective-permute-done.30.refs_1_ = bf16[512,2048]{1,0:T(8,128)(2,1)} collective-permute-done((bf16[512,2048]{1,0:T(8,128)(2,1)S(1)}, bf16[512,2048]{1,0:T(8,128)(2,1)}, u32[]{:S(2)}, u32[]{:S(2)}) %collective-permute-start.30) | collective-permute-done | bytes 2097184 | tf_op jit(solution)/shard_map/ppermute | solution.py:146
  429.8 14.2 %collective-permute-done.33 = bf16[1,128,2048]{2,1,0:T(8,128)(2,1)S(1)} collective-permute-done((bf16[1,128,2048]{2,1,0:T(8,128)(2,1)S(1)}, bf16[1,128,2048]{2,1,0:T(8,128)(2,1)S(1)}, u32[]{:S(2)}, u32[]{:S(2)}) %collective-permute-start.33) | collective-permute-done | bytes 524320 | tf_op jit(solution)/shard_map/ppermute | solution.py:62
  447.3 9.2 %shard_map.209 = (bf16[512,2048]{1,0:T(8,128)(2,1)}, f32[512,2048]{1,0:T(8,128)}, f32[2,2048]{1,0:T(2,128)}) custom-call(s32[16]{0:T(128)} %copy-done.52, f32[512,2048]{1,0:T(8,128)} %get-tuple-element.367.hid_ref, bf16[512,2048]{1,0:T(8,128)(2,1)} %go_ref, f32[512,1]{1,0:T(8,128)} %get-tuple-element.330.mean_ref, f32[512,1]{1,0:T(8,128)} %get-tuple-element.331.rate_ref, ...), custom_call_target="tpu_custom_call" | custom-call | flops 1000 | bytes 1000 | tf_op jit(solution)/shard_map/pallas_call | solution.py:166
  469.1 8.4 %shard_map.210 = (bf16[512,1024]{1,0:T(8,128)(2,1)S(1)}, f32[4,512,256]{2,1,0:T(8,128)S(1)}) custom-call(s32[1]{0:T(128)} %bitcast.26.z_ref, bf16[512,1024]{1,0:T(8,128)(2,1)S(1)} %add_convert_fusion.7.q_ref, bf16[4,512,256]{2,1,0:T(8,128)(2,1)S(1)} %pad_maximum_fusion.5.kv_ref, bf16[512,1024]{1,0:T(8,128)(2,1)S(1)} %add_convert_fusion.6.d_ref, ...), custom_call_target="tpu_custom_call" | custom-call | flops 1000 | bytes 1000 | tf_op jit(solution)/shard_map/pallas_call | solution.py:586
  491.2 13.9 %collective-permute-done.42 = bf16[1,512,2048]{2,1,0:T(8,128)(2,1)} collective-permute-done((bf16[1,512,2048]{2,1,0:T(8,128)(2,1)}, bf16[1,512,2048]{2,1,0:T(8,128)(2,1)}, u32[]{:S(2)}, u32[]{:S(2)}) %collective-permute-start.42) | collective-permute-done | bytes 2097184 | tf_op jit(solution)/shard_map/ppermute | solution.py:65
  521.0 11.6 %collective-permute-done.40 = bf16[512,256]{1,0:T(8,128)(2,1)} collective-permute-done((bf16[512,256]{1,0:T(8,128)(2,1)}, bf16[512,256]{1,0:T(8,128)(2,1)}, u32[]{:S(2)}, u32[]{:S(2)}) %collective-permute-start.40) | collective-permute-done | bytes 262176 | tf_op jit(solution)/shard_map/ppermute | solution.py:62
  560.2 42.6 %collective-permute-done.45 = bf16[512,256]{1,0:T(8,128)(2,1)S(1)} collective-permute-done((bf16[512,256]{1,0:T(8,128)(2,1)S(1)}, bf16[512,256]{1,0:T(8,128)(2,1)S(1)}, u32[]{:S(2)}, u32[]{:S(2)}) %collective-permute-start.45) | collective-permute-done | bytes 262176 | tf_op jit(solution)/shard_map/ppermute | solution.py:146
  612.0 9.8 %collective-permute-done.48 = bf16[1,128,2048]{2,1,0:T(8,128)(2,1)S(1)} collective-permute-done((bf16[1,128,2048]{2,1,0:T(8,128)(2,1)S(1)}, bf16[1,128,2048]{2,1,0:T(8,128)(2,1)S(1)}, u32[]{:S(2)}, u32[]{:S(2)}) %collective-permute-start.48) | collective-permute-done | bytes 524320 | tf_op jit(solution)/shard_map/ppermute | solution.py:62
  626.6 9.6 %shard_map.211 = (f32[512,2048]{1,0:T(8,128)}, f32[2,2048]{1,0:T(2,128)}) custom-call(s32[16]{0:T(128)} %copy-done.52, bf16[512,2048]{1,0:T(8,128)(2,1)} %tok_ref.2, f32[512,2048]{1,0:T(8,128)} %get-tuple-element.396.gh_ref, f32[512,1]{1,0:T(8,128)} %get-tuple-element.397.mean_ref, f32[512,1]{1,0:T(8,128)} %get-tuple-element.398.rate_ref, ...), custom_call_target="tpu_custom_call" | custom-call | flops 1000 | bytes 1000 | tf_op jit(solution)/shard_map/pallas_call | solution.py:166
  647.5 12.1 %collective-permute-done.78 = f32[3,128]{0,1:T(8,128)S(1)} collective-permute-done((f32[3,128]{0,1:T(8,128)S(1)}, f32[3,128]{0,1:T(8,128)S(1)}, u32[]{:S(2)}, u32[]{:S(2)}) %collective-permute-start.78) | collective-permute-done | bytes 1568 | tf_op jit(solution)/shard_map/ppermute | solution.py:120
  673.8 12.6 %collective-permute-done.62 = bf16[512,1024]{1,0:T(8,128)(2,1)S(1)} collective-permute-done((bf16[512,1024]{1,0:T(8,128)(2,1)}, bf16[512,1024]{1,0:T(8,128)(2,1)S(1)}, u32[]{:S(2)}, u32[]{:S(2)}) %collective-permute-start.62) | collective-permute-done | bytes 1048608 | tf_op jit(solution)/shard_map/ppermute | solution.py:65
  692.3 21.9 %collective-permute-done.59 = bf16[1,128,2048]{2,1,0:T(8,128)(2,1)S(1)} collective-permute-done((bf16[1,128,2048]{2,1,0:T(8,128)(2,1)S(1)}, bf16[1,128,2048]{2,1,0:T(8,128)(2,1)S(1)}, u32[]{:S(2)}, u32[]{:S(2)}) %collective-permute-start.59) | collective-permute-done | bytes 524320 | tf_op jit(solution)/shard_map/ppermute | solution.py:62
  726.7 19.6 %collective-permute-done.63 = bf16[128,1024]{1,0:T(8,128)(2,1)S(1)} collective-permute-done((bf16[128,1024]{1,0:T(8,128)(2,1)S(1)}, bf16[128,1024]{1,0:T(8,128)(2,1)S(1)}, u32[]{:S(2)}, u32[]{:S(2)}) %collective-permute-start.63) | collective-permute-done | bytes 262176 | tf_op jit(solution)/shard_map/ppermute | solution.py:62
  (419 shorter events, 306.9 us)
Async XLA Ops:
  7.2 211.1 %all-gather.5.cloned.1.call-start = ((), (), s32[]{:S(2)}) async-start(), calls=%async_computation.1 | async-start | bytes 17825792 | tf_op jit(solution)/shard_map/all_gather | solution.py:645
  18.9 293.8 %all-gather.3.cloned.1.call-start = ((), (), s32[]{:S(2)}) async-start(), calls=%async_computation | async-start | bytes 17825792 | tf_op jit(solution)/shard_map/all_gather | solution.py:646
  75.4 75.2 %collective-permute-start.22 = (bf16[128,1024]{1,0:T(8,128)(2,1)S(1)}, bf16[128,1024]{1,0:T(8,128)(2,1)S(1)}, u32[]{:S(2)}, u32[]{:S(2)}) collective-permute-start(bf16[128,1024]{1,0:T(8,128)(2,1)S(1)} %copy-done.43), channel_id=1, source_target_pairs={{0,16},{8,24},{16,0},{24,8},{1,17},{9,25},{17,1},{25,9},{2,18},{10... | collective-permute-start | bytes 786440 | tf_op jit(solution)/shard_map/ppermute | solution.py:65
  107.0 43.6 %collective-permute-start.23 = (bf16[128,1024]{1,0:T(8,128)(2,1)S(1)}, bf16[128,1024]{1,0:T(8,128)(2,1)S(1)}, u32[]{:S(2)}, u32[]{:S(2)}) collective-permute-start(bf16[128,1024]{1,0:T(8,128)(2,1)S(1)} %collective-permute-done.19), channel_id=1, source_target_pairs={{0,16},{8,24},{16,0},{24,8},{1,17},{9,25},{17,1},{25,9},{2,18},{10... | collective-permute-start | bytes 786440 | tf_op jit(solution)/shard_map/ppermute | solution.py:65
  160.2 47.7 %collective-permute-start.27 = (bf16[512,2048]{1,0:T(8,128)(2,1)S(1)}, bf16[512,2048]{1,0:T(8,128)(2,1)S(1)}, u32[]{:S(2)}, u32[]{:S(2)}) collective-permute-start(bf16[512,2048]{1,0:T(8,128)(2,1)S(1)} %pad_maximum_fusion.refs_0_), channel_id=1, source_target_pairs={{0,1},{1,0},{2,3},{3,2},{4,5},{5,4},{6,7},{7,6},{8,9},{9,8},{10,11... | collective-permute-start | bytes 6291464 | tf_op jit(solution)/shard_map/ppermute | solution.py:146
  365.4 55.3 %collective-permute-start.35 = (bf16[1,1024,2048]{2,1,0:T(8,128)(2,1)}, bf16[1,1024,2048]{2,1,0:T(8,128)(2,1)S(1)}, u32[]{:S(2)}, u32[]{:S(2)}) collective-permute-start(bf16[1,1024,2048]{2,1,0:T(8,128)(2,1)} %get-tuple-element.461), channel_id=1, source_target_pairs={{0,8},{8,0},{16,24},{24,16},{1,9},{9,1},{17,25},{25,17},{2,10},{10... | collective-permute-start | bytes 12582920 | tf_op jit(solution)/shard_map/ppermute | solution.py:68
  365.6 61.3 %collective-permute-start.34 = (bf16[1,1024,2048]{2,1,0:T(8,128)(2,1)}, bf16[1,1024,2048]{2,1,0:T(8,128)(2,1)S(1)}, u32[]{:S(2)}, u32[]{:S(2)}) collective-permute-start(bf16[1,1024,2048]{2,1,0:T(8,128)(2,1)} %get-tuple-element.462), channel_id=1, source_target_pairs={{0,8},{8,0},{16,24},{24,16},{1,9},{9,1},{17,25},{25,17},{2,10},{10... | collective-permute-start | bytes 12582920 | tf_op jit(solution)/shard_map/ppermute | solution.py:68
  365.9 47.9 %collective-permute-start.30 = (bf16[512,2048]{1,0:T(8,128)(2,1)S(1)}, bf16[512,2048]{1,0:T(8,128)(2,1)}, u32[]{:S(2)}, u32[]{:S(2)}) collective-permute-start(bf16[512,2048]{1,0:T(8,128)(2,1)S(1)} %copy-done.24), channel_id=1, source_target_pairs={{0,1},{1,0},{2,3},{3,2},{4,5},{5,4},{6,7},{7,6},{8,9},{9,8},{10,11... | collective-permute-start | bytes 6291464 | tf_op jit(solution)/shard_map/ppermute | solution.py:146
  367.4 48.8 %collective-permute-start.32 = (bf16[1,512,2048]{2,1,0:T(8,128)(2,1)}, bf16[1,512,2048]{2,1,0:T(8,128)(2,1)}, u32[]{:S(2)}, u32[]{:S(2)}) collective-permute-start(bf16[1,512,2048]{2,1,0:T(8,128)(2,1)} %add_convert_fusion.3), channel_id=1, source_target_pairs={{0,16},{8,24},{16,0},{24,8},{1,17},{9,25},{17,1},{25,9},{2,18},{10... | collective-permute-start | bytes 6291464 | tf_op jit(solution)/shard_map/ppermute | solution.py:65
  368.5 92.6 %collective-permute-start.36 = (bf16[1,512,2048]{2,1,0:T(8,128)(2,1)}, bf16[1,512,2048]{2,1,0:T(8,128)(2,1)}, u32[]{:S(2)}, u32[]{:S(2)}) collective-permute-start(bf16[1,512,2048]{2,1,0:T(8,128)(2,1)} %add_convert_fusion.2), channel_id=1, source_target_pairs={{0,16},{8,24},{16,0},{24,8},{1,17},{9,25},{17,1},{25,9},{2,18},{10... | collective-permute-start | bytes 6291464 | tf_op jit(solution)/shard_map/ppermute | solution.py:65
  413.8 121.3 %collective-permute-start.31 = (bf16[512,2048]{1,0:T(8,128)(2,1)}, bf16[512,2048]{1,0:T(8,128)(2,1)}, u32[]{:S(2)}, u32[]{:S(2)}) collective-permute-start(bf16[512,2048]{1,0:T(8,128)(2,1)} %get-tuple-element.368), channel_id=1, source_target_pairs={{0,1},{1,0},{2,3},{3,2},{4,5},{5,4},{6,7},{7,6},{8,9},{9,8},{10,11... | collective-permute-start | bytes 6291464 | tf_op jit(solution)/shard_map/ppermute | solution.py:146
  420.7 48.4 %collective-permute-start.38 = (bf16[1,128,2048]{2,1,0:T(8,128)(2,1)}, bf16[1,128,2048]{2,1,0:T(8,128)(2,1)}, u32[]{:S(2)}, u32[]{:S(2)}) collective-permute-start(bf16[1,128,2048]{2,1,0:T(8,128)(2,1)} %get-tuple-element.456), channel_id=1, source_target_pairs={{0,2},{2,4},{4,6},{6,0},{1,3},{3,5},{5,7},{7,1},{8,10},{10,12},{12... | collective-permute-start | bytes 1572872 | tf_op jit(solution)/shard_map/ppermute | solution.py:62
  426.9 78.2 %collective-permute-start.42 = (bf16[1,512,2048]{2,1,0:T(8,128)(2,1)}, bf16[1,512,2048]{2,1,0:T(8,128)(2,1)}, u32[]{:S(2)}, u32[]{:S(2)}) collective-permute-start(bf16[1,512,2048]{2,1,0:T(8,128)(2,1)} %add_convert_fusion.1), channel_id=1, source_target_pairs={{0,16},{8,24},{16,0},{24,8},{1,17},{9,25},{17,1},{25,9},{2,18},{10... | collective-permute-start | bytes 6291464 | tf_op jit(solution)/shard_map/ppermute | solution.py:65
  479.0 40.8 %collective-permute-start.41 = (bf16[512,256]{1,0:T(8,128)(2,1)S(1)}, bf16[512,256]{1,0:T(8,128)(2,1)}, u32[]{:S(2)}, u32[]{:S(2)}) collective-permute-start(bf16[512,256]{1,0:T(8,128)(2,1)S(1)} %get-tuple-element.487), channel_id=1, source_target_pairs={{0,2},{2,4},{4,6},{6,0},{1,3},{3,5},{5,7},{7,1},{8,10},{10,12},{12... | collective-permute-start | bytes 786440 | tf_op jit(solution)/shard_map/ppermute | solution.py:62
  544.1 117.0 %collective-permute-start.58 = (bf16[1,512,2048]{2,1,0:T(8,128)(2,1)}, bf16[1,512,2048]{2,1,0:T(8,128)(2,1)}, u32[]{:S(2)}, u32[]{:S(2)}) collective-permute-start(bf16[1,512,2048]{2,1,0:T(8,128)(2,1)} %add_convert_fusion), channel_id=1, source_target_pairs={{0,16},{8,24},{16,0},{24,8},{1,17},{9,25},{17,1},{25,9},{2,18},{10... | collective-permute-start | bytes 6291464 | tf_op jit(solution)/shard_map/ppermute | solution.py:65
  544.7 67.2 %collective-permute-start.49 = (bf16[1,128,2048]{2,1,0:T(8,128)(2,1)S(1)}, bf16[1,128,2048]{2,1,0:T(8,128)(2,1)S(1)}, u32[]{:S(2)}, u32[]{:S(2)}) collective-permute-start(bf16[1,128,2048]{2,1,0:T(8,128)(2,1)S(1)} %copy-done.38), channel_id=1, source_target_pairs={{0,2},{2,4},{4,6},{6,0},{1,3},{3,5},{5,7},{7,1},{8,10},{10,12},{12... | collective-permute-start | bytes 1572872 | tf_op jit(solution)/shard_map/ppermute | solution.py:62
  549.7 75.6 %collective-permute-start.44 = (bf16[512,2048]{1,0:T(8,128)(2,1)S(1)}, bf16[512,2048]{1,0:T(8,128)(2,1)S(1)}, u32[]{:S(2)}, u32[]{:S(2)}) collective-permute-start(bf16[512,2048]{1,0:T(8,128)(2,1)S(1)} %copy-done.13), channel_id=1, source_target_pairs={{0,1},{1,0},{2,3},{3,2},{4,5},{5,4},{6,7},{7,6},{8,9},{9,8},{10,11... | collective-permute-start | bytes 6291464 | tf_op jit(solution)/shard_map/ppermute | solution.py:146
  550.8 52.0 %collective-permute-start.45 = (bf16[512,256]{1,0:T(8,128)(2,1)S(1)}, bf16[512,256]{1,0:T(8,128)(2,1)S(1)}, u32[]{:S(2)}, u32[]{:S(2)}) collective-permute-start(bf16[512,256]{1,0:T(8,128)(2,1)S(1)} %fusion.14), channel_id=1, source_target_pairs={{0,1},{1,0},{2,3},{3,2},{4,5},{5,4},{6,7},{7,6},{8,9},{9,8},{10,11... | collective-permute-start | bytes 786440 | tf_op jit(solution)/shard_map/ppermute | solution.py:146
  555.0 52.4 %collective-permute-start.51 = (bf16[1,128,2048]{2,1,0:T(8,128)(2,1)S(1)}, bf16[1,128,2048]{2,1,0:T(8,128)(2,1)S(1)}, u32[]{:S(2)}, u32[]{:S(2)}) collective-permute-start(bf16[1,128,2048]{2,1,0:T(8,128)(2,1)S(1)} %copy-done.41), channel_id=1, source_target_pairs={{0,6},{2,0},{4,2},{6,4},{1,7},{3,1},{5,3},{7,5},{8,14},{10,8},{12,... | collective-permute-start | bytes 1572872 | tf_op jit(solution)/shard_map/ppermute | solution.py:62
  639.6 48.6 %collective-permute-start.61 = (bf16[1,128,2048]{2,1,0:T(8,128)(2,1)}, bf16[1,128,2048]{2,1,0:T(8,128)(2,1)S(1)}, u32[]{:S(2)}, u32[]{:S(2)}) collective-permute-start(bf16[1,128,2048]{2,1,0:T(8,128)(2,1)} %get-tuple-element.448), channel_id=1, source_target_pairs={{0,2},{2,4},{4,6},{6,0},{1,3},{3,5},{5,7},{7,1},{8,10},{10,12},{12... | collective-permute-start | bytes 1572872 | tf_op jit(solution)/shard_map/ppermute | solution.py:62
  671.2 43.3 %collective-permute-start.57 = (bf16[512,1024]{1,0:T(8,128)(2,1)S(1)}, bf16[512,1024]{1,0:T(8,128)(2,1)S(1)}, u32[]{:S(2)}, u32[]{:S(2)}) collective-permute-start(bf16[512,1024]{1,0:T(8,128)(2,1)S(1)} %copy-done.34), channel_id=1, source_target_pairs={{0,16},{8,24},{16,0},{24,8},{1,17},{9,25},{17,1},{25,9},{2,18},{10... | collective-permute-start | bytes 3145736 | tf_op jit(solution)/shard_map/ppermute | solution.py:65
  672.2 53.1 %collective-permute-start.64 = (bf16[512,256]{1,0:T(8,128)(2,1)S(1)}, bf16[512,256]{1,0:T(8,128)(2,1)S(1)}, u32[]{:S(2)}, u32[]{:S(2)}) collective-permute-start(bf16[512,256]{1,0:T(8,128)(2,1)S(1)} %add_convert_fusion.32), channel_id=1, source_target_pairs={{0,16},{8,24},{16,0},{24,8},{1,17},{9,25},{17,1},{25,9},{2,18},{10... | collective-permute-start | bytes 786440 | tf_op jit(solution)/shard_map/ppermute | solution.py:65
  686.4 66.1 %collective-permute-start.71 = (bf16[1,128,2048]{2,1,0:T(8,128)(2,1)S(1)}, bf16[1,128,2048]{2,1,0:T(8,128)(2,1)S(1)}, u32[]{:S(2)}, u32[]{:S(2)}) collective-permute-start(bf16[1,128,2048]{2,1,0:T(8,128)(2,1)S(1)} %get-tuple-element.444), channel_id=1, source_target_pairs={{0,2},{2,4},{4,6},{6,0},{1,3},{3,5},{5,7},{7,1},{8,10},{10,12},{12... | collective-permute-start | bytes 1572872 | tf_op jit(solution)/shard_map/ppermute | solution.py:62
  692.1 62.7 %collective-permute-start.69 = (bf16[128,1024]{1,0:T(8,128)(2,1)S(1)}, bf16[128,1024]{1,0:T(8,128)(2,1)S(1)}, u32[]{:S(2)}, u32[]{:S(2)}) collective-permute-start(bf16[128,1024]{1,0:T(8,128)(2,1)S(1)} %get-tuple-element.469), channel_id=1, source_target_pairs={{0,2},{2,4},{4,6},{6,0},{1,3},{3,5},{5,7},{7,1},{8,10},{10,12},{12... | collective-permute-start | bytes 786440 | tf_op jit(solution)/shard_map/ppermute | solution.py:62
  (127 other events, 1763.9 us)
Sparse Core Ops, SparseCore 0:
  19.0 164.8 all-gather.4
  186.1 126.5 all-gather.2

commit v3 on v2

--- a/solution.py
+++ b/solution.py
@@ -8,7 +8,7 @@
 from jax.sharding import PartitionSpec as P
 
 BLOCK = 256
-FF_SPLIT = (2048, 2048)
+FF_SPLIT = (2560, 1536)
 FF_TILE = 256
 EPS = 1e-05
 NEG = -1e30
@@ -17,6 +17,8 @@
 LOG2E = 1.4426950408889634
 F32 = jnp.float32
 SMALL = pl.CostEstimate(flops=1000, transcendentals=0, bytes_accessed=1000)
+MIDDLE = pl.CostEstimate(flops=46 * 10**8, transcendentals=0, bytes_accessed=14 * 10**6)
+COST = [SMALL]
 BF16 = jnp.bfloat16
 
 
@@ -49,7 +51,7 @@
 
 
 def join(axis):
-    return lambda *parts: jnp.concatenate(parts, axis=axis)
+    return lambda *parts: join_call(axis, *parts)
 
 
 class Ring:
@@ -92,22 +94,14 @@
                     out.append((xx * 2 + cc) * self.nz + zz)
         return jnp.stack(out).astype(jnp.int32)
 
-    def side_parts(self, mine, other, axis):
-        width = mine.shape[axis] // self.nx
-        return [
-            (cut(mine, k * width, width, axis) + cut(other, k * width, width, axis)).astype(BF16)
-            for k in range(1, self.nx)
-        ]
-
-    def block_parts(self, mine, other, crossed, axis):
-        size = mine.shape[axis] // self.nx // self.nz
-        out = []
-        for k in range(self.nz):
-            part = cut(mine, k * size, size, axis) + cut(other, k * size, size, axis)
-            for c in crossed:
-                part = part + cut(c, k * size, size, axis)
-            out.append(part.astype(BF16) if k else part)
-        return out
+    def places(self):
+        dp, z = lax.axis_index("dp"), lax.axis_index("ctx")
+        block = jnp.arange(self.ndp * self.nz, dtype=jnp.int32)
+        zz, cc, xx = block % self.nz, block // self.nz % 2, block // (2 * self.nz)
+        dz = (z - zz + self.nz) % self.nz
+        dx = (dp // 2 - xx + self.nx) % self.nx
+        dc = (dp % 2 + cc) % 2
+        return ((dc * self.nx + dx) * self.nz + dz).astype(jnp.int32)
 
     def small_sum(self, value):
         value = value + self.core(value)
@@ -130,10 +124,6 @@
         return added([base[:, :size]] + [self.z(base[:, k * size : (k + 1) * size], -k) for k in range(1, self.nz)])
 
 
-def cut(a, start, length, axis):
-    return lax.slice_in_dim(a, start, start + length, axis=axis).astype(F32)
-
-
 def added(parts):
     out = parts[0].astype(F32)
     for p in parts[1:]:
@@ -173,7 +163,7 @@
             scratch_shapes=[pltpu.VMEM((tile, w), d) for w, d in scratch],
         ),
         out_shape=[jax.ShapeDtypeStruct(shape, dtype) for _, shape, dtype in outs],
-        cost_estimate=SMALL,
+        cost_estimate=COST[0],
     )(order, *[a for _, a in ins])
 
 
@@ -354,23 +344,29 @@
     return act, (d_act * slope).astype(BF16)
 
 
-def ff_grads(act, d_pre, ntt, got, gm, gp):
+def ff_grads(act, d_pre, ntt, got, gm, pieces):
     half = gm.shape[1]
-    for g, rows in ((gm, slice(0, half)), (gp, slice(half, 2 * half))):
-        g[0] = dot_nn(ntt[rows, :], d_pre).astype(g.dtype)
-        g[1] = dot_nn(got[rows, :], act).astype(g.dtype)
-
-
-def ff_first_kernel(nt, ntt, go, got, up, down, gm, gp, br, dn):
+    each = pieces[0].shape[0]
+    for kind, (rows, units) in enumerate(((ntt, d_pre), (got, act))):
+        gm[kind] = dot_nn(rows[:half, :], units).astype(BF16)
+        for k in range(half // each):
+            start = half + k * each
+            out = pieces[kind * (half // each) + k]
+            out[...] = dot_nn(rows[start : start + each, :], units).astype(BF16)
+
+
+def ff_full_kernel(count, nt, ntt, go, got, up, down, *refs):
+    carry, (gm, *pieces, br, dn) = refs[:count], refs[count:]
+
     @pl.when(pl.program_id(0) == 0)
     def _():
-        br[...] = jnp.zeros_like(br)
-        dn[...] = jnp.zeros_like(dn)
+        br[...] = carry[0][...] if carry else jnp.zeros_like(br)
+        dn[...] = carry[1][...] if carry else jnp.zeros_like(dn)
 
     act, d_pre = ff_hidden(nt, go, up, down)
     dn[...] += dot_nt(d_pre, up[...])
     br[...] += dot_nt(act, down[...])
-    ff_grads(act, d_pre, ntt, got, gm, gp)
+    ff_grads(act, d_pre, ntt, got, gm, pieces)
 
 
 def ff_hidden_kernel(nt, go, up, down, dn_in, act_out, d_pre_out, dn, acc):
@@ -388,13 +384,15 @@
         dn[...] = acc[...].astype(dn.dtype)
 
 
-def ff_grad_kernel(act, d_pre, ntt, got, down, br_in, gm, gp, br, acc):
+def ff_grad_kernel(act, d_pre, ntt, got, down, br_in, gm, *refs):
+    *pieces, br, acc = refs
+
     @pl.when(pl.program_id(0) == 0)
     def _():
         acc[...] = br_in[...]
 
     acc[...] += dot_nt(act[...], down[...])
-    ff_grads(act[...], d_pre[...], ntt, got, gm, gp)
+    ff_grads(act[...], d_pre[...], ntt, got, gm, pieces)
 
     @pl.when(pl.program_id(0) == pl.num_programs(0) - 1)
     def _():
@@ -402,24 +400,26 @@
 
 
 class FeedForward:
-    def __init__(self, rows, width, n):
+    def __init__(self, rows, width, n, nx):
         self.rows, self.width, self.n = rows, width, n
         self.tile = min(FF_TILE, n)
         once = pl.Buffered(1)
         steps = n // self.tile
+        half = width // 2
         self.full = pl.BlockSpec((rows, width), lambda j: (0, 0), pipeline_mode=once)
         self.full_t = pl.BlockSpec((width, rows), lambda j: (0, 0), pipeline_mode=once)
         self.up = pl.BlockSpec((width, self.tile), lambda j: (0, j))
         self.down = pl.BlockSpec((width, self.tile), lambda j: (0, steps + j))
         self.act = pl.BlockSpec((rows, self.tile), lambda j: (0, j))
-        self.grad = pl.BlockSpec((2, width // 2, self.tile), lambda j: (0, 0, j))
+        self.grads = [pl.BlockSpec((2, half, self.tile), lambda j: (0, 0, j))]
+        self.grads += [pl.BlockSpec((half // nx, self.tile), lambda j: (0, j))] * (2 * nx)
         shape = jax.ShapeDtypeStruct
-        self.grad_shape = shape((2, width // 2, n), BF16)
+        self.grad_shapes = [shape((2, half, n), BF16)] + [shape((half // nx, n), BF16)] * (2 * nx)
         self.act_shape = shape((rows, n), BF16)
         self.high = shape((rows, width), F32)
         self.low = shape((rows, width), BF16)
 
-    def call(self, kernel, in_specs, out_specs, out_shape, args, scratch=1):
+    def call(self, kernel, in_specs, out_specs, out_shape, args, scratch):
         return pl.pallas_call(
             kernel,
             grid=(self.n // self.tile,),
@@ -428,16 +428,16 @@
             out_shape=out_shape,
             scratch_shapes=[pltpu.VMEM((self.rows, self.width), F32)] * scratch,
             compiler_params=pltpu.CompilerParams(vmem_limit_bytes=56 * 1024 * 1024),
-            cost_estimate=SMALL,
+            cost_estimate=COST[0],
         )(*args)
 
-    def first(self, nt, ntt, go, got, w):
+    def complete(self, nt, ntt, go, got, w, *carry):
         return self.call(
-            ff_first_kernel,
-            [self.full, self.full_t, self.full, self.full_t, self.up, self.down],
-            [self.grad, self.grad, self.full, self.full],
-            [self.grad_shape, self.grad_shape, self.high, self.high],
-            (nt, ntt, go, got, w, w),
+            functools.partial(ff_full_kernel, len(carry)),
+            [self.full, self.full_t, self.full, self.full_t, self.up, self.down] + [self.full] * len(carry),
+            [*self.grads, self.full, self.full],
+            [*self.grad_shapes, self.high, self.high],
+            (nt, ntt, go, got, w, w, *carry),
             0,
         )
 
@@ -448,16 +448,205 @@
             [self.act, self.act, self.full],
             [self.act_shape, self.act_shape, self.low],
             (nt, go, w, w, dn),
+            1,
         )
 
-    def grads(self, act, d_pre, ntt, got, w, br):
+    def grad(self, act, d_pre, ntt, got, w, br):
         return self.call(
             ff_grad_kernel,
             [self.act, self.act, self.full_t, self.full_t, self.down, self.full],
-            [self.grad, self.grad, self.full],
-            [self.grad_shape, self.grad_shape, self.low],
+            [*self.grads, self.full],
+            [*self.grad_shapes, self.low],
             (act, d_pre, ntt, got, w, br),
+            1,
         )
+
+
+def join_call(axis, *parts):
+    block = parts[0].shape
+    shape = tuple(d * len(parts) if i == axis else d for i, d in enumerate(block))
+
+    def kernel(*refs):
+        for k, ref in enumerate(refs[:-1]):
+
+            @pl.when(pl.program_id(0) == k)
+            def _():
+                refs[-1][...] = ref[...]
+
+    def place(k):
+        return tuple(k if i == axis else 0 for i in range(len(block)))
+
+    return pl.pallas_call(
+        kernel,
+        grid=(len(parts),),
+        in_specs=[pl.BlockSpec(block, lambda k: (0,) * len(block), pipeline_mode=pl.Buffered(1))] * len(parts),
+        out_specs=pl.BlockSpec(block, place),
+        out_shape=jax.ShapeDtypeStruct(shape, parts[0].dtype),
+        compiler_params=pltpu.CompilerParams(vmem_limit_bytes=24 * 1024 * 1024),
+        cost_estimate=COST[0],
+    )(*parts)
+
+
+def sum_kernel(*refs):
+    *ins, out = refs
+    out[...] = added([r[...] for r in ins]).astype(out.dtype)
+
+
+def side_kernel(mine, *refs):
+    *others, out = refs
+    for kind, other in enumerate(others):
+        out[kind] = (mine[kind].astype(F32) + other[...].astype(F32)).astype(BF16)
+
+
+def side_call(mine, others, k, count):
+    kinds, rows, n = mine.shape
+    size = rows // count
+    tile = min(size, 128)
+    steps = size // tile
+    return pl.pallas_call(
+        side_kernel,
+        grid=(steps,),
+        in_specs=[pl.BlockSpec((kinds, tile, n), lambda i: (0, k * steps + i, 0))]
+        + [pl.BlockSpec((tile, n), lambda i: (i, 0))] * kinds,
+        out_specs=pl.BlockSpec((kinds, tile, n), lambda i: (0, i, 0)),
+        out_shape=jax.ShapeDtypeStruct((kinds, size, n), BF16),
+        compiler_params=pltpu.CompilerParams(vmem_limit_bytes=24 * 1024 * 1024),
+        cost_estimate=COST[0],
+    )(mine, *others)
+
+
+def plus_call(*arrays):
+    kinds, rows, n = arrays[0].shape
+    tile = min(rows, 128)
+    spec = pl.BlockSpec((1, tile, n), lambda g, i: (g, i, 0))
+    return pl.pallas_call(
+        sum_kernel,
+        grid=(kinds, rows // tile),
+        in_specs=[spec] * len(arrays),
+        out_specs=spec,
+        out_shape=jax.ShapeDtypeStruct((kinds, rows, n), BF16),
+        cost_estimate=COST[0],
+    )(*arrays)
+
+
+def block_call(mine, others, crossed, count, size):
+    kinds, _, n = mine.shape
+    tile = min(size, 32)
+    steps = size // tile
+
+    def kernel(*refs):
+        ins, outs = refs[: len(refs) - count], refs[len(refs) - count :]
+        for k, out in enumerate(outs):
+            whole, *rest = ins[k::count]
+            for kind in range(kinds):
+                terms = [whole[kind], rest[kind][...]] + [c[kind] for c in rest[kinds:]]
+                out[kind] = added(terms).astype(out.dtype)
+
+    three = [pl.BlockSpec((kinds, tile, n), lambda i, k=k: (0, k * steps + i, 0)) for k in range(count)]
+    two = [pl.BlockSpec((tile, n), lambda i, k=k: (k * steps + i, 0)) for k in range(count)]
+    shape = jax.ShapeDtypeStruct
+    return pl.pallas_call(
+        kernel,
+        grid=(steps,),
+        in_specs=three + two * kinds + three * len(crossed),
+        out_specs=[pl.BlockSpec((kinds, tile, n), lambda i: (0, i, 0))] * count,
+        out_shape=[shape((kinds, size, n), BF16 if k else F32) for k in range(count)],
+        compiler_params=pltpu.CompilerParams(vmem_limit_bytes=24 * 1024 * 1024),
+        cost_estimate=COST[0],
+    )(*[a for a in (mine, *others, *crossed) for _ in range(count)])
+
+
+def project_kernel(a, mine, other, out):
+    half = mine.shape[0]
+    out[...] = (dot_nn(a[:, :half], mine[...]) + dot_nn(a[:, half:], other[...])).astype(BF16)
+
+
+def project(a, mine, other):
+    rows, width = a.shape
+    half, n = mine.shape
+    tile = min(n, 256)
+    w = pl.BlockSpec((half, tile), lambda j: (0, j))
+    return pl.pallas_call(
+        project_kernel,
+        grid=(n // tile,),
+        in_specs=[pl.BlockSpec((rows, width), lambda j: (0, 0)), w, w],
+        out_specs=pl.BlockSpec((rows, tile), lambda j: (0, j)),
+        out_shape=jax.ShapeDtypeStruct((rows, n), BF16),
+        compiler_params=pltpu.CompilerParams(vmem_limit_bytes=24 * 1024 * 1024),
+        cost_estimate=COST[0],
+    )(a, mine, other)
+
+
+def widened(a, mine, other):
+    rows, n = a.shape
+    half = mine.shape[0]
+    tile = min(half, 256)
+    steps = half // tile
+
+    def kernel(a, mine, other, out):
+        @pl.when(pl.program_id(0) < steps)
+        def _():
+            out[...] = dot_nt(a[...], mine[...]).astype(BF16)
+
+        @pl.when(pl.program_id(0) >= steps)
+        def _():
+            out[...] = dot_nt(a[...], other[...]).astype(BF16)
+
+    return pl.pallas_call(
+        kernel,
+        grid=(2 * steps,),
+        in_specs=[
+            pl.BlockSpec((rows, n), lambda j: (0, 0)),
+            pl.BlockSpec((tile, n), lambda j: (jnp.minimum(j, steps - 1), 0)),
+            pl.BlockSpec((tile, n), lambda j: (jnp.maximum(j - steps, 0), 0)),
+        ],
+        out_specs=pl.BlockSpec((rows, tile), lambda j: (0, j)),
+        out_shape=jax.ShapeDtypeStruct((rows, 2 * half), BF16),
+        compiler_params=pltpu.CompilerParams(vmem_limit_bytes=24 * 1024 * 1024),
+        cost_estimate=COST[0],
+    )(a, mine, other)
+
+
+def outer(pairs, count):
+    rows, width = pairs[0][0].shape
+    n = pairs[0][1].shape[1]
+    half, kinds = width // 2, len(pairs)
+    shape = jax.ShapeDtypeStruct
+
+    def part(start, size, joined):
+        tile = min(size, 256)
+
+        def kernel(*refs):
+            for kind in range(kinds):
+                value = dot_tn(refs[2 * kind][...], refs[2 * kind + 1][...]).astype(BF16)
+                if joined:
+                    refs[-1][kind] = value
+                else:
+                    refs[2 * kinds + kind][...] = value
+
+        if joined:
+            specs = [pl.BlockSpec((kinds, tile, n), lambda i: (0, i, 0))]
+            shapes = [shape((kinds, size, n), BF16)]
+        else:
+            specs = [pl.BlockSpec((tile, n), lambda i: (i, 0))] * kinds
+            shapes = [shape((size, n), BF16)] * kinds
+        return pl.pallas_call(
+            kernel,
+            grid=(size // tile,),
+            in_specs=[
+                pl.BlockSpec((rows, tile), lambda i: (0, start // tile + i)),
+                pl.BlockSpec((rows, n), lambda i: (0, 0)),
+            ]
+            * kinds,
+            out_specs=specs,
+            out_shape=shapes,
+            compiler_params=pltpu.CompilerParams(vmem_limit_bytes=24 * 1024 * 1024),
+            cost_estimate=COST[0],
+        )(*[a for pair in pairs for a in pair])
+
+    each = half // count
+    parts = [part(half + k * each, each, False) for k in range(count)]
+    return [*part(0, half, True)] + [parts[k][kind] for kind in range(kinds) for k in range(count)]
 
 
 def diagonal_mask(rows):
@@ -532,7 +721,7 @@
             shape((heads, 1, rows), F32),
         ],
         compiler_params=pltpu.CompilerParams(vmem_limit_bytes=32 * 1024 * 1024),
-        cost_estimate=SMALL,
+        cost_estimate=COST[0],
     )(z, queries, kv)
 
 
@@ -600,7 +789,7 @@
         ),
         out_shape=[shape((rows, cols), BF16), shape(kv.shape, F32)],
         compiler_params=pltpu.CompilerParams(vmem_limit_bytes=32 * 1024 * 1024),
-        cost_estimate=SMALL,
+        cost_estimate=COST[0],
     )(z, queries, kv, d_heads, out, lse)
 
 
@@ -608,6 +797,7 @@
     tokens, gain_one, bias_one, w_query, w_keyval, w_out, gain_two, bias_two, w_up, w_down, grad_out
 ):
     ring, todo = Ring(), Order()
+    COST[0] = MIDDLE
     run = todo.run
     nz = ring.nz
     rows, width = tokens.shape
@@ -620,6 +810,7 @@
     order = ring.order()
     entries = rows * ring.ndp * nz * width
     split = FF_SPLIT if sum(FF_SPLIT) == ff_cols else (ff_cols // 2, ff_cols - ff_cols // 2)
+    starts = [sum(split[:k]) for k in range(len(split))]
 
     small = jnp.stack([gain_one, bias_one, gain_two, bias_two])
     small = jnp.pad(small, ((0, 12), (0, w_keyval.shape[1] - own_d)))
@@ -629,130 +820,106 @@
         across = [ring.x_all(p) for p in parts]
         return parts + [s[k] for k in range(ring.nx - 1) for s in across]
 
-    kv_blocks = sides([kv_shard, *ring.z_all(kv_shard)])
+    kv_blocks = sides([kv_shard, *[ring.z(kv_shard, k) for k in range(1, nz)]])
     q_parts = [w_query, *ring.z_all(w_query)]
+    q_blocks = sides(q_parts)
     got = run(turned, grad_out, order)
     kv_mine = run(join(0), *kv_blocks, wait=(q_parts[1], q_parts[-1]))
     kv_other = ring.core(kv_mine)
-    q_blocks = sides(q_parts)
-
-    cols_a, cols_b = slice(0, split[0]), slice(split[0], ff_cols)
-    both = ("dp", "ctx")
-
-    def ff_shard(cols, *others):
-        return after(jnp.concatenate([w_up[:, cols], w_down[:, cols]], axis=1), *others)
-
-    ff_a = lax.all_gather(ff_shard(cols_a, q_parts[1]), both, axis=0, tiled=True)
-    ff_b = lax.all_gather(ff_shard(cols_b, q_parts[1]), both, axis=0, tiled=True)
 
     def split_rows(*kv_rows):
         parts = [r.reshape(-1, own_d + 16, r.shape[1]) for r in kv_rows]
         weights = [p[:, :own_d].reshape(half, -1) for p in parts]
         small = jnp.concatenate([p[:, own_d : own_d + 4, :own_d] for p in parts], axis=0)
         small = small.transpose(1, 0, 2).reshape(4, width)
-        return weights, gathered(small, jnp.argsort(order)).astype(F32)
+        return weights, gathered(small, ring.places()).astype(F32)
 
     w_kv, gains = run(split_rows, kv_mine, kv_other)
     normed, mean1, rate1 = run(first_norm, tokens, gains[0:2], order)
-
-    def project(normed, mine, other):
-        return (dot_nn(normed[:, :half], mine) + dot_nn(normed[:, half:], other)).astype(BF16)
-
+    q_mine = run(join(0), *q_blocks)
+    q_other = ring.core(q_mine)
     keyval = run(project, normed, *w_kv)
     tiles = [keyval, *ring.z_all(keyval)]
-    q_mine = run(join(0), *q_blocks)
-    q_other = ring.core(q_mine)
-    o_parts = [w_out, *ring.z_all(after(w_out, q_mine))]
+    both = ("dp", "ctx")
+
+    def ff_gather(k):
+        cols = slice(starts[k], starts[k] + split[k])
+        shard = after(jnp.concatenate([w_up[:, cols], w_down[:, cols]], axis=1), tiles[1])
+        return lax.all_gather(shard, both, axis=0, tiled=True)
+
+    ff_w = [ff_gather(k) for k in range(len(split))]
+
+    o_parts = [w_out, *ring.z_all(after(w_out, tiles[1]))]
     o_blocks = sides(o_parts)
     queries = run(project, normed, q_mine, q_other)
     keyval_all = run(lambda *t: jnp.stack(t), *tiles, wait=(o_parts[1], o_parts[-1]))
     attn_t, attn_low, lse = run(lambda q, kv: attn_call(scale, z, q, kv), queries, keyval_all)
     o_mine = run(join(0), *o_blocks)
     o_other = ring.core(o_mine)
-
-    def widened(a, mine, other):
-        return jnp.concatenate([dot_nt(a, mine), dot_nt(a, other)], axis=1).astype(BF16)
-
     part = run(widened, attn_low, o_mine, o_other)
     parts = [part, *tp_others(part)]
     nt, ntt, hidden, mean2, rate2, attn_square = run(
         lambda *a: second_norm(a[0], a[2:], a[1], order), tokens, gains[2:4], *parts
     )
 
-    def scatter_core(pieces):
-        return [(m, ring.core(o)) for m, o in pieces]
-
-    def scatter_x(pair, axis):
-        mine, other = pair
-        across = run(lambda m, o: ring.side_parts(m, o, axis), mine, other)
-        return mine, other, [ring.x(p, -k - 1) for k, p in enumerate(across)]
+    COST[0] = SMALL
 
     far = nz // 2
 
-    def scatter_z(triple, axis):
-        blocks = run(lambda m, o, c: ring.block_parts(m, o, c, axis), *triple)
+    def scatter_core(mine, *pieces, later=()):
+        got = [None] * len(pieces)
+        for k in list(range(len(pieces))):
+            if k % ring.nx:
+                got[k] = ring.core(pieces[k])
+        for k in range(0, len(pieces), ring.nx):
+            got[k] = ring.core(after(pieces[k], *later))
+        return mine, got
+
+    def scatter_x(pair):
+        mine, got = pair
+        across = [
+            run(lambda m, o, k=k: side_call(m, o, k, ring.nx), mine, got[k :: ring.nx])
+            for k in range(1, ring.nx)
+        ]
+        return mine, got[:: ring.nx], [ring.x(p, -k - 1) for k, p in enumerate(across)]
+
+    def scatter_z(triple):
+        mine, got, crossed = triple
+        size = mine.shape[1] // ring.nx // nz
+        blocks = run(lambda *a: block_call(*a, nz, size), mine, got, crossed)
         downs = ring.z(blocks[far], -1) if far else None
         ups = ring.z(blocks[far + 1], 1) if far + 1 < nz else None
         return blocks, downs, ups
 
-    def plus(a, b):
-        return (a.astype(F32) + b.astype(F32)).astype(BF16)
-
     def scatter_mid(state):
         blocks, downs, ups = state
         for k in range(far - 1, 0, -1):
-            downs = ring.z(run(plus, blocks[k], downs), -1)
+            downs = ring.z(run(plus_call, blocks[k], downs), -1)
         for k in range(far + 2, nz):
-            ups = ring.z(run(plus, blocks[k], ups), 1)
+            ups = ring.z(run(plus_call, blocks[k], ups), 1)
         return [blocks[0]] + [m for m in (downs, ups) if m is not None]
 
     def scatter_end(parts):
         return run(lambda *p: added(p), *parts)
 
-    def halves(gm, gp):
-        return [(gm[k : k + 1], gp[k : k + 1]) for k in (1, 0)]
-
-    ff1 = FeedForward(rows, width, split[0])
-    ff2 = FeedForward(rows, width, split[1])
-    gm, gp, br, dn = run(ff1.first, nt, ntt, grad_out, got, ff_a)
-    a_c = scatter_core(halves(gm, gp))
-    a0 = scatter_x(a_c[0], 1)
-    a1 = scatter_x(a_c[1], 1)
-    act, d_pre, dn = run(ff2.hidden, nt, grad_out, ff_b, dn)
+    ff = [FeedForward(rows, width, n, ring.nx) for n in split]
+    *g_a, br, dn = run(ff[0].complete, nt, ntt, grad_out, got, ff_w[0])
+    g_a = scatter_x(scatter_core(*g_a))
+    act, d_pre, dn = run(ff[1].hidden, nt, grad_out, ff_w[1], dn, wait=g_a[1])
     dn_parts = [dn, *tp_others(dn)]
-    gm, gp, br = run(ff2.grads, act, d_pre, ntt, got, ff_b, br)
-    b_c = scatter_core(halves(gm, gp))
-    a0 = scatter_z(a0, 1)
-    b0 = scatter_x(b_c[0], 1)
-    b1 = scatter_x(b_c[1], 1)
-    a0 = scatter_mid(a0)
+    *g_b, br = run(ff[1].grad, act, d_pre, ntt, got, ff_w[1], br)
+    g_b = scatter_x(scatter_core(*g_b, later=(dn_parts[-1],)))
     d_branch, grad_hidden, d_two = run(
         lambda *a: second_back(*a[:5], a[5:], order),
         hidden, grad_out, mean2, rate2, gains[2:3], *dn_parts,
     )
-    br_parts = [br, *tp_others(after(br, dn_parts[-1]))]
+    br_parts = [br, *tp_others(after(br, d_branch))]
     d_heads = run(project, d_branch, o_mine, o_other)
-    a1 = scatter_z(a1, 1)
+    g_a = scatter_z(g_a)
     dq, dkv = run(
         lambda *a: attn_back_call(scale, z, *a), queries, keyval_all, d_heads, attn_t, lse,
-        wait=a0,
-    )
-    sends = run(lambda d: [d[k].astype(BF16) for k in range(1, nz)], dkv)
-    got_kv = [ring.z(s, -k - 1) for k, s in enumerate(sends)]
-    dq_part = run(widened, dq, q_mine, q_other)
-    dq_parts = [dq_part, *tp_others(after(dq_part, br_parts[-1]))]
-    a1 = scatter_mid(a1)
-
-    def outer(a, b):
-        full = dot_tn(a, b).astype(BF16)
-        return full[:half], full[half:]
-
-    b0 = scatter_z(b0, 1)
-    g_out = run(outer, d_branch, attn_low)
-    g_q = run(outer, normed, dq)
-    o_c, q_c = scatter_core([g_out, g_q])
-    mine_kv = run(lambda d, *g: added([d[0], *g]).astype(BF16), dkv, *got_kv)
-    kv_parts = [mine_kv, *tp_others(mine_kv)]
+        wait=g_b[1],
+    )
 
     def finish(hidden, *parts):
         branch = added(parts)
@@ -760,36 +927,41 @@
         return result.astype(BF16), jnp.sum(result * result), jnp.sum(branch * branch)
 
     layer_out, square_r, square_m = run(finish, hidden, *br_parts)
-    squares = jnp.stack([square_r, jnp.sum(attn_square), square_m])
-    rms_values = jnp.sqrt(ring.small_sum(jnp.broadcast_to(squares[:, None], (3, 128)))[:, 0] / entries)
-    o_s = scatter_x(o_c, 0)
-    q_s = scatter_x(q_c, 0)
+    dq_part = run(widened, dq, q_mine, q_other)
+    dq_parts = [dq_part, *tp_others(dq_part)]
+    sends = run(lambda d: [d[k].astype(BF16) for k in range(1, nz)], dkv)
+    got_kv = [ring.z(s, -k - 1) for k, s in enumerate(sends)]
+    oq_s = scatter_core(*run(lambda *a: outer((a[:2], a[2:]), ring.nx), d_branch, attn_low, normed, dq))
+    g_a = scatter_mid(g_a)
+    mine_kv = run(lambda d, *g: added([d[0], *g]).astype(BF16), dkv, *got_kv)
+    kv_parts = [mine_kv, *tp_others(mine_kv)]
+    oq_s = scatter_x(oq_s)
+    g_b = scatter_z(g_b)
     dkv_low = run(lambda *p: added(p).astype(BF16), *kv_parts)
-    g_kv = run(outer, normed, dkv_low)
-    kv_c = scatter_core([g_kv])[0]
+    kv_s = scatter_core(*run(lambda *a: outer((a,), ring.nx), normed, dkv_low))
     dkv_part = run(widened, dkv_low, *w_kv)
-    b0 = scatter_mid(b0)
-    kv_s = scatter_x(kv_c, 0)
-    a1_end = scatter_end(a1)
-    a0_end = scatter_end(a0)
+    kv_s = scatter_x(kv_s)
     input_grad, d_one = run(
         lambda *a: first_back(*a[:5], a[5:], order),
         tokens, grad_hidden, mean1, rate1, gains[0:1], *dq_parts, dkv_part,
     )
-    small = ring.small_scatter(gathered(jnp.concatenate([d_one, d_two], axis=0), order))
-    b1 = scatter_z(b1, 1)
-    o_s = scatter_z(o_s, 0)
-    b0_end = scatter_end(b0)
-    b1 = scatter_mid(b1)
-    q_s = scatter_z(q_s, 0)
-    o_s = scatter_mid(o_s)
-    kv_s = scatter_z(kv_s, 0)
-    q_s = scatter_mid(q_s)
+    end_a = scatter_end(g_a)
+    g_b = scatter_mid(g_b)
+    oq_s = scatter_z(oq_s)
+    kv_s = scatter_z(kv_s)
+    end_b = scatter_end(g_b)
+    oq_s = scatter_mid(oq_s)
     kv_s = scatter_mid(kv_s)
-    b1_end = scatter_end(b1)
-    grad_out_proj, grad_query, grad_keyval = (scatter_end(e) for e in (o_s, q_s, kv_s))
-    grad_down = jnp.concatenate([a0_end[0], b0_end[0]], axis=1)
-    grad_up = jnp.concatenate([a1_end[0], b1_end[0]], axis=1)
+    squares = jnp.stack([square_r, jnp.sum(attn_square), square_m])
+    squares = after(jnp.broadcast_to(squares[:, None], (3, 128)), oq_s[-1])
+    rms_values = jnp.sqrt(ring.small_sum(squares)[:, 0] / entries)
+    small = gathered(jnp.concatenate([d_one, d_two], axis=0), order)
+    small = ring.small_scatter(after(small, oq_s[-1]))
+    grad_out_proj, grad_query = scatter_end(oq_s)
+    grad_keyval = scatter_end(kv_s)[0]
+    grad_up, grad_down = (
+        jnp.concatenate([e[k] for e in (end_a, end_b)], axis=1) for k in range(2)
+    )
     return (
         layer_out, input_grad, small[0], small[1], grad_query, grad_keyval, grad_out_proj,
         small[2], small[3], grad_up, grad_down, rms_values,

time: 780 us -> 706 us (0.905)
  waiting for transfers between devices: 382 us -> 288 us
  Pallas kernels: 136 us -> 203 us
  other arithmetic: 67.6 us -> 28.3 us
  matrix products: 21 us -> 0 us
  local copies, waits for them, and re-layouts: 38.9 us -> 55.9 us
    pallas_call x0 -> x27, Pallas kernels: none -> 66.2 us  [the longest x4 13.7 us: block_call(): pl.pallas_call(kernel, grid=(steps,), in_specs=three + two * kinds + thre...]
    ppermute x5, waiting for transfers between devices: 131 us -> 79.5 us  [tp_others(): lax.ppermute(part, 'tp', [(i, (i + k) % n) for i in range(n)])]
    convert_element_type x22 -> x1, other arithmetic: 38.3 us -> 0.02 us  [split_rows(): return (weights, gathered(small, ring.places()).astype(F32))]
    unnamed x161 -> x186, local copies, waits for them, and re-layouts: 13.9 us -> 50.6 us
    ppermute x39 -> x30, waiting for transfers between devices: 158 us -> 126 us  [z(): lax.ppermute(value, 'ctx', [(i, (i + k) % self.nz) for i in range(self.nz)])]
    ppermute x20 -> x17, waiting for transfers between devices: 31.8 us -> 5.24 us  [x(): lax.ppermute(value, 'dp', [(i, (i + 2 * k) % self.ndp) for i in range(sel...]
    dot_general x15 -> x0, matrix products: 21 us -> none  [the longest x6 9.42 us: dot_nn(): lax.dot_general(a, b, (((1,), (0,)), ((), ())), preferred_element_type=F32)]
    slice x9 -> x8, local copies, waits for them, and re-layouts: 20.7 us -> 0.01 us  [the longest x4 0.01 us: ff_gather(): w_up[:, cols]]
  transfers between devices with their start and end apart: 81 -> 76, of which waited for: 33 -> 30; matrix products, arithmetic and copies ran while one was open for 14% -> 5% of each run, Pallas kernels for 12% -> 29%
where the time goes in v3:
time: 706 us; the launch traced here: 697 us
  waiting for transfers between devices  288 us (41%)
  Pallas kernels  203 us (29%)
  starting transfers between devices  106 us (15%)
  local copies, waits for them, and re-layouts  55.9 us (8%)
  other arithmetic  28.3 us (4%)
  between operations  15.7 us (2%)
    ppermute x30, waiting for transfers between devices, z(): lax.ppermute(value, 'ctx', [(i, (i + k) % self.nz) for i in range(self.nz)])  126 us
    pallas_call x3, Pallas kernels, call(): pl.pallas_call(kernel, grid=(self.n // self.tile,), in_specs=in_specs, ou...  83.3 us
    ppermute x5, waiting for transfers between devices, tp_others(): lax.ppermute(part, 'tp', [(i, (i + k) % n) for i in range(n)])  79.5 us
    ppermute x30, starting transfers between devices, z(): lax.ppermute(value, 'ctx', [(i, (i + k) % self.nz) for i in range(self.nz)])  72.8 us
    all_gather x2, waiting for transfers between devices, ff_gather(): return lax.all_gather(shard, both, axis=0, tiled=True)  50.7 us
    unnamed x186, local copies, waits for them, and re-layouts  50.6 us
    pallas_call x5, Pallas kernels, row_call(): pl.pallas_call(kernel, grid_spec=pltpu.PrefetchScalarGridSpec(num_scalar_...  38.2 us
    ppermute x19, waiting for transfers between devices, core(): return lax.ppermute(value, 'dp', [(i, i ^ 1) for i in range(self.ndp)])  21 us
  transfers between devices with their start and end apart: 76, of which 30 were waited for; matrix products, arithmetic and copies ran while one was open for 5% of the time, Pallas kernels for 29%

profile of v3, /device:TPU:0, one launch (start us, length us, event | category | flops | bytes accessed | tf_op | source)
XLA Modules:
  0.0 697.0 jit_solution(1015315267782634127)
XLA Ops:
  83.9 7.7 %collective-permute-done.19.refs_1_ = bf16[128,1024]{1,0:T(8,128)(2,1)S(1)} collective-permute-done((bf16[128,1024]{1,0:T(8,128)(2,1)S(1)}, bf16[128,1024]{1,0:T(8,128)(2,1)S(1)}, u32[]{:S(2)}, u32[]{:S(2)}) %collective-permute-start.19) | collective-permute-done | bytes 262176 | tf_op jit(solution)/shard_map/ppermute | solution.py:64
  105.8 19.0 %collective-permute-done.21.refs_2_ = bf16[128,1024]{1,0:T(8,128)(2,1)S(1)} collective-permute-done((bf16[128,1024]{1,0:T(8,128)(2,1)S(1)}, bf16[128,1024]{1,0:T(8,128)(2,1)S(1)}, u32[]{:S(2)}, u32[]{:S(2)}) %collective-permute-start.21) | collective-permute-done | bytes 262176 | tf_op jit(solution)/shard_map/ppermute | solution.py:64
  126.8 6.9 shard_map.208
  145.6 46.1 %collective-permute-done.27.refs_1_ = bf16[512,2048]{1,0:T(8,128)(2,1)S(1)} collective-permute-done((bf16[512,2048]{1,0:T(8,128)(2,1)S(1)}, bf16[512,2048]{1,0:T(8,128)(2,1)S(1)}, u32[]{:S(2)}, u32[]{:S(2)}) %collective-permute-start.27) | collective-permute-done | bytes 2097184 | tf_op jit(solution)/shard_map/ppermute | solution.py:136
  193.0 9.2 %shard_map.211 = (bf16[512,2048]{1,0:T(8,128)(2,1)}, bf16[2048,512]{1,0:T(8,128)(2,1)}, f32[512,2048]{1,0:T(8,128)}, f32[512,1]{1,0:T(8,128)}, f32[512,1]{1,0:T(8,128)}, /*index=5*/f32[512,1]{1,0:T(8,128)}) custom-call(s32[16]{0:T(128)} %stack.143.order_ref, bf16[512,2048]{1,0:T(8,128)(2,1)} %tok_ref.2, bf16[512,2048]{1,0:T(8,128)(2,1)} %copy-done.52, ...), custom_call_target="tpu_custom_call" | custom-call | flops 4600000000 | bytes 14000000 | tf_op jit(solution)/shard_map/pallas_call | solution.py:156
  202.2 14.9 %all-gather.5.cloned.1.call-done.up.down = bf16[2048,5120]{1,0:T(8,128)(2,1)} async-done(((bf16[128,5120]{1,0:T(8,128)(2,1)}), bf16[2048,5120]{1,0:T(8,128)(2,1)}) %all-gather.5.cloned.1.call-update) | async-done | bytes 20971536 | tf_op jit(solution)/shard_map/all_gather | solution.py:848
  217.1 46.2 %shard_map.212 = (bf16[2,1024,2560]{2,1,0:T(8,128)(2,1)}, bf16[512,2560]{1,0:T(8,128)(2,1)}, bf16[512,2560]{1,0:T(8,128)(2,1)}, bf16[512,2560]{1,0:T(8,128)(2,1)...) custom-call(bf16[512,2048]{1,0:T(8,128)(2,1)} %get-tuple-element.304.nt, ...), custom_call_target="tpu_custom_call" | custom-call | flops 1000 | bytes 1000 | tf_op jit(solution)/shard_map/pallas_call | solution.py:423
  268.5 7.8 %collective-permute-done.29.refs_1_ = bf16[512,2560]{1,0:T(8,128)(2,1)S(1)} collective-permute-done((bf16[512,2560]{1,0:T(8,128)(2,1)}, bf16[512,2560]{1,0:T(8,128)(2,1)S(1)}, u32[]{:S(2)}, u32[]{:S(2)}) %collective-permute-start.29) | collective-permute-done | bytes 2621472 | tf_op jit(solution)/shard_map/ppermute | solution.py:70
  288.1 35.8 %all-gather.3.cloned.1.call-done.up.down = bf16[2048,3072]{1,0:T(8,128)(2,1)} async-done(((bf16[128,3072]{1,0:T(8,128)(2,1)}), bf16[2048,3072]{1,0:T(8,128)(2,1)}) %all-gather.3.cloned.1.call-update) | async-done | bytes 12582928 | tf_op jit(solution)/shard_map/all_gather | solution.py:848
  323.9 18.6 %shard_map.214 = (bf16[512,1536]{1,0:T(8,128)(2,1)}, bf16[512,1536]{1,0:T(8,128)(2,1)}, bf16[512,2048]{1,0:T(8,128)(2,1)}) custom-call(bf16[512,2048]{1,0:T(8,128)(2,1)} %get-tuple-element.304.nt, bf16[512,2048]{1,0:T(8,128)(2,1)} %go_ref, bf16[2048,3072]{1,0:T(8,128)(2,1)} %all-gather.3.cloned.1.call-done.up.down, ...), custom_call_target="tpu_custom_call" | custom-call | flops 1000 | bytes 1000 | tf_op jit(solution)/shard_map/pallas_call | solution.py:423
  343.5 18.6 %shard_map.215 = (bf16[2,1024,1536]{2,1,0:T(8,128)(2,1)}, bf16[512,1536]{1,0:T(8,128)(2,1)}, bf16[512,1536]{1,0:T(8,128)(2,1)}, bf16[512,1536]{1,0:T(8,128)(2,1)...) custom-call(bf16[512,1536]{1,0:T(8,128)(2,1)} %get-tuple-element.311.act, ...), custom_call_target="tpu_custom_call" | custom-call | flops 1000 | bytes 1000 | tf_op jit(solution)/shard_map/pallas_call | solution.py:423
  373.8 16.7 %collective-permute-done.32.refs_1_ = bf16[512,2048]{1,0:T(8,128)(2,1)S(1)} collective-permute-done((bf16[512,2048]{1,0:T(8,128)(2,1)}, bf16[512,2048]{1,0:T(8,128)(2,1)S(1)}, u32[]{:S(2)}, u32[]{:S(2)}) %collective-permute-start.32) | collective-permute-done | bytes 2097184 | tf_op jit(solution)/shard_map/ppermute | solution.py:136
  391.8 9.2 %shard_map.217 = (bf16[512,2048]{1,0:T(8,128)(2,1)}, f32[512,2048]{1,0:T(8,128)}, f32[2,2048]{1,0:T(2,128)}) custom-call(s32[16]{0:T(128)} %stack.143.order_ref, f32[512,2048]{1,0:T(8,128)} %get-tuple-element.355.hid_ref, bf16[512,2048]{1,0:T(8,128)(2,1)} %go_ref, f32[512,1]{1,0:T(8,128)} %get-tuple-element.329.mean_ref, ...), custom_call_target="tpu_custom_call" | custom-call | flops 1000 | bytes 1000 | tf_op jit(solution)/shard_map/pallas_call | solution.py:156
  423.4 8.4 %shard_map.220 = (bf16[512,1024]{1,0:T(8,128)(2,1)S(1)}, f32[4,512,256]{2,1,0:T(8,128)S(1)}) custom-call(s32[1]{0:T(128)} %bitcast.27.z_ref, bf16[512,1024]{1,0:T(8,128)(2,1)S(1)} %copy-done.46, bf16[4,512,256]{2,1,0:T(8,128)(2,1)S(1)} %copy-done.21, bf16[512,1024]{1,0:T(8,128)(2,1)S(1)} %shard_map.218.d_ref, f32[8,128,512]{2,1,0:T(8,128)S(1)} %copy-done.35, ...), custom_call_target="tpu_custom_call" | custom-call | flops 1000 | bytes 1000 | tf_op jit(solution)/shard_map/pallas_call | solution.py:775
  431.9 16.6 %collective-permute-done.35 = bf16[512,2048]{1,0:T(8,128)(2,1)} collective-permute-done((bf16[512,2048]{1,0:T(8,128)(2,1)}, bf16[512,2048]{1,0:T(8,128)(2,1)}, u32[]{:S(2)}, u32[]{:S(2)}) %collective-permute-start.35) | collective-permute-done | bytes 2097184 | tf_op jit(solution)/shard_map/ppermute | solution.py:136
  470.3 18.2 %collective-permute-done.40 = bf16[512,256]{1,0:T(8,128)(2,1)S(1)} collective-permute-done((bf16[512,256]{1,0:T(8,128)(2,1)S(1)}, bf16[512,256]{1,0:T(8,128)(2,1)S(1)}, u32[]{:S(2)}, u32[]{:S(2)}) %collective-permute-start.40) | collective-permute-done | bytes 262176 | tf_op jit(solution)/shard_map/ppermute | solution.py:64
  488.5 9.7 %collective-permute-done.41 = bf16[512,256]{1,0:T(8,128)(2,1)S(1)} collective-permute-done((bf16[512,256]{1,0:T(8,128)(2,1)S(1)}, bf16[512,256]{1,0:T(8,128)(2,1)S(1)}, u32[]{:S(2)}, u32[]{:S(2)}) %collective-permute-start.41) | collective-permute-done | bytes 262176 | tf_op jit(solution)/shard_map/ppermute | solution.py:64
  549.7 9.5 %shard_map.231 = (f32[512,2048]{1,0:T(8,128)}, f32[2,2048]{1,0:T(2,128)}) custom-call(s32[16]{0:T(128)} %stack.143.order_ref, bf16[512,2048]{1,0:T(8,128)(2,1)} %tok_ref.2, f32[512,2048]{1,0:T(8,128)} %get-tuple-element.398.gh_ref, f32[512,1]{1,0:T(8,128)} %get-tuple-element.399.mean_ref, f32[512,1]{1,0:T(8,128)} %get-tuple-element.400.rate_ref, ...), custom_call_target="tpu_custom_call" | custom-call | flops 1000 | bytes 1000 | tf_op jit(solution)/shard_map/pallas_call | solution.py:156
  560.6 20.8 %collective-permute-start.52 = (bf16[2,128,1536]{2,1,0:T(8,128)(2,1)}, bf16[2,128,1536]{2,1,0:T(8,128)(2,1)S(1)}, u32[]{:S(2)}, u32[]{:S(2)}) collective-permute-start(bf16[2,128,1536]{2,1,0:T(8,128)(2,1)} %copy-done.57), channel_id=1, source_target_pairs={{0,6},{2,0},{4,2},{6,4},{1,7},{3,1},{5,3},{7,5},{8,14},{10,8},{12,... | collective-permute-start | bytes 2359304 | tf_op jit(solution)/shard_map/ppermute | solution.py:64
  585.9 8.0 %collective-permute-done.52.refs_1_ = bf16[2,128,1536]{2,1,0:T(8,128)(2,1)S(1)} collective-permute-done((bf16[2,128,1536]{2,1,0:T(8,128)(2,1)}, bf16[2,128,1536]{2,1,0:T(8,128)(2,1)S(1)}, u32[]{:S(2)}, u32[]{:S(2)}) %collective-permute-start.52) | collective-permute-done | bytes 786464 | tf_op jit(solution)/shard_map/ppermute | solution.py:64
  598.7 7.5 %collective-permute-start.62 = (bf16[2,128,1536]{2,1,0:T(8,128)(2,1)}, bf16[2,128,1536]{2,1,0:T(8,128)(2,1)S(1)}, u32[]{:S(2)}, u32[]{:S(2)}) collective-permute-start(bf16[2,128,1536]{2,1,0:T(8,128)(2,1)} %shard_map.233), channel_id=1, source_target_pairs={{0,6},{2,0},{4,2},{6,4},{1,7},{3,1},{5,3},{7,5},{8,14},{10,8},{12,... | collective-permute-start | bytes 2359304 | tf_op jit(solution)/shard_map/ppermute | solution.py:64
  618.8 16.6 %collective-permute-done.62 = bf16[2,128,1536]{2,1,0:T(8,128)(2,1)S(1)} collective-permute-done((bf16[2,128,1536]{2,1,0:T(8,128)(2,1)}, bf16[2,128,1536]{2,1,0:T(8,128)(2,1)S(1)}, u32[]{:S(2)}, u32[]{:S(2)}) %collective-permute-start.62) | collective-permute-done | bytes 786464 | tf_op jit(solution)/shard_map/ppermute | solution.py:64
  635.4 9.5 %collective-permute-done.55 = bf16[2,128,1024]{2,1,0:T(8,128)(2,1)S(1)} collective-permute-done((bf16[2,128,1024]{2,1,0:T(8,128)(2,1)S(1)}, bf16[2,128,1024]{2,1,0:T(8,128)(2,1)S(1)}, u32[]{:S(2)}, u32[]{:S(2)}) %collective-permute-start.55) | collective-permute-done | bytes 524320 | tf_op jit(solution)/shard_map/ppermute | solution.py:64
  655.9 9.3 %collective-permute-done.61.refs_1_ = bf16[2,128,1024]{2,1,0:T(8,128)(2,1)S(1)} collective-permute-done((bf16[2,128,1024]{2,1,0:T(8,128)(2,1)S(1)}, bf16[2,128,1024]{2,1,0:T(8,128)(2,1)S(1)}, u32[]{:S(2)}, u32[]{:S(2)}) %collective-permute-start.61) | collective-permute-done | bytes 524320 | tf_op jit(solution)/shard_map/ppermute | solution.py:64
  (416 shorter events, 290.4 us)
Async XLA Ops:
  7.2 210.0 %all-gather.5.cloned.1.call-start = ((), (), s32[]{:S(2)}) async-start(), calls=%async_computation.1 | async-start | bytes 22282240 | tf_op jit(solution)/shard_map/all_gather | solution.py:848
  77.6 246.3 %all-gather.3.cloned.1.call-start = ((), (), s32[]{:S(2)}) async-start(), calls=%async_computation | async-start | bytes 13369344 | tf_op jit(solution)/shard_map/all_gather | solution.py:848
  78.9 54.9 %collective-permute-start.22 = (bf16[128,1024]{1,0:T(8,128)(2,1)S(1)}, bf16[128,1024]{1,0:T(8,128)(2,1)S(1)}, u32[]{:S(2)}, u32[]{:S(2)}) collective-permute-start(bf16[128,1024]{1,0:T(8,128)(2,1)S(1)} %copy-done.59), channel_id=1, source_target_pairs={{0,16},{8,24},{16,0},{24,8},{1,17},{9,25},{17,1},{25,9},{2,18},{10... | collective-permute-start | bytes 786440 | tf_op jit(solution)/shard_map/ppermute | solution.py:67
  91.6 34.1 %collective-permute-start.17 = (bf16[512,256]{1,0:T(8,128)(2,1)}, bf16[512,256]{1,0:T(8,128)(2,1)S(1)}, u32[]{:S(2)}, u32[]{:S(2)}) collective-permute-start(bf16[512,256]{1,0:T(8,128)(2,1)} %copy-done.86), channel_id=1, source_target_pairs={{0,2},{2,4},{4,6},{6,0},{1,3},{3,5},{5,7},{7,1},{8,10},{10,12},{12... | collective-permute-start | bytes 786440 | tf_op jit(solution)/shard_map/ppermute | solution.py:64
  91.6 33.2 %collective-permute-start.21 = (bf16[128,1024]{1,0:T(8,128)(2,1)S(1)}, bf16[128,1024]{1,0:T(8,128)(2,1)S(1)}, u32[]{:S(2)}, u32[]{:S(2)}) collective-permute-start(bf16[128,1024]{1,0:T(8,128)(2,1)S(1)} %collective-permute-done.19.refs_1_), channel_id=1, source_target_pairs={{0,2},{2,4},{4,6},{6,0},{1,3},{3,5},{5,7},{7,1},{8,10},{10,12},{12... | collective-permute-start | bytes 786440 | tf_op jit(solution)/shard_map/ppermute | solution.py:64
  97.8 36.0 %collective-permute-start.23 = (bf16[128,1024]{1,0:T(8,128)(2,1)S(1)}, bf16[128,1024]{1,0:T(8,128)(2,1)S(1)}, u32[]{:S(2)}, u32[]{:S(2)}) collective-permute-start(bf16[128,1024]{1,0:T(8,128)(2,1)S(1)} %collective-permute-done.19.refs_1_), channel_id=1, source_target_pairs={{0,16},{8,24},{16,0},{24,8},{1,17},{9,25},{17,1},{25,9},{2,18},{10... | collective-permute-start | bytes 786440 | tf_op jit(solution)/shard_map/ppermute | solution.py:67
  144.0 47.7 %collective-permute-start.27 = (bf16[512,2048]{1,0:T(8,128)(2,1)S(1)}, bf16[512,2048]{1,0:T(8,128)(2,1)S(1)}, u32[]{:S(2)}, u32[]{:S(2)}) collective-permute-start(bf16[512,2048]{1,0:T(8,128)(2,1)S(1)} %shard_map.210.refs_0_), channel_id=1, source_target_pairs={{0,1},{1,0},{2,3},{3,2},{4,5},{5,4},{6,7},{7,6},{8,9},{9,8},{10,11... | collective-permute-start | bytes 6291464 | tf_op jit(solution)/shard_map/ppermute | solution.py:136
  263.9 60.0 %collective-permute-start.30 = (bf16[512,2560]{1,0:T(8,128)(2,1)}, bf16[512,2560]{1,0:T(8,128)(2,1)}, u32[]{:S(2)}, u32[]{:S(2)}) collective-permute-start(bf16[512,2560]{1,0:T(8,128)(2,1)} %get-tuple-element.302), channel_id=1, source_target_pairs={{0,8},{8,0},{16,24},{24,16},{1,9},{9,1},{17,25},{25,17},{2,10},{10... | collective-permute-start | bytes 7864328 | tf_op jit(solution)/shard_map/ppermute | solution.py:70
  264.0 59.9 %collective-permute-start.31 = (bf16[512,2560]{1,0:T(8,128)(2,1)}, bf16[512,2560]{1,0:T(8,128)(2,1)}, u32[]{:S(2)}, u32[]{:S(2)}) collective-permute-start(bf16[512,2560]{1,0:T(8,128)(2,1)} %get-tuple-element.303), channel_id=1, source_target_pairs={{0,8},{8,0},{16,24},{24,16},{1,9},{9,1},{17,25},{25,17},{2,10},{10... | collective-permute-start | bytes 7864328 | tf_op jit(solution)/shard_map/ppermute | solution.py:70
  283.7 127.3 %collective-permute-start.36 = (bf16[2,512,2560]{2,1,0:T(8,128)(2,1)}, bf16[2,512,2560]{2,1,0:T(8,128)(2,1)}, u32[]{:S(2)}, u32[]{:S(2)}) collective-permute-start(bf16[2,512,2560]{2,1,0:T(8,128)(2,1)} %shard_map.213), channel_id=1, source_target_pairs={{0,16},{8,24},{16,0},{24,8},{1,17},{9,25},{17,1},{25,9},{2,18},{10... | collective-permute-start | bytes 15728648 | tf_op jit(solution)/shard_map/ppermute | solution.py:67
  342.4 48.1 %collective-permute-start.32 = (bf16[512,2048]{1,0:T(8,128)(2,1)}, bf16[512,2048]{1,0:T(8,128)(2,1)S(1)}, u32[]{:S(2)}, u32[]{:S(2)}) collective-permute-start(bf16[512,2048]{1,0:T(8,128)(2,1)} %get-tuple-element.332.refs_0_), channel_id=1, source_target_pairs={{0,1},{1,0},{2,3},{3,2},{4,5},{5,4},{6,7},{7,6},{8,9},{9,8},{10,11... | collective-permute-start | bytes 6291464 | tf_op jit(solution)/shard_map/ppermute | solution.py:136
  401.1 47.4 %collective-permute-start.35 = (bf16[512,2048]{1,0:T(8,128)(2,1)}, bf16[512,2048]{1,0:T(8,128)(2,1)}, u32[]{:S(2)}, u32[]{:S(2)}) collective-permute-start(bf16[512,2048]{1,0:T(8,128)(2,1)} %get-tuple-element.356), channel_id=1, source_target_pairs={{0,1},{1,0},{2,3},{3,2},{4,5},{5,4},{6,7},{7,6},{8,9},{9,8},{10,11... | collective-permute-start | bytes 6291464 | tf_op jit(solution)/shard_map/ppermute | solution.py:136
  402.7 120.5 %collective-permute-start.45 = (bf16[2,512,1536]{2,1,0:T(8,128)(2,1)}, bf16[2,512,1536]{2,1,0:T(8,128)(2,1)}, u32[]{:S(2)}, u32[]{:S(2)}) collective-permute-start(bf16[2,512,1536]{2,1,0:T(8,128)(2,1)} %copy-done.23), channel_id=1, source_target_pairs={{0,16},{8,24},{16,0},{24,8},{1,17},{9,25},{17,1},{25,9},{2,18},{10... | collective-permute-start | bytes 9437192 | tf_op jit(solution)/shard_map/ppermute | solution.py:67
  448.5 49.7 %collective-permute-start.43 = (bf16[2,128,2560]{2,1,0:T(8,128)(2,1)S(1)}, bf16[2,128,2560]{2,1,0:T(8,128)(2,1)S(1)}, u32[]{:S(2)}, u32[]{:S(2)}) collective-permute-start(bf16[2,128,2560]{2,1,0:T(8,128)(2,1)S(1)} %copy-done.55), channel_id=1, source_target_pairs={{0,6},{2,0},{4,2},{6,4},{1,7},{3,1},{5,3},{7,5},{8,14},{10,8},{12,... | collective-permute-start | bytes 3932168 | tf_op jit(solution)/shard_map/ppermute | solution.py:64
  467.2 82.5 %collective-permute-start.39 = (bf16[512,2048]{1,0:T(8,128)(2,1)}, bf16[512,2048]{1,0:T(8,128)(2,1)}, u32[]{:S(2)}, u32[]{:S(2)}) collective-permute-start(bf16[512,2048]{1,0:T(8,128)(2,1)} %shard_map.221.refs_0_), channel_id=1, source_target_pairs={{0,1},{1,0},{2,3},{3,2},{4,5},{5,4},{6,7},{7,6},{8,9},{9,8},{10,11... | collective-permute-start | bytes 6291464 | tf_op jit(solution)/shard_map/ppermute | solution.py:136
  512.0 48.6 %collective-permute-start.54 = (bf16[2,128,2560]{2,1,0:T(8,128)(2,1)}, bf16[2,128,2560]{2,1,0:T(8,128)(2,1)}, u32[]{:S(2)}, u32[]{:S(2)}) collective-permute-start(bf16[2,128,2560]{2,1,0:T(8,128)(2,1)} %copy-done.53), channel_id=1, source_target_pairs={{0,2},{2,4},{4,6},{6,0},{1,3},{3,5},{5,7},{7,1},{8,10},{10,12},{12... | collective-permute-start | bytes 3932168 | tf_op jit(solution)/shard_map/ppermute | solution.py:64
  512.1 69.3 %collective-permute-start.53 = (bf16[2,128,2560]{2,1,0:T(8,128)(2,1)}, bf16[2,128,2560]{2,1,0:T(8,128)(2,1)}, u32[]{:S(2)}, u32[]{:S(2)}) collective-permute-start(bf16[2,128,2560]{2,1,0:T(8,128)(2,1)} %shard_map.223), channel_id=1, source_target_pairs={{0,6},{2,0},{4,2},{6,4},{1,7},{3,1},{5,3},{7,5},{8,14},{10,8},{12,... | collective-permute-start | bytes 3932168 | tf_op jit(solution)/shard_map/ppermute | solution.py:64
  523.2 83.1 %collective-permute-start.51 = (bf16[2,512,1024]{2,1,0:T(8,128)(2,1)}, bf16[2,512,1024]{2,1,0:T(8,128)(2,1)}, u32[]{:S(2)}, u32[]{:S(2)}) collective-permute-start(bf16[2,512,1024]{2,1,0:T(8,128)(2,1)} %shard_map.225), channel_id=1, source_target_pairs={{0,16},{8,24},{16,0},{24,8},{1,17},{9,25},{17,1},{25,9},{2,18},{10... | collective-permute-start | bytes 6291464 | tf_op jit(solution)/shard_map/ppermute | solution.py:67
  547.3 49.7 %collective-permute-start.49 = (bf16[512,1024]{1,0:T(8,128)(2,1)}, bf16[512,1024]{1,0:T(8,128)(2,1)S(1)}, u32[]{:S(2)}, u32[]{:S(2)}) collective-permute-start(bf16[512,1024]{1,0:T(8,128)(2,1)} %get-tuple-element.408), channel_id=1, source_target_pairs={{0,8},{8,0},{16,24},{24,16},{1,9},{9,1},{17,25},{25,17},{2,10},{10... | collective-permute-start | bytes 3145736 | tf_op jit(solution)/shard_map/ppermute | solution.py:70
  549.6 49.1 %collective-permute-start.50 = (bf16[512,1024]{1,0:T(8,128)(2,1)}, bf16[512,1024]{1,0:T(8,128)(2,1)S(1)}, u32[]{:S(2)}, u32[]{:S(2)}) collective-permute-start(bf16[512,1024]{1,0:T(8,128)(2,1)} %get-tuple-element.409), channel_id=1, source_target_pairs={{0,8},{8,0},{16,24},{24,16},{1,9},{9,1},{17,25},{25,17},{2,10},{10... | collective-permute-start | bytes 3145736 | tf_op jit(solution)/shard_map/ppermute | solution.py:70
  560.6 33.3 %collective-permute-start.52 = (bf16[2,128,1536]{2,1,0:T(8,128)(2,1)}, bf16[2,128,1536]{2,1,0:T(8,128)(2,1)S(1)}, u32[]{:S(2)}, u32[]{:S(2)}) collective-permute-start(bf16[2,128,1536]{2,1,0:T(8,128)(2,1)} %copy-done.57), channel_id=1, source_target_pairs={{0,6},{2,0},{4,2},{6,4},{1,7},{3,1},{5,3},{7,5},{8,14},{10,8},{12,... | collective-permute-start | bytes 2359304 | tf_op jit(solution)/shard_map/ppermute | solution.py:64
  581.4 37.4 %collective-permute-start.63 = (bf16[2,128,1536]{2,1,0:T(8,128)(2,1)}, bf16[2,128,1536]{2,1,0:T(8,128)(2,1)}, u32[]{:S(2)}, u32[]{:S(2)}) collective-permute-start(bf16[2,128,1536]{2,1,0:T(8,128)(2,1)} %copy-done.56), channel_id=1, source_target_pairs={{0,2},{2,4},{4,6},{6,0},{1,3},{3,5},{5,7},{7,1},{8,10},{10,12},{12... | collective-permute-start | bytes 2359304 | tf_op jit(solution)/shard_map/ppermute | solution.py:64
  598.7 36.7 %collective-permute-start.62 = (bf16[2,128,1536]{2,1,0:T(8,128)(2,1)}, bf16[2,128,1536]{2,1,0:T(8,128)(2,1)S(1)}, u32[]{:S(2)}, u32[]{:S(2)}) collective-permute-start(bf16[2,128,1536]{2,1,0:T(8,128)(2,1)} %shard_map.233), channel_id=1, source_target_pairs={{0,6},{2,0},{4,2},{6,4},{1,7},{3,1},{5,3},{7,5},{8,14},{10,8},{12,... | collective-permute-start | bytes 2359304 | tf_op jit(solution)/shard_map/ppermute | solution.py:64
  649.1 40.0 %collective-permute-start.69 = (bf16[1,128,256]{2,1,0:T(8,128)(2,1)S(1)}, bf16[1,128,256]{2,1,0:T(8,128)(2,1)S(1)}, u32[]{:S(2)}, u32[]{:S(2)}) collective-permute-start(bf16[1,128,256]{2,1,0:T(8,128)(2,1)S(1)} %get-tuple-element.444), channel_id=1, source_target_pairs={{0,2},{2,4},{4,6},{6,0},{1,3},{3,5},{5,7},{7,1},{8,10},{10,12},{12... | collective-permute-start | bytes 196616 | tf_op jit(solution)/shard_map/ppermute | solution.py:64
  (149 other events, 1400.6 us)
Sparse Core Ops, SparseCore 0:
  77.7 139.4 all-gather.4
  219.4 104.3 all-gather.2

commit v4 on v3

--- a/solution.py
+++ b/solution.py
@@ -609,44 +609,43 @@
 
 def outer(pairs, count):
     rows, width = pairs[0][0].shape
-    n = pairs[0][1].shape[1]
-    half, kinds = width // 2, len(pairs)
+    half = width // 2
+    spans, n = [], 0
+    for _, b in pairs:
+        spans.append(slice(n, n + b.shape[1]))
+        n += b.shape[1]
     shape = jax.ShapeDtypeStruct
 
-    def part(start, size, joined):
+    def part(start, size, lead):
         tile = min(size, 256)
 
         def kernel(*refs):
-            for kind in range(kinds):
-                value = dot_tn(refs[2 * kind][...], refs[2 * kind + 1][...]).astype(BF16)
-                if joined:
-                    refs[-1][kind] = value
+            for k, span in enumerate(spans):
+                value = dot_tn(refs[2 * k][...], refs[2 * k + 1][...]).astype(BF16)
+                if lead:
+                    refs[-1][0, :, span] = value
                 else:
-                    refs[2 * kinds + kind][...] = value
-
-        if joined:
-            specs = [pl.BlockSpec((kinds, tile, n), lambda i: (0, i, 0))]
-            shapes = [shape((kinds, size, n), BF16)]
-        else:
-            specs = [pl.BlockSpec((tile, n), lambda i: (i, 0))] * kinds
-            shapes = [shape((size, n), BF16)] * kinds
+                    refs[-1][:, span] = value
+
+        specs = []
+        for a, b in pairs:
+            specs.append(pl.BlockSpec((rows, tile), lambda i: (0, start // tile + i)))
+            specs.append(pl.BlockSpec(b.shape, lambda i: (0, 0)))
         return pl.pallas_call(
             kernel,
             grid=(size // tile,),
-            in_specs=[
-                pl.BlockSpec((rows, tile), lambda i: (0, start // tile + i)),
-                pl.BlockSpec((rows, n), lambda i: (0, 0)),
-            ]
-            * kinds,
-            out_specs=specs,
-            out_shape=shapes,
+            in_specs=specs,
+            out_specs=pl.BlockSpec((*lead, tile, n), lambda i: (*(0 for _ in lead), i, 0)),
+            out_shape=shape((*lead, size, n), BF16),
             compiler_params=pltpu.CompilerParams(vmem_limit_bytes=24 * 1024 * 1024),
             cost_estimate=COST[0],
         )(*[a for pair in pairs for a in pair])
 
     each = half // count
-    parts = [part(half + k * each, each, False) for k in range(count)]
-    return [*part(0, half, True)] + [parts[k][kind] for kind in range(kinds) for k in range(count)]
+    parts = [[part(half, each, ())]]
+    for k in range(1, count):
+        parts.append([part(half + k * each + h * each // 2, each // 2, ()) for h in range(2)])
+    return part(0, half, (1,)), parts
 
 
 def diagonal_mask(rows):
@@ -926,39 +925,47 @@
         result = hidden + branch
         return result.astype(BF16), jnp.sum(result * result), jnp.sum(branch * branch)
 
-    layer_out, square_r, square_m = run(finish, hidden, *br_parts)
+    sends = run(lambda d: [d[k].astype(BF16) for k in range(1, nz)], dkv)
+    got_kv = [ring.z(s, -k - 1) for k, s in enumerate(sends)]
     dq_part = run(widened, dq, q_mine, q_other)
     dq_parts = [dq_part, *tp_others(dq_part)]
-    sends = run(lambda d: [d[k].astype(BF16) for k in range(1, nz)], dkv)
-    got_kv = [ring.z(s, -k - 1) for k, s in enumerate(sends)]
-    oq_s = scatter_core(*run(lambda *a: outer((a[:2], a[2:]), ring.nx), d_branch, attn_low, normed, dq))
+    layer_out, square_r, square_m = run(finish, hidden, *br_parts)
     g_a = scatter_mid(g_a)
-    mine_kv = run(lambda d, *g: added([d[0], *g]).astype(BF16), dkv, *got_kv)
-    kv_parts = [mine_kv, *tp_others(mine_kv)]
-    oq_s = scatter_x(oq_s)
+    dkv_own = run(lambda d, *g: added([d[0], *g]).astype(BF16), dkv, *got_kv)
+    kv_parts = [dkv_own, *tp_others(dkv_own)]
+    okv_own, okv_pieces = run(
+        lambda *a: outer(((a[0], a[1]), (a[2], a[3]), (a[2], a[4])), ring.nx),
+        d_branch, attn_low, normed, dq, dkv_own,
+    )
+    okv_got = [[ring.core(p) for p in piece] for piece in okv_pieces[1:]]
+    okv_late = ring.core(after(okv_pieces[0][0], dq_parts[-1]))
     g_b = scatter_z(g_b)
-    dkv_low = run(lambda *p: added(p).astype(BF16), *kv_parts)
-    kv_s = scatter_core(*run(lambda *a: outer((a,), ring.nx), normed, dkv_low))
-    dkv_part = run(widened, dkv_low, *w_kv)
-    kv_s = scatter_x(kv_s)
+    okv_x = []
+    for k, got in enumerate(okv_got):
+        side = run(
+            lambda m, *o, k=k: side_call(m, [jnp.concatenate(o, axis=0)], k + 1, ring.nx), okv_own, *got
+        )
+        okv_x.append(ring.x(side, -k - 1))
+    dkv_part = run(lambda a, b, *p: widened(added(p).astype(BF16), a, b), *w_kv, *kv_parts)
     input_grad, d_one = run(
         lambda *a: first_back(*a[:5], a[5:], order),
         tokens, grad_hidden, mean1, rate1, gains[0:1], *dq_parts, dkv_part,
     )
+    g_b = scatter_mid(g_b)
     end_a = scatter_end(g_a)
-    g_b = scatter_mid(g_b)
-    oq_s = scatter_z(oq_s)
-    kv_s = scatter_z(kv_s)
-    end_b = scatter_end(g_b)
-    oq_s = scatter_mid(oq_s)
-    kv_s = scatter_mid(kv_s)
+    okv = scatter_z((okv_own, [okv_late], okv_x))
     squares = jnp.stack([square_r, jnp.sum(attn_square), square_m])
-    squares = after(jnp.broadcast_to(squares[:, None], (3, 128)), oq_s[-1])
+    squares = after(jnp.broadcast_to(squares[:, None], (3, 128)), okv[-1])
     rms_values = jnp.sqrt(ring.small_sum(squares)[:, 0] / entries)
     small = gathered(jnp.concatenate([d_one, d_two], axis=0), order)
-    small = ring.small_scatter(after(small, oq_s[-1]))
-    grad_out_proj, grad_query = scatter_end(oq_s)
-    grad_keyval = scatter_end(kv_s)[0]
+    small = ring.small_scatter(after(small, okv[-1]))
+    end_b = scatter_end(g_b)
+    okv = scatter_mid(okv)
+    last = scatter_end(okv)[0]
+    q_cols = w_query.shape[1]
+    grad_out_proj, grad_query = last[:, :q_cols], last[:, q_cols : 2 * q_cols]
+    grad_keyval = last[:, 2 * q_cols :]
+    grad_keyval = added([grad_keyval, *tp_others(grad_keyval)])
     grad_up, grad_down = (
         jnp.concatenate([e[k] for e in (end_a, end_b)], axis=1) for k in range(2)
     )

time: 706 us -> 678 us (0.960)
  starting transfers between devices: 106 us -> 98.7 us
    ppermute x5 -> x6, waiting for transfers between devices: 79.5 us -> 65.5 us  [tp_others(): lax.ppermute(part, 'tp', [(i, (i + k) % n) for i in range(n)])]
    ppermute x30 -> x27, starting transfers between devices: 72.8 us -> 64.8 us  [z(): lax.ppermute(value, 'ctx', [(i, (i + k) % self.nz) for i in range(self.nz)])]
    unnamed x186 -> x158, local copies, waits for them, and re-layouts: 50.6 us -> 44.1 us
    ppermute x30 -> x27, waiting for transfers between devices: 126 us -> 132 us  [z(): lax.ppermute(value, 'ctx', [(i, (i + k) % self.nz) for i in range(self.nz)])]
    ppermute x17 -> x16, starting transfers between devices: 20.6 us -> 20 us  [x(): lax.ppermute(value, 'dp', [(i, (i + 2 * k) % self.ndp) for i in range(sel...]
    ppermute x19 -> x16, waiting for transfers between devices: 21 us -> 21 us  [core(): return lax.ppermute(value, 'dp', [(i, i ^ 1) for i in range(self.ndp)])]
  transfers between devices with their start and end apart: 76 -> 70, of which waited for: 30 -> 28; matrix products, arithmetic and copies ran while one was open for 5% -> 4% of each run, Pallas kernels for 29% -> 29%
where the time goes in v4:
time: 678 us; the launch traced here: 672 us
  waiting for transfers between devices  285 us (42%)
  Pallas kernels  197 us (29%)
  starting transfers between devices  98.7 us (15%)
  local copies, waits for them, and re-layouts  50.4 us (7%)
  other arithmetic  25.7 us (4%)
  between operations  15.6 us (2%)
    ppermute x27, waiting for transfers between devices, z(): lax.ppermute(value, 'ctx', [(i, (i + k) % self.nz) for i in range(self.nz)])  132 us
    pallas_call x3, Pallas kernels, call(): pl.pallas_call(kernel, grid=(self.n // self.tile,), in_specs=in_specs, ou...  83.3 us
    ppermute x6, waiting for transfers between devices, tp_others(): lax.ppermute(part, 'tp', [(i, (i + k) % n) for i in range(n)])  65.5 us
    ppermute x27, starting transfers between devices, z(): lax.ppermute(value, 'ctx', [(i, (i + k) % self.nz) for i in range(self.nz)])  64.8 us
    all_gather x2, waiting for transfers between devices, ff_gather(): return lax.all_gather(shard, both, axis=0, tiled=True)  51 us
    unnamed x158, local copies, waits for them, and re-layouts  44.1 us
    pallas_call x5, Pallas kernels, row_call(): pl.pallas_call(kernel, grid_spec=pltpu.PrefetchScalarGridSpec(num_scalar_...  38.3 us
    ppermute x16, waiting for transfers between devices, core(): return lax.ppermute(value, 'dp', [(i, i ^ 1) for i in range(self.ndp)])  21 us
  transfers between devices with their start and end apart: 70, of which 28 were waited for; matrix products, arithmetic and copies ran while one was open for 4% of the time, Pallas kernels for 29%

profile of v4, /device:TPU:0, one launch (start us, length us, event | category | flops | bytes accessed | tf_op | source)
XLA Modules:
  0.0 672.4 jit_solution(17576000300032698641)
XLA Ops:
  83.8 7.8 %collective-permute-done.19.refs_1_ = bf16[128,1024]{1,0:T(8,128)(2,1)S(1)} collective-permute-done((bf16[128,1024]{1,0:T(8,128)(2,1)S(1)}, bf16[128,1024]{1,0:T(8,128)(2,1)S(1)}, u32[]{:S(2)}, u32[]{:S(2)}) %collective-permute-start.19) | collective-permute-done | bytes 262176 | tf_op jit(solution)/shard_map/ppermute | solution.py:64
  98.5 6.9 %collective-permute-done.20.refs_3_ = bf16[128,1024]{1,0:T(8,128)(2,1)S(1)} collective-permute-done((bf16[128,1024]{1,0:T(8,128)(2,1)S(1)}, bf16[128,1024]{1,0:T(8,128)(2,1)S(1)}, u32[]{:S(2)}, u32[]{:S(2)}) %collective-permute-start.20) | collective-permute-done | bytes 262176 | tf_op jit(solution)/shard_map/ppermute | solution.py:64
  105.9 18.9 %collective-permute-done.21.refs_2_ = bf16[128,1024]{1,0:T(8,128)(2,1)S(1)} collective-permute-done((bf16[128,1024]{1,0:T(8,128)(2,1)S(1)}, bf16[128,1024]{1,0:T(8,128)(2,1)S(1)}, u32[]{:S(2)}, u32[]{:S(2)}) %collective-permute-start.21) | collective-permute-done | bytes 262176 | tf_op jit(solution)/shard_map/ppermute | solution.py:64
  126.7 6.9 %shard_map.208 = (f32[8,128,512]{2,1,0:T(8,128)S(1)}, bf16[512,1024]{1,0:T(8,128)(2,1)S(1)}, f32[8,1,512]{2,1,0:T(1,128)S(1)}) custom-call(s32[1]{0:T(128)} %bitcast.27.z_ref, bf16[512,1024]{1,0:T(8,128)(2,1)S(1)} %shard_map.207.q_ref, bf16[4,512,256]{2,1,0:T(8,128)(2,1)S(1)} %pad_maximum_fusion.4.kv_ref), custom_call_target="tpu_custom_call" | custom-call | flops 4600000000 | bytes 14000000 | tf_op jit(solution)/shard_map/pallas_call | solution.py:701
  145.6 46.1 %collective-permute-done.27.refs_1_ = bf16[512,2048]{1,0:T(8,128)(2,1)S(1)} collective-permute-done((bf16[512,2048]{1,0:T(8,128)(2,1)S(1)}, bf16[512,2048]{1,0:T(8,128)(2,1)S(1)}, u32[]{:S(2)}, u32[]{:S(2)}) %collective-permute-start.27) | collective-permute-done | bytes 2097184 | tf_op jit(solution)/shard_map/ppermute | solution.py:136
  193.1 9.2 %shard_map.211 = (bf16[512,2048]{1,0:T(8,128)(2,1)}, bf16[2048,512]{1,0:T(8,128)(2,1)}, f32[512,2048]{1,0:T(8,128)}, f32[512,1]{1,0:T(8,128)}, f32[512,1]{1,0:T(8,128)}, /*index=5*/f32[512,1]{1,0:T(8,128)}) custom-call(s32[16]{0:T(128)} %stack.143.order_ref, bf16[512,2048]{1,0:T(8,128)(2,1)} %tok_ref.2, bf16[512,2048]{1,0:T(8,128)(2,1)} %copy-done.46, ...), custom_call_target="tpu_custom_call" | custom-call | flops 4600000000 | bytes 14000000 | tf_op jit(solution)/shard_map/pallas_call | solution.py:156
  202.2 15.0 %all-gather.5.cloned.1.call-done.up.down = bf16[2048,5120]{1,0:T(8,128)(2,1)} async-done(((bf16[128,5120]{1,0:T(8,128)(2,1)}), bf16[2048,5120]{1,0:T(8,128)(2,1)}) %all-gather.5.cloned.1.call-update) | async-done | bytes 20971536 | tf_op jit(solution)/shard_map/all_gather | solution.py:847
  217.2 46.2 %shard_map.212 = (bf16[2,1024,2560]{2,1,0:T(8,128)(2,1)}, bf16[512,2560]{1,0:T(8,128)(2,1)}, bf16[512,2560]{1,0:T(8,128)(2,1)}, bf16[512,2560]{1,0:T(8,128)(2,1)...) custom-call(bf16[512,2048]{1,0:T(8,128)(2,1)} %get-tuple-element.284.nt, ...), custom_call_target="tpu_custom_call" | custom-call | flops 1000 | bytes 1000 | tf_op jit(solution)/shard_map/pallas_call | solution.py:423
  268.5 7.8 %collective-permute-done.29.refs_1_ = bf16[512,2560]{1,0:T(8,128)(2,1)S(1)} collective-permute-done((bf16[512,2560]{1,0:T(8,128)(2,1)}, bf16[512,2560]{1,0:T(8,128)(2,1)S(1)}, u32[]{:S(2)}, u32[]{:S(2)}) %collective-permute-start.29) | collective-permute-done | bytes 2621472 | tf_op jit(solution)/shard_map/ppermute | solution.py:70
  287.9 36.1 %all-gather.3.cloned.1.call-done.up.down = bf16[2048,3072]{1,0:T(8,128)(2,1)} async-done(((bf16[128,3072]{1,0:T(8,128)(2,1)}), bf16[2048,3072]{1,0:T(8,128)(2,1)}) %all-gather.3.cloned.1.call-update) | async-done | bytes 12582928 | tf_op jit(solution)/shard_map/all_gather | solution.py:847
  324.0 18.6 %shard_map.214 = (bf16[512,1536]{1,0:T(8,128)(2,1)}, bf16[512,1536]{1,0:T(8,128)(2,1)}, bf16[512,2048]{1,0:T(8,128)(2,1)}) custom-call(bf16[512,2048]{1,0:T(8,128)(2,1)} %get-tuple-element.284.nt, bf16[512,2048]{1,0:T(8,128)(2,1)} %go_ref, bf16[2048,3072]{1,0:T(8,128)(2,1)} %all-gather.3.cloned.1.call-done.up.down, ...), custom_call_target="tpu_custom_call" | custom-call | flops 1000 | bytes 1000 | tf_op jit(solution)/shard_map/pallas_call | solution.py:423
  343.6 18.6 %shard_map.215 = (bf16[2,1024,1536]{2,1,0:T(8,128)(2,1)}, bf16[512,1536]{1,0:T(8,128)(2,1)}, bf16[512,1536]{1,0:T(8,128)(2,1)}, bf16[512,1536]{1,0:T(8,128)(2,1)...) custom-call(bf16[512,1536]{1,0:T(8,128)(2,1)} %get-tuple-element.291.act, ...), custom_call_target="tpu_custom_call" | custom-call | flops 1000 | bytes 1000 | tf_op jit(solution)/shard_map/pallas_call | solution.py:423
  373.5 17.2 %collective-permute-done.32.refs_1_ = bf16[512,2048]{1,0:T(8,128)(2,1)} collective-permute-done((bf16[512,2048]{1,0:T(8,128)(2,1)}, bf16[512,2048]{1,0:T(8,128)(2,1)}, u32[]{:S(2)}, u32[]{:S(2)}) %collective-permute-start.32) | collective-permute-done | bytes 2097184 | tf_op jit(solution)/shard_map/ppermute | solution.py:136
  390.7 9.3 %shard_map.217 = (bf16[512,2048]{1,0:T(8,128)(2,1)}, f32[512,2048]{1,0:T(8,128)}, f32[2,2048]{1,0:T(2,128)}) custom-call(s32[16]{0:T(128)} %stack.143.order_ref, f32[512,2048]{1,0:T(8,128)} %get-tuple-element.340.hid_ref, bf16[512,2048]{1,0:T(8,128)(2,1)} %go_ref, f32[512,1]{1,0:T(8,128)} %get-tuple-element.309.mean_ref, ...), custom_call_target="tpu_custom_call" | custom-call | flops 1000 | bytes 1000 | tf_op jit(solution)/shard_map/pallas_call | solution.py:156
  422.4 8.4 %shard_map.220 = (bf16[512,1024]{1,0:T(8,128)(2,1)S(1)}, f32[4,512,256]{2,1,0:T(8,128)S(1)}) custom-call(s32[1]{0:T(128)} %bitcast.27.z_ref, bf16[512,1024]{1,0:T(8,128)(2,1)S(1)} %copy-done.43, bf16[4,512,256]{2,1,0:T(8,128)(2,1)S(1)} %copy-done.19, bf16[512,1024]{1,0:T(8,128)(2,1)S(1)} %shard_map.218.d_ref, f32[8,128,512]{2,1,0:T(8,128)S(1)} %copy-done.32, ...), custom_call_target="tpu_custom_call" | custom-call | flops 1000 | bytes 1000 | tf_op jit(solution)/shard_map/pallas_call | solution.py:774
  440.7 23.3 %collective-permute-start.40 = (bf16[512,256]{1,0:T(8,128)(2,1)}, bf16[512,256]{1,0:T(8,128)(2,1)}, u32[]{:S(2)}, u32[]{:S(2)}) collective-permute-start(bf16[512,256]{1,0:T(8,128)(2,1)} %get-tuple-element.421), channel_id=1, source_target_pairs={{0,6},{2,0},{4,2},{6,4},{1,7},{3,1},{5,3},{7,5},{8,14},{10,8},{12,... | collective-permute-start | bytes 786440 | tf_op jit(solution)/shard_map/ppermute | solution.py:64
  473.0 10.8 %collective-permute-done.41 = bf16[512,256]{1,0:T(8,128)(2,1)} collective-permute-done((bf16[512,256]{1,0:T(8,128)(2,1)}, bf16[512,256]{1,0:T(8,128)(2,1)}, u32[]{:S(2)}, u32[]{:S(2)}) %collective-permute-start.41) | collective-permute-done | bytes 262176 | tf_op jit(solution)/shard_map/ppermute | solution.py:64
  531.1 9.5 %shard_map.229 = (f32[512,2048]{1,0:T(8,128)}, f32[2,2048]{1,0:T(2,128)}) custom-call(s32[16]{0:T(128)} %stack.143.order_ref, bf16[512,2048]{1,0:T(8,128)(2,1)} %tok_ref.2, f32[512,2048]{1,0:T(8,128)} %get-tuple-element.372.gh_ref, f32[512,1]{1,0:T(8,128)} %get-tuple-element.373.mean_ref, f32[512,1]{1,0:T(8,128)} %get-tuple-element.374.rate_ref, ...), custom_call_target="tpu_custom_call" | custom-call | flops 1000 | bytes 1000 | tf_op jit(solution)/shard_map/pallas_call | solution.py:156
  540.6 28.7 %collective-permute-done.52.refs_1_ = bf16[2,128,1536]{2,1,0:T(8,128)(2,1)} collective-permute-done((bf16[2,128,1536]{2,1,0:T(8,128)(2,1)}, bf16[2,128,1536]{2,1,0:T(8,128)(2,1)}, u32[]{:S(2)}, u32[]{:S(2)}) %collective-permute-start.52) | collective-permute-done | bytes 786464 | tf_op jit(solution)/shard_map/ppermute | solution.py:64
  583.3 8.5 %collective-permute-done.61 = bf16[2,128,1536]{2,1,0:T(8,128)(2,1)} collective-permute-done((bf16[2,128,1536]{2,1,0:T(8,128)(2,1)}, bf16[2,128,1536]{2,1,0:T(8,128)(2,1)}, u32[]{:S(2)}, u32[]{:S(2)}) %collective-permute-start.61) | collective-permute-done | bytes 786464 | tf_op jit(solution)/shard_map/ppermute | solution.py:64
  591.9 16.7 %collective-permute-done.60 = bf16[2,128,1536]{2,1,0:T(8,128)(2,1)S(1)} collective-permute-done((bf16[2,128,1536]{2,1,0:T(8,128)(2,1)}, bf16[2,128,1536]{2,1,0:T(8,128)(2,1)S(1)}, u32[]{:S(2)}, u32[]{:S(2)}) %collective-permute-start.60) | collective-permute-done | bytes 786464 | tf_op jit(solution)/shard_map/ppermute | solution.py:64
  608.5 11.8 %collective-permute-done.53 = bf16[1,128,2304]{2,1,0:T(8,128)(2,1)S(1)} collective-permute-done((bf16[1,128,2304]{2,1,0:T(8,128)(2,1)S(1)}, bf16[1,128,2304]{2,1,0:T(8,128)(2,1)S(1)}, u32[]{:S(2)}, u32[]{:S(2)}) %collective-permute-start.53) | collective-permute-done | bytes 589856 | tf_op jit(solution)/shard_map/ppermute | solution.py:64
  631.0 9.0 %collective-permute-done.59.refs_1_ = bf16[1,128,2304]{2,1,0:T(8,128)(2,1)S(1)} collective-permute-done((bf16[1,128,2304]{2,1,0:T(8,128)(2,1)S(1)}, bf16[1,128,2304]{2,1,0:T(8,128)(2,1)S(1)}, u32[]{:S(2)}, u32[]{:S(2)}) %collective-permute-start.59) | collective-permute-done | bytes 589856 | tf_op jit(solution)/shard_map/ppermute | solution.py:64
  650.5 7.5 %collective-permute-done.67 = f32[3,128]{0,1:T(8,128)S(1)} collective-permute-done((f32[3,128]{0,1:T(8,128)S(1)}, f32[3,128]{0,1:T(8,128)S(1)}, u32[]{:S(2)}, u32[]{:S(2)}) %collective-permute-start.67) | collective-permute-done | bytes 1568 | tf_op jit(solution)/shard_map/ppermute | solution.py:114
  (374 shorter events, 258.1 us)
Async XLA Ops:
  7.2 210.0 %all-gather.5.cloned.1.call-start = ((), (), s32[]{:S(2)}) async-start(), calls=%async_computation.1 | async-start | bytes 22282240 | tf_op jit(solution)/shard_map/all_gather | solution.py:847
  77.6 246.4 %all-gather.3.cloned.1.call-start = ((), (), s32[]{:S(2)}) async-start(), calls=%async_computation | async-start | bytes 13369344 | tf_op jit(solution)/shard_map/all_gather | solution.py:847
  79.0 54.7 %collective-permute-start.22 = (bf16[128,1024]{1,0:T(8,128)(2,1)S(1)}, bf16[128,1024]{1,0:T(8,128)(2,1)S(1)}, u32[]{:S(2)}, u32[]{:S(2)}) collective-permute-start(bf16[128,1024]{1,0:T(8,128)(2,1)S(1)} %copy-done.50), channel_id=1, source_target_pairs={{0,16},{8,24},{16,0},{24,8},{1,17},{9,25},{17,1},{25,9},{2,18},{10... | collective-permute-start | bytes 786440 | tf_op jit(solution)/shard_map/ppermute | solution.py:67
  91.6 34.0 %collective-permute-start.17 = (bf16[512,256]{1,0:T(8,128)(2,1)}, bf16[512,256]{1,0:T(8,128)(2,1)S(1)}, u32[]{:S(2)}, u32[]{:S(2)}) collective-permute-start(bf16[512,256]{1,0:T(8,128)(2,1)} %copy-done.70), channel_id=1, source_target_pairs={{0,2},{2,4},{4,6},{6,0},{1,3},{3,5},{5,7},{7,1},{8,10},{10,12},{12... | collective-permute-start | bytes 786440 | tf_op jit(solution)/shard_map/ppermute | solution.py:64
  91.6 33.2 %collective-permute-start.21 = (bf16[128,1024]{1,0:T(8,128)(2,1)S(1)}, bf16[128,1024]{1,0:T(8,128)(2,1)S(1)}, u32[]{:S(2)}, u32[]{:S(2)}) collective-permute-start(bf16[128,1024]{1,0:T(8,128)(2,1)S(1)} %collective-permute-done.19.refs_1_), channel_id=1, source_target_pairs={{0,2},{2,4},{4,6},{6,0},{1,3},{3,5},{5,7},{7,1},{8,10},{10,12},{12... | collective-permute-start | bytes 786440 | tf_op jit(solution)/shard_map/ppermute | solution.py:64
  97.8 35.9 %collective-permute-start.23 = (bf16[128,1024]{1,0:T(8,128)(2,1)S(1)}, bf16[128,1024]{1,0:T(8,128)(2,1)S(1)}, u32[]{:S(2)}, u32[]{:S(2)}) collective-permute-start(bf16[128,1024]{1,0:T(8,128)(2,1)S(1)} %collective-permute-done.19.refs_1_), channel_id=1, source_target_pairs={{0,16},{8,24},{16,0},{24,8},{1,17},{9,25},{17,1},{25,9},{2,18},{10... | collective-permute-start | bytes 786440 | tf_op jit(solution)/shard_map/ppermute | solution.py:67
  105.4 28.3 %collective-permute-start.25 = (bf16[128,1024]{1,0:T(8,128)(2,1)S(1)}, bf16[128,1024]{1,0:T(8,128)(2,1)S(1)}, u32[]{:S(2)}, u32[]{:S(2)}) collective-permute-start(bf16[128,1024]{1,0:T(8,128)(2,1)S(1)} %collective-permute-done.20.refs_3_), channel_id=1, source_target_pairs={{0,16},{8,24},{16,0},{24,8},{1,17},{9,25},{17,1},{25,9},{2,18},{10... | collective-permute-start | bytes 786440 | tf_op jit(solution)/shard_map/ppermute | solution.py:67
  143.9 47.8 %collective-permute-start.27 = (bf16[512,2048]{1,0:T(8,128)(2,1)S(1)}, bf16[512,2048]{1,0:T(8,128)(2,1)S(1)}, u32[]{:S(2)}, u32[]{:S(2)}) collective-permute-start(bf16[512,2048]{1,0:T(8,128)(2,1)S(1)} %shard_map.210.refs_0_), channel_id=1, source_target_pairs={{0,1},{1,0},{2,3},{3,2},{4,5},{5,4},{6,7},{7,6},{8,9},{9,8},{10,11... | collective-permute-start | bytes 6291464 | tf_op jit(solution)/shard_map/ppermute | solution.py:136
  263.9 60.1 %collective-permute-start.30 = (bf16[512,2560]{1,0:T(8,128)(2,1)}, bf16[512,2560]{1,0:T(8,128)(2,1)}, u32[]{:S(2)}, u32[]{:S(2)}) collective-permute-start(bf16[512,2560]{1,0:T(8,128)(2,1)} %get-tuple-element.282), channel_id=1, source_target_pairs={{0,8},{8,0},{16,24},{24,16},{1,9},{9,1},{17,25},{25,17},{2,10},{10... | collective-permute-start | bytes 7864328 | tf_op jit(solution)/shard_map/ppermute | solution.py:70
  264.0 60.0 %collective-permute-start.31 = (bf16[512,2560]{1,0:T(8,128)(2,1)}, bf16[512,2560]{1,0:T(8,128)(2,1)}, u32[]{:S(2)}, u32[]{:S(2)}) collective-permute-start(bf16[512,2560]{1,0:T(8,128)(2,1)} %get-tuple-element.283), channel_id=1, source_target_pairs={{0,8},{8,0},{16,24},{24,16},{1,9},{9,1},{17,25},{25,17},{2,10},{10... | collective-permute-start | bytes 7864328 | tf_op jit(solution)/shard_map/ppermute | solution.py:70
  283.7 126.2 %collective-permute-start.36 = (bf16[2,512,2560]{2,1,0:T(8,128)(2,1)}, bf16[2,512,2560]{2,1,0:T(8,128)(2,1)}, u32[]{:S(2)}, u32[]{:S(2)}) collective-permute-start(bf16[2,512,2560]{2,1,0:T(8,128)(2,1)} %shard_map.213), channel_id=1, source_target_pairs={{0,16},{8,24},{16,0},{24,8},{1,17},{9,25},{17,1},{25,9},{2,18},{10... | collective-permute-start | bytes 15728648 | tf_op jit(solution)/shard_map/ppermute | solution.py:67
  342.6 48.2 %collective-permute-start.32 = (bf16[512,2048]{1,0:T(8,128)(2,1)}, bf16[512,2048]{1,0:T(8,128)(2,1)}, u32[]{:S(2)}, u32[]{:S(2)}) collective-permute-start(bf16[512,2048]{1,0:T(8,128)(2,1)} %get-tuple-element.312.refs_0_), channel_id=1, source_target_pairs={{0,1},{1,0},{2,3},{3,2},{4,5},{5,4},{6,7},{7,6},{8,9},{9,8},{10,11... | collective-permute-start | bytes 6291464 | tf_op jit(solution)/shard_map/ppermute | solution.py:136
  400.0 64.0 %collective-permute-start.35 = (bf16[512,2048]{1,0:T(8,128)(2,1)}, bf16[512,2048]{1,0:T(8,128)(2,1)}, u32[]{:S(2)}, u32[]{:S(2)}) collective-permute-start(bf16[512,2048]{1,0:T(8,128)(2,1)} %get-tuple-element.341), channel_id=1, source_target_pairs={{0,1},{1,0},{2,3},{3,2},{4,5},{5,4},{6,7},{7,6},{8,9},{9,8},{10,11... | collective-permute-start | bytes 6291464 | tf_op jit(solution)/shard_map/ppermute | solution.py:136
  420.1 43.9 %collective-permute-start.43 = (bf16[2,128,2560]{2,1,0:T(8,128)(2,1)S(1)}, bf16[2,128,2560]{2,1,0:T(8,128)(2,1)S(1)}, u32[]{:S(2)}, u32[]{:S(2)}) collective-permute-start(bf16[2,128,2560]{2,1,0:T(8,128)(2,1)S(1)} %get-tuple-element.347), channel_id=1, source_target_pairs={{0,6},{2,0},{4,2},{6,4},{1,7},{3,1},{5,3},{7,5},{8,14},{10,8},{12,... | collective-permute-start | bytes 3932168 | tf_op jit(solution)/shard_map/ppermute | solution.py:64
  422.3 83.5 %collective-permute-start.47 = (bf16[2,512,1536]{2,1,0:T(8,128)(2,1)}, bf16[2,512,1536]{2,1,0:T(8,128)(2,1)}, u32[]{:S(2)}, u32[]{:S(2)}) collective-permute-start(bf16[2,512,1536]{2,1,0:T(8,128)(2,1)} %shard_map.216), channel_id=1, source_target_pairs={{0,16},{8,24},{16,0},{24,8},{1,17},{9,25},{17,1},{25,9},{2,18},{10... | collective-permute-start | bytes 9437192 | tf_op jit(solution)/shard_map/ppermute | solution.py:67
  439.3 72.8 %collective-permute-start.39 = (bf16[512,2048]{1,0:T(8,128)(2,1)}, bf16[512,2048]{1,0:T(8,128)(2,1)}, u32[]{:S(2)}, u32[]{:S(2)}) collective-permute-start(bf16[512,2048]{1,0:T(8,128)(2,1)} %shard_map.221.refs_0_), channel_id=1, source_target_pairs={{0,1},{1,0},{2,3},{3,2},{4,5},{5,4},{6,7},{7,6},{8,9},{9,8},{10,11... | collective-permute-start | bytes 6291464 | tf_op jit(solution)/shard_map/ppermute | solution.py:136
  440.7 32.3 %collective-permute-start.40 = (bf16[512,256]{1,0:T(8,128)(2,1)}, bf16[512,256]{1,0:T(8,128)(2,1)}, u32[]{:S(2)}, u32[]{:S(2)}) collective-permute-start(bf16[512,256]{1,0:T(8,128)(2,1)} %get-tuple-element.421), channel_id=1, source_target_pairs={{0,6},{2,0},{4,2},{6,4},{1,7},{3,1},{5,3},{7,5},{8,14},{10,8},{12,... | collective-permute-start | bytes 786440 | tf_op jit(solution)/shard_map/ppermute | solution.py:64
  491.3 81.5 %collective-permute-start.51 = (bf16[2,128,2560]{2,1,0:T(8,128)(2,1)}, bf16[2,128,2560]{2,1,0:T(8,128)(2,1)}, u32[]{:S(2)}, u32[]{:S(2)}) collective-permute-start(bf16[2,128,2560]{2,1,0:T(8,128)(2,1)} %copy-done.47), channel_id=1, source_target_pairs={{0,2},{2,4},{4,6},{6,0},{1,3},{3,5},{5,7},{7,1},{8,10},{10,12},{12... | collective-permute-start | bytes 3932168 | tf_op jit(solution)/shard_map/ppermute | solution.py:64
  512.1 64.0 %collective-permute-start.50 = (bf16[2,128,2560]{2,1,0:T(8,128)(2,1)}, bf16[2,128,2560]{2,1,0:T(8,128)(2,1)}, u32[]{:S(2)}, u32[]{:S(2)}) collective-permute-start(bf16[2,128,2560]{2,1,0:T(8,128)(2,1)} %shard_map.222), channel_id=1, source_target_pairs={{0,6},{2,0},{4,2},{6,4},{1,7},{3,1},{5,3},{7,5},{8,14},{10,8},{12,... | collective-permute-start | bytes 3932168 | tf_op jit(solution)/shard_map/ppermute | solution.py:64
  513.0 56.3 %collective-permute-start.52 = (bf16[2,128,1536]{2,1,0:T(8,128)(2,1)}, bf16[2,128,1536]{2,1,0:T(8,128)(2,1)}, u32[]{:S(2)}, u32[]{:S(2)}) collective-permute-start(bf16[2,128,1536]{2,1,0:T(8,128)(2,1)} %get-tuple-element.385), channel_id=1, source_target_pairs={{0,6},{2,0},{4,2},{6,4},{1,7},{3,1},{5,3},{7,5},{8,14},{10,8},{12,... | collective-permute-start | bytes 2359304 | tf_op jit(solution)/shard_map/ppermute | solution.py:64
  515.8 63.2 %collective-permute-start.48 = (bf16[512,2304]{1,0:T(8,128)(2,1)}, bf16[512,2304]{1,0:T(8,128)(2,1)S(1)}, u32[]{:S(2)}, u32[]{:S(2)}) collective-permute-start(bf16[512,2304]{1,0:T(8,128)(2,1)} %shard_map.230), channel_id=1, source_target_pairs={{0,8},{8,0},{16,24},{24,16},{1,9},{9,1},{17,25},{25,17},{2,10},{10... | collective-permute-start | bytes 7077896 | tf_op jit(solution)/shard_map/ppermute | solution.py:70
  519.9 59.1 %collective-permute-start.49 = (bf16[1,512,2304]{2,1,0:T(8,128)(2,1)}, bf16[1,512,2304]{2,1,0:T(8,128)(2,1)}, u32[]{:S(2)}, u32[]{:S(2)}) collective-permute-start(bf16[1,512,2304]{2,1,0:T(8,128)(2,1)} %shard_map.227), channel_id=1, source_target_pairs={{0,16},{8,24},{16,0},{24,8},{1,17},{9,25},{17,1},{25,9},{2,18},{10... | collective-permute-start | bytes 7077896 | tf_op jit(solution)/shard_map/ppermute | solution.py:67
  572.8 35.7 %collective-permute-start.60 = (bf16[2,128,1536]{2,1,0:T(8,128)(2,1)}, bf16[2,128,1536]{2,1,0:T(8,128)(2,1)S(1)}, u32[]{:S(2)}, u32[]{:S(2)}) collective-permute-start(bf16[2,128,1536]{2,1,0:T(8,128)(2,1)} %shard_map.231), channel_id=1, source_target_pairs={{0,6},{2,0},{4,2},{6,4},{1,7},{3,1},{5,3},{7,5},{8,14},{10,8},{12,... | collective-permute-start | bytes 2359304 | tf_op jit(solution)/shard_map/ppermute | solution.py:64
  582.1 38.2 %collective-permute-start.53 = (bf16[1,128,2304]{2,1,0:T(8,128)(2,1)S(1)}, bf16[1,128,2304]{2,1,0:T(8,128)(2,1)S(1)}, u32[]{:S(2)}, u32[]{:S(2)}) collective-permute-start(bf16[1,128,2304]{2,1,0:T(8,128)(2,1)S(1)} %get-tuple-element.394), channel_id=1, source_target_pairs={{0,2},{2,4},{4,6},{6,0},{1,3},{3,5},{5,7},{7,1},{8,10},{10,12},{12... | collective-permute-start | bytes 1769480 | tf_op jit(solution)/shard_map/ppermute | solution.py:64
  (129 other events, 1238.2 us)
Sparse Core Ops, SparseCore 0:
  77.7 139.4 all-gather.4
  219.5 104.4 all-gather.2

commit v5 on v4

--- a/solution.py
+++ b/solution.py
@@ -843,7 +843,7 @@
 
     def ff_gather(k):
         cols = slice(starts[k], starts[k] + split[k])
-        shard = after(jnp.concatenate([w_up[:, cols], w_down[:, cols]], axis=1), tiles[1])
+        shard = after(jnp.concatenate([w_up[:, cols], w_down[:, cols]], axis=1), q_mine)
         return lax.all_gather(shard, both, axis=0, tiled=True)
 
     ff_w = [ff_gather(k) for k in range(len(split))]

time: 678 us -> 663 us (0.978)
  starting transfers between devices: 98.7 us -> 90.9 us
  local copies, waits for them, and re-layouts: 50.4 us -> 43.1 us
    all_gather x2, waiting for transfers between devices: 51 us -> 39.4 us  [ff_gather(): return lax.all_gather(shard, both, axis=0, tiled=True)]
    ppermute x27, waiting for transfers between devices: 132 us -> 143 us  [z(): lax.ppermute(value, 'ctx', [(i, (i + k) % self.nz) for i in range(self.nz)])]
    unnamed x158 -> x130, local copies, waits for them, and re-layouts: 44.1 us -> 34.1 us
  transfers between devices with their start and end apart: 70 -> 70, of which waited for: 28 -> 27; matrix products, arithmetic and copies ran while one was open for 4% -> 5% of each run, Pallas kernels for 29% -> 30%
where the time goes in v5:
time: 663 us; the launch traced here: 658 us
  waiting for transfers between devices  286 us (43%)
  Pallas kernels  198 us (30%)
  starting transfers between devices  90.9 us (14%)
  local copies, waits for them, and re-layouts  43.1 us (7%)
  other arithmetic  24.9 us (4%)
  between operations  15.6 us (2%)
    ppermute x27, waiting for transfers between devices, z(): lax.ppermute(value, 'ctx', [(i, (i + k) % self.nz) for i in range(self.nz)])  143 us
    pallas_call x3, Pallas kernels, call(): pl.pallas_call(kernel, grid=(self.n // self.tile,), in_specs=in_specs, ou...  83.3 us
    ppermute x6, waiting for transfers between devices, tp_others(): lax.ppermute(part, 'tp', [(i, (i + k) % n) for i in range(n)])  66 us
    ppermute x27, starting transfers between devices, z(): lax.ppermute(value, 'ctx', [(i, (i + k) % self.nz) for i in range(self.nz)])  59.6 us
    all_gather x2, waiting for transfers between devices, ff_gather(): return lax.all_gather(shard, both, axis=0, tiled=True)  39.4 us
    pallas_call x5, Pallas kernels, row_call(): pl.pallas_call(kernel, grid_spec=pltpu.PrefetchScalarGridSpec(num_scalar_...  38.2 us
    unnamed x130, local copies, waits for them, and re-layouts  34.1 us
    ppermute x16, waiting for transfers between devices, core(): return lax.ppermute(value, 'dp', [(i, i ^ 1) for i in range(self.ndp)])  20.7 us
  transfers between devices with their start and end apart: 70, of which 27 were waited for; matrix products, arithmetic and copies ran while one was open for 5% of the time, Pallas kernels for 30%

profile of v5, /device:TPU:0, one launch (start us, length us, event | category | flops | bytes accessed | tf_op | source)
XLA Modules:
  0.0 658.1 jit_solution(11775085322531731022)
XLA Ops:
  63.6 13.0 %collective-permute-done.16 = bf16[512,256]{1,0:T(8,128)(2,1)S(1)} collective-permute-done((bf16[512,256]{1,0:T(8,128)(2,1)S(1)}, bf16[512,256]{1,0:T(8,128)(2,1)S(1)}, u32[]{:S(2)}, u32[]{:S(2)}) %collective-permute-start.16) | collective-permute-done | bytes 262176 | tf_op jit(solution)/shard_map/ppermute | solution.py:64
  80.5 9.9 %collective-permute-done.19.refs_1_ = bf16[128,1024]{1,0:T(8,128)(2,1)S(1)} collective-permute-done((bf16[128,1024]{1,0:T(8,128)(2,1)S(1)}, bf16[128,1024]{1,0:T(8,128)(2,1)S(1)}, u32[]{:S(2)}, u32[]{:S(2)}) %collective-permute-start.19) | collective-permute-done | bytes 262176 | tf_op jit(solution)/shard_map/ppermute | solution.py:64
  95.2 7.8 %collective-permute-done.20.refs_3_ = bf16[128,1024]{1,0:T(8,128)(2,1)S(1)} collective-permute-done((bf16[128,1024]{1,0:T(8,128)(2,1)S(1)}, bf16[128,1024]{1,0:T(8,128)(2,1)S(1)}, u32[]{:S(2)}, u32[]{:S(2)}) %collective-permute-start.20) | collective-permute-done | bytes 262176 | tf_op jit(solution)/shard_map/ppermute | solution.py:64
  103.3 20.2 %collective-permute-done.21.refs_2_ = bf16[128,1024]{1,0:T(8,128)(2,1)S(1)} collective-permute-done((bf16[128,1024]{1,0:T(8,128)(2,1)S(1)}, bf16[128,1024]{1,0:T(8,128)(2,1)S(1)}, u32[]{:S(2)}, u32[]{:S(2)}) %collective-permute-start.21) | collective-permute-done | bytes 262176 | tf_op jit(solution)/shard_map/ppermute | solution.py:64
  123.6 6.9 %shard_map.208 = (f32[8,128,512]{2,1,0:T(8,128)S(1)}, bf16[512,1024]{1,0:T(8,128)(2,1)S(1)}, f32[8,1,512]{2,1,0:T(1,128)S(1)}) custom-call(s32[1]{0:T(128)} %bitcast.27.z_ref, bf16[512,1024]{1,0:T(8,128)(2,1)S(1)} %shard_map.207.q_ref, bf16[4,512,256]{2,1,0:T(8,128)(2,1)S(1)} %pad_maximum_fusion.4.kv_ref), custom_call_target="tpu_custom_call" | custom-call | flops 4600000000 | bytes 14000000 | tf_op jit(solution)/shard_map/pallas_call | solution.py:701
  144.9 46.2 %collective-permute-done.27.refs_1_ = bf16[512,2048]{1,0:T(8,128)(2,1)S(1)} collective-permute-done((bf16[512,2048]{1,0:T(8,128)(2,1)S(1)}, bf16[512,2048]{1,0:T(8,128)(2,1)S(1)}, u32[]{:S(2)}, u32[]{:S(2)}) %collective-permute-start.27) | collective-permute-done | bytes 2097184 | tf_op jit(solution)/shard_map/ppermute | solution.py:136
  192.4 9.2 %shard_map.211 = (bf16[512,2048]{1,0:T(8,128)(2,1)}, bf16[2048,512]{1,0:T(8,128)(2,1)}, f32[512,2048]{1,0:T(8,128)}, f32[512,1]{1,0:T(8,128)}, f32[512,1]{1,0:T(8,128)}, /*index=5*/f32[512,1]{1,0:T(8,128)}) custom-call(s32[16]{0:T(128)} %stack.143.order_ref, bf16[512,2048]{1,0:T(8,128)(2,1)} %tok_ref.2, bf16[512,2048]{1,0:T(8,128)(2,1)} %copy-done.46, ...), custom_call_target="tpu_custom_call" | custom-call | flops 4600000000 | bytes 14000000 | tf_op jit(solution)/shard_map/pallas_call | solution.py:156
  205.9 46.2 %shard_map.212 = (bf16[2,1024,2560]{2,1,0:T(8,128)(2,1)}, bf16[512,2560]{1,0:T(8,128)(2,1)}, bf16[512,2560]{1,0:T(8,128)(2,1)}, bf16[512,2560]{1,0:T(8,128)(2,1)...) custom-call(bf16[512,2048]{1,0:T(8,128)(2,1)} %get-tuple-element.284.nt, ...), custom_call_target="tpu_custom_call" | custom-call | flops 1000 | bytes 1000 | tf_op jit(solution)/shard_map/pallas_call | solution.py:423
  257.3 7.6 %collective-permute-done.29.refs_1_ = bf16[512,2560]{1,0:T(8,128)(2,1)S(1)} collective-permute-done((bf16[512,2560]{1,0:T(8,128)(2,1)}, bf16[512,2560]{1,0:T(8,128)(2,1)S(1)}, u32[]{:S(2)}, u32[]{:S(2)}) %collective-permute-start.29) | collective-permute-done | bytes 2621472 | tf_op jit(solution)/shard_map/ppermute | solution.py:70
  277.7 35.1 %all-gather.3.cloned.1.call-done.up.down = bf16[2048,3072]{1,0:T(8,128)(2,1)} async-done(((bf16[128,3072]{1,0:T(8,128)(2,1)}), bf16[2048,3072]{1,0:T(8,128)(2,1)}) %all-gather.3.cloned.1.call-update) | async-done | bytes 12582928 | tf_op jit(solution)/shard_map/all_gather | solution.py:847
  312.8 18.6 %shard_map.214 = (bf16[512,1536]{1,0:T(8,128)(2,1)}, bf16[512,1536]{1,0:T(8,128)(2,1)}, bf16[512,2048]{1,0:T(8,128)(2,1)}) custom-call(bf16[512,2048]{1,0:T(8,128)(2,1)} %get-tuple-element.284.nt, bf16[512,2048]{1,0:T(8,128)(2,1)} %go_ref, bf16[2048,3072]{1,0:T(8,128)(2,1)} %all-gather.3.cloned.1.call-done.up.down, ...), custom_call_target="tpu_custom_call" | custom-call | flops 1000 | bytes 1000 | tf_op jit(solution)/shard_map/pallas_call | solution.py:423
  332.9 18.5 %shard_map.215 = (bf16[2,1024,1536]{2,1,0:T(8,128)(2,1)}, bf16[512,1536]{1,0:T(8,128)(2,1)}, bf16[512,1536]{1,0:T(8,128)(2,1)}, bf16[512,1536]{1,0:T(8,128)(2,1)...) custom-call(bf16[512,1536]{1,0:T(8,128)(2,1)} %get-tuple-element.291.act, ...), custom_call_target="tpu_custom_call" | custom-call | flops 1000 | bytes 1000 | tf_op jit(solution)/shard_map/pallas_call | solution.py:423
  362.9 16.7 %collective-permute-done.32.refs_1_ = bf16[512,2048]{1,0:T(8,128)(2,1)} collective-permute-done((bf16[512,2048]{1,0:T(8,128)(2,1)}, bf16[512,2048]{1,0:T(8,128)(2,1)}, u32[]{:S(2)}, u32[]{:S(2)}) %collective-permute-start.32) | collective-permute-done | bytes 2097184 | tf_op jit(solution)/shard_map/ppermute | solution.py:136
  379.6 9.3 %shard_map.217 = (bf16[512,2048]{1,0:T(8,128)(2,1)}, f32[512,2048]{1,0:T(8,128)}, f32[2,2048]{1,0:T(2,128)}) custom-call(s32[16]{0:T(128)} %stack.143.order_ref, f32[512,2048]{1,0:T(8,128)} %get-tuple-element.340.hid_ref, bf16[512,2048]{1,0:T(8,128)(2,1)} %go_ref, f32[512,1]{1,0:T(8,128)} %get-tuple-element.309.mean_ref, ...), custom_call_target="tpu_custom_call" | custom-call | flops 1000 | bytes 1000 | tf_op jit(solution)/shard_map/pallas_call | solution.py:156
  412.1 8.4 %shard_map.220 = (bf16[512,1024]{1,0:T(8,128)(2,1)S(1)}, f32[4,512,256]{2,1,0:T(8,128)S(1)}) custom-call(s32[1]{0:T(128)} %bitcast.27.z_ref, bf16[512,1024]{1,0:T(8,128)(2,1)S(1)} %copy-done.43, bf16[4,512,256]{2,1,0:T(8,128)(2,1)S(1)} %copy-done.19, bf16[512,1024]{1,0:T(8,128)(2,1)S(1)} %shard_map.218.d_ref, f32[8,128,512]{2,1,0:T(8,128)S(1)} %copy-done.32, ...), custom_call_target="tpu_custom_call" | custom-call | flops 1000 | bytes 1000 | tf_op jit(solution)/shard_map/pallas_call | solution.py:774
  430.5 20.0 %collective-permute-start.40 = (bf16[512,256]{1,0:T(8,128)(2,1)}, bf16[512,256]{1,0:T(8,128)(2,1)}, u32[]{:S(2)}, u32[]{:S(2)}) collective-permute-start(bf16[512,256]{1,0:T(8,128)(2,1)} %get-tuple-element.421), channel_id=1, source_target_pairs={{0,6},{2,0},{4,2},{6,4},{1,7},{3,1},{5,3},{7,5},{8,14},{10,8},{12,... | collective-permute-start | bytes 786440 | tf_op jit(solution)/shard_map/ppermute | solution.py:64
  459.6 10.3 %collective-permute-done.41 = bf16[512,256]{1,0:T(8,128)(2,1)} collective-permute-done((bf16[512,256]{1,0:T(8,128)(2,1)}, bf16[512,256]{1,0:T(8,128)(2,1)}, u32[]{:S(2)}, u32[]{:S(2)}) %collective-permute-start.41) | collective-permute-done | bytes 262176 | tf_op jit(solution)/shard_map/ppermute | solution.py:64
  516.3 9.5 %shard_map.229 = (f32[512,2048]{1,0:T(8,128)}, f32[2,2048]{1,0:T(2,128)}) custom-call(s32[16]{0:T(128)} %stack.143.order_ref, bf16[512,2048]{1,0:T(8,128)(2,1)} %tok_ref.2, f32[512,2048]{1,0:T(8,128)} %get-tuple-element.372.gh_ref, f32[512,1]{1,0:T(8,128)} %get-tuple-element.373.mean_ref, f32[512,1]{1,0:T(8,128)} %get-tuple-element.374.rate_ref, ...), custom_call_target="tpu_custom_call" | custom-call | flops 1000 | bytes 1000 | tf_op jit(solution)/shard_map/pallas_call | solution.py:156
  525.8 29.5 %collective-permute-done.52.refs_1_ = bf16[2,128,1536]{2,1,0:T(8,128)(2,1)} collective-permute-done((bf16[2,128,1536]{2,1,0:T(8,128)(2,1)}, bf16[2,128,1536]{2,1,0:T(8,128)(2,1)}, u32[]{:S(2)}, u32[]{:S(2)}) %collective-permute-start.52) | collective-permute-done | bytes 786464 | tf_op jit(solution)/shard_map/ppermute | solution.py:64
  569.3 8.6 %collective-permute-done.61 = bf16[2,128,1536]{2,1,0:T(8,128)(2,1)} collective-permute-done((bf16[2,128,1536]{2,1,0:T(8,128)(2,1)}, bf16[2,128,1536]{2,1,0:T(8,128)(2,1)}, u32[]{:S(2)}, u32[]{:S(2)}) %collective-permute-start.61) | collective-permute-done | bytes 786464 | tf_op jit(solution)/shard_map/ppermute | solution.py:64
  577.9 16.7 %collective-permute-done.60 = bf16[2,128,1536]{2,1,0:T(8,128)(2,1)S(1)} collective-permute-done((bf16[2,128,1536]{2,1,0:T(8,128)(2,1)}, bf16[2,128,1536]{2,1,0:T(8,128)(2,1)S(1)}, u32[]{:S(2)}, u32[]{:S(2)}) %collective-permute-start.60) | collective-permute-done | bytes 786464 | tf_op jit(solution)/shard_map/ppermute | solution.py:64
  594.5 11.8 %collective-permute-done.53 = bf16[1,128,2304]{2,1,0:T(8,128)(2,1)S(1)} collective-permute-done((bf16[1,128,2304]{2,1,0:T(8,128)(2,1)S(1)}, bf16[1,128,2304]{2,1,0:T(8,128)(2,1)S(1)}, u32[]{:S(2)}, u32[]{:S(2)}) %collective-permute-start.53) | collective-permute-done | bytes 589856 | tf_op jit(solution)/shard_map/ppermute | solution.py:64
  616.7 9.0 %collective-permute-done.59.refs_1_ = bf16[1,128,2304]{2,1,0:T(8,128)(2,1)S(1)} collective-permute-done((bf16[1,128,2304]{2,1,0:T(8,128)(2,1)S(1)}, bf16[1,128,2304]{2,1,0:T(8,128)(2,1)S(1)}, u32[]{:S(2)}, u32[]{:S(2)}) %collective-permute-start.59) | collective-permute-done | bytes 589856 | tf_op jit(solution)/shard_map/ppermute | solution.py:64
  636.1 7.6 %collective-permute-done.67 = f32[3,128]{0,1:T(8,128)S(1)} collective-permute-done((f32[3,128]{0,1:T(8,128)S(1)}, f32[3,128]{0,1:T(8,128)S(1)}, u32[]{:S(2)}, u32[]{:S(2)}) %collective-permute-start.67) | collective-permute-done | bytes 1568 | tf_op jit(solution)/shard_map/ppermute | solution.py:114
  (346 shorter events, 246.1 us)
Async XLA Ops:
  7.2 198.7 %all-gather.5.cloned.1.call-start = ((), (), s32[]{:S(2)}) async-start(), calls=%async_computation.1 | async-start | bytes 22282240 | tf_op jit(solution)/shard_map/all_gather | solution.py:847
  59.2 253.6 %all-gather.3.cloned.1.call-start = ((), (), s32[]{:S(2)}) async-start(), calls=%async_computation | async-start | bytes 13369344 | tf_op jit(solution)/shard_map/all_gather | solution.py:847
  61.3 29.1 %collective-permute-start.15 = (bf16[1024,1024]{1,0:T(8,128)(2,1)}, bf16[1024,1024]{1,0:T(8,128)(2,1)S(1)}, u32[]{:S(2)}, u32[]{:S(2)}) collective-permute-start(bf16[1024,1024]{1,0:T(8,128)(2,1)} %copy-done.22), channel_id=1, source_target_pairs={{0,8},{8,0},{16,24},{24,16},{1,9},{9,1},{17,25},{25,17},{2,10},{10... | collective-permute-start | bytes 6291464 | tf_op jit(solution)/shard_map/ppermute | solution.py:70
  76.7 54.0 %collective-permute-start.22 = (bf16[128,1024]{1,0:T(8,128)(2,1)S(1)}, bf16[128,1024]{1,0:T(8,128)(2,1)S(1)}, u32[]{:S(2)}, u32[]{:S(2)}) collective-permute-start(bf16[128,1024]{1,0:T(8,128)(2,1)S(1)} %copy-done.50), channel_id=1, source_target_pairs={{0,16},{8,24},{16,0},{24,8},{1,17},{9,25},{17,1},{25,9},{2,18},{10... | collective-permute-start | bytes 786440 | tf_op jit(solution)/shard_map/ppermute | solution.py:67
  90.4 33.1 %collective-permute-start.17 = (bf16[512,256]{1,0:T(8,128)(2,1)S(1)}, bf16[512,256]{1,0:T(8,128)(2,1)S(1)}, u32[]{:S(2)}, u32[]{:S(2)}) collective-permute-start(bf16[512,256]{1,0:T(8,128)(2,1)S(1)} %collective-permute-done.16), channel_id=1, source_target_pairs={{0,2},{2,4},{4,6},{6,0},{1,3},{3,5},{5,7},{7,1},{8,10},{10,12},{12... | collective-permute-start | bytes 786440 | tf_op jit(solution)/shard_map/ppermute | solution.py:64
  90.4 33.1 %collective-permute-start.21 = (bf16[128,1024]{1,0:T(8,128)(2,1)S(1)}, bf16[128,1024]{1,0:T(8,128)(2,1)S(1)}, u32[]{:S(2)}, u32[]{:S(2)}) collective-permute-start(bf16[128,1024]{1,0:T(8,128)(2,1)S(1)} %collective-permute-done.19.refs_1_), channel_id=1, source_target_pairs={{0,2},{2,4},{4,6},{6,0},{1,3},{3,5},{5,7},{7,1},{8,10},{10,12},{12... | collective-permute-start | bytes 786440 | tf_op jit(solution)/shard_map/ppermute | solution.py:64
  94.6 36.1 %collective-permute-start.23 = (bf16[128,1024]{1,0:T(8,128)(2,1)S(1)}, bf16[128,1024]{1,0:T(8,128)(2,1)S(1)}, u32[]{:S(2)}, u32[]{:S(2)}) collective-permute-start(bf16[128,1024]{1,0:T(8,128)(2,1)S(1)} %collective-permute-done.19.refs_1_), channel_id=1, source_target_pairs={{0,16},{8,24},{16,0},{24,8},{1,17},{9,25},{17,1},{25,9},{2,18},{10... | collective-permute-start | bytes 786440 | tf_op jit(solution)/shard_map/ppermute | solution.py:67
  143.2 47.9 %collective-permute-start.27 = (bf16[512,2048]{1,0:T(8,128)(2,1)S(1)}, bf16[512,2048]{1,0:T(8,128)(2,1)S(1)}, u32[]{:S(2)}, u32[]{:S(2)}) collective-permute-start(bf16[512,2048]{1,0:T(8,128)(2,1)S(1)} %shard_map.210.refs_0_), channel_id=1, source_target_pairs={{0,1},{1,0},{2,3},{3,2},{4,5},{5,4},{6,7},{7,6},{8,9},{9,8},{10,11... | collective-permute-start | bytes 6291464 | tf_op jit(solution)/shard_map/ppermute | solution.py:136
  252.6 60.2 %collective-permute-start.30 = (bf16[512,2560]{1,0:T(8,128)(2,1)}, bf16[512,2560]{1,0:T(8,128)(2,1)}, u32[]{:S(2)}, u32[]{:S(2)}) collective-permute-start(bf16[512,2560]{1,0:T(8,128)(2,1)} %get-tuple-element.282), channel_id=1, source_target_pairs={{0,8},{8,0},{16,24},{24,16},{1,9},{9,1},{17,25},{25,17},{2,10},{10... | collective-permute-start | bytes 7864328 | tf_op jit(solution)/shard_map/ppermute | solution.py:70
  252.7 60.1 %collective-permute-start.31 = (bf16[512,2560]{1,0:T(8,128)(2,1)}, bf16[512,2560]{1,0:T(8,128)(2,1)}, u32[]{:S(2)}, u32[]{:S(2)}) collective-permute-start(bf16[512,2560]{1,0:T(8,128)(2,1)} %get-tuple-element.283), channel_id=1, source_target_pairs={{0,8},{8,0},{16,24},{24,16},{1,9},{9,1},{17,25},{25,17},{2,10},{10... | collective-permute-start | bytes 7864328 | tf_op jit(solution)/shard_map/ppermute | solution.py:70
  272.3 126.8 %collective-permute-start.36 = (bf16[2,512,2560]{2,1,0:T(8,128)(2,1)}, bf16[2,512,2560]{2,1,0:T(8,128)(2,1)}, u32[]{:S(2)}, u32[]{:S(2)}) collective-permute-start(bf16[2,512,2560]{2,1,0:T(8,128)(2,1)} %shard_map.213), channel_id=1, source_target_pairs={{0,16},{8,24},{16,0},{24,8},{1,17},{9,25},{17,1},{25,9},{2,18},{10... | collective-permute-start | bytes 15728648 | tf_op jit(solution)/shard_map/ppermute | solution.py:67
  331.4 48.2 %collective-permute-start.32 = (bf16[512,2048]{1,0:T(8,128)(2,1)}, bf16[512,2048]{1,0:T(8,128)(2,1)}, u32[]{:S(2)}, u32[]{:S(2)}) collective-permute-start(bf16[512,2048]{1,0:T(8,128)(2,1)} %get-tuple-element.312.refs_0_), channel_id=1, source_target_pairs={{0,1},{1,0},{2,3},{3,2},{4,5},{5,4},{6,7},{7,6},{8,9},{9,8},{10,11... | collective-permute-start | bytes 6291464 | tf_op jit(solution)/shard_map/ppermute | solution.py:136
  388.8 61.6 %collective-permute-start.35 = (bf16[512,2048]{1,0:T(8,128)(2,1)}, bf16[512,2048]{1,0:T(8,128)(2,1)}, u32[]{:S(2)}, u32[]{:S(2)}) collective-permute-start(bf16[512,2048]{1,0:T(8,128)(2,1)} %get-tuple-element.341), channel_id=1, source_target_pairs={{0,1},{1,0},{2,3},{3,2},{4,5},{5,4},{6,7},{7,6},{8,9},{9,8},{10,11... | collective-permute-start | bytes 6291464 | tf_op jit(solution)/shard_map/ppermute | solution.py:136
  409.4 41.1 %collective-permute-start.43 = (bf16[2,128,2560]{2,1,0:T(8,128)(2,1)S(1)}, bf16[2,128,2560]{2,1,0:T(8,128)(2,1)S(1)}, u32[]{:S(2)}, u32[]{:S(2)}) collective-permute-start(bf16[2,128,2560]{2,1,0:T(8,128)(2,1)S(1)} %get-tuple-element.347), channel_id=1, source_target_pairs={{0,6},{2,0},{4,2},{6,4},{1,7},{3,1},{5,3},{7,5},{8,14},{10,8},{12,... | collective-permute-start | bytes 3932168 | tf_op jit(solution)/shard_map/ppermute | solution.py:64
  411.6 80.1 %collective-permute-start.47 = (bf16[2,512,1536]{2,1,0:T(8,128)(2,1)}, bf16[2,512,1536]{2,1,0:T(8,128)(2,1)}, u32[]{:S(2)}, u32[]{:S(2)}) collective-permute-start(bf16[2,512,1536]{2,1,0:T(8,128)(2,1)} %shard_map.216), channel_id=1, source_target_pairs={{0,16},{8,24},{16,0},{24,8},{1,17},{9,25},{17,1},{25,9},{2,18},{10... | collective-permute-start | bytes 9437192 | tf_op jit(solution)/shard_map/ppermute | solution.py:67
  429.0 68.6 %collective-permute-start.39 = (bf16[512,2048]{1,0:T(8,128)(2,1)}, bf16[512,2048]{1,0:T(8,128)(2,1)}, u32[]{:S(2)}, u32[]{:S(2)}) collective-permute-start(bf16[512,2048]{1,0:T(8,128)(2,1)} %shard_map.221.refs_0_), channel_id=1, source_target_pairs={{0,1},{1,0},{2,3},{3,2},{4,5},{5,4},{6,7},{7,6},{8,9},{9,8},{10,11... | collective-permute-start | bytes 6291464 | tf_op jit(solution)/shard_map/ppermute | solution.py:136
  430.5 29.1 %collective-permute-start.40 = (bf16[512,256]{1,0:T(8,128)(2,1)}, bf16[512,256]{1,0:T(8,128)(2,1)}, u32[]{:S(2)}, u32[]{:S(2)}) collective-permute-start(bf16[512,256]{1,0:T(8,128)(2,1)} %get-tuple-element.421), channel_id=1, source_target_pairs={{0,6},{2,0},{4,2},{6,4},{1,7},{3,1},{5,3},{7,5},{8,14},{10,8},{12,... | collective-permute-start | bytes 786440 | tf_op jit(solution)/shard_map/ppermute | solution.py:64
  477.3 81.5 %collective-permute-start.51 = (bf16[2,128,2560]{2,1,0:T(8,128)(2,1)}, bf16[2,128,2560]{2,1,0:T(8,128)(2,1)}, u32[]{:S(2)}, u32[]{:S(2)}) collective-permute-start(bf16[2,128,2560]{2,1,0:T(8,128)(2,1)} %copy-done.47), channel_id=1, source_target_pairs={{0,2},{2,4},{4,6},{6,0},{1,3},{3,5},{5,7},{7,1},{8,10},{10,12},{12... | collective-permute-start | bytes 3932168 | tf_op jit(solution)/shard_map/ppermute | solution.py:64
  497.6 64.5 %collective-permute-start.50 = (bf16[2,128,2560]{2,1,0:T(8,128)(2,1)}, bf16[2,128,2560]{2,1,0:T(8,128)(2,1)}, u32[]{:S(2)}, u32[]{:S(2)}) collective-permute-start(bf16[2,128,2560]{2,1,0:T(8,128)(2,1)} %shard_map.222), channel_id=1, source_target_pairs={{0,6},{2,0},{4,2},{6,4},{1,7},{3,1},{5,3},{7,5},{8,14},{10,8},{12,... | collective-permute-start | bytes 3932168 | tf_op jit(solution)/shard_map/ppermute | solution.py:64
  498.4 56.9 %collective-permute-start.52 = (bf16[2,128,1536]{2,1,0:T(8,128)(2,1)}, bf16[2,128,1536]{2,1,0:T(8,128)(2,1)}, u32[]{:S(2)}, u32[]{:S(2)}) collective-permute-start(bf16[2,128,1536]{2,1,0:T(8,128)(2,1)} %get-tuple-element.385), channel_id=1, source_target_pairs={{0,6},{2,0},{4,2},{6,4},{1,7},{3,1},{5,3},{7,5},{8,14},{10,8},{12,... | collective-permute-start | bytes 2359304 | tf_op jit(solution)/shard_map/ppermute | solution.py:64
  501.3 63.8 %collective-permute-start.48 = (bf16[512,2304]{1,0:T(8,128)(2,1)}, bf16[512,2304]{1,0:T(8,128)(2,1)S(1)}, u32[]{:S(2)}, u32[]{:S(2)}) collective-permute-start(bf16[512,2304]{1,0:T(8,128)(2,1)} %shard_map.230), channel_id=1, source_target_pairs={{0,8},{8,0},{16,24},{24,16},{1,9},{9,1},{17,25},{25,17},{2,10},{10... | collective-permute-start | bytes 7077896 | tf_op jit(solution)/shard_map/ppermute | solution.py:70
  505.4 59.7 %collective-permute-start.49 = (bf16[1,512,2304]{2,1,0:T(8,128)(2,1)}, bf16[1,512,2304]{2,1,0:T(8,128)(2,1)}, u32[]{:S(2)}, u32[]{:S(2)}) collective-permute-start(bf16[1,512,2304]{2,1,0:T(8,128)(2,1)} %shard_map.227), channel_id=1, source_target_pairs={{0,16},{8,24},{16,0},{24,8},{1,17},{9,25},{17,1},{25,9},{2,18},{10... | collective-permute-start | bytes 7077896 | tf_op jit(solution)/shard_map/ppermute | solution.py:67
  558.8 35.7 %collective-permute-start.60 = (bf16[2,128,1536]{2,1,0:T(8,128)(2,1)}, bf16[2,128,1536]{2,1,0:T(8,128)(2,1)S(1)}, u32[]{:S(2)}, u32[]{:S(2)}) collective-permute-start(bf16[2,128,1536]{2,1,0:T(8,128)(2,1)} %shard_map.231), channel_id=1, source_target_pairs={{0,6},{2,0},{4,2},{6,4},{1,7},{3,1},{5,3},{7,5},{8,14},{10,8},{12,... | collective-permute-start | bytes 2359304 | tf_op jit(solution)/shard_map/ppermute | solution.py:64
  568.2 38.2 %collective-permute-start.53 = (bf16[1,128,2304]{2,1,0:T(8,128)(2,1)S(1)}, bf16[1,128,2304]{2,1,0:T(8,128)(2,1)S(1)}, u32[]{:S(2)}, u32[]{:S(2)}) collective-permute-start(bf16[1,128,2304]{2,1,0:T(8,128)(2,1)S(1)} %get-tuple-element.394), channel_id=1, source_target_pairs={{0,2},{2,4},{4,6},{6,0},{1,3},{3,5},{5,7},{7,1},{8,10},{10,12},{12... | collective-permute-start | bytes 1769480 | tf_op jit(solution)/shard_map/ppermute | solution.py:64
  (115 other events, 1233.3 us)
Sparse Core Ops, SparseCore 0:
  59.4 146.4 all-gather.4
  208.2 104.5 all-gather.2

commit v6 on v5

--- a/solution.py
+++ b/solution.py
@@ -843,7 +843,7 @@
 
     def ff_gather(k):
         cols = slice(starts[k], starts[k] + split[k])
-        shard = after(jnp.concatenate([w_up[:, cols], w_down[:, cols]], axis=1), q_mine)
+        shard = after(jnp.concatenate([w_up[:, cols], w_down[:, cols]], axis=1), kv_mine)
         return lax.all_gather(shard, both, axis=0, tiled=True)
 
     ff_w = [ff_gather(k) for k in range(len(split))]

time: 663 us -> 675 us (1.018)
  starting transfers between devices: 90.9 us -> 99.4 us
    all_gather x2, waiting for transfers between devices: 39.4 us -> 12.9 us  [ff_gather(): return lax.all_gather(shard, both, axis=0, tiled=True)]
    ppermute x16, waiting for transfers between devices: 7.49 us -> 29.2 us  [x(): lax.ppermute(value, 'dp', [(i, (i + 2 * k) % self.ndp) for i in range(sel...]
    ppermute x27, starting transfers between devices: 59.6 us -> 73.4 us  [z(): lax.ppermute(value, 'ctx', [(i, (i + k) % self.nz) for i in range(self.nz)])]
    unnamed x130 -> x150, local copies, waits for them, and re-layouts: 34.1 us -> 41.7 us
  transfers between devices with their start and end apart: 70 -> 70, of which waited for: 27 -> 29; matrix products, arithmetic and copies ran while one was open for 5% -> 4% of each run, Pallas kernels for 30% -> 29%
where the time goes in v6:
time: 675 us; the launch traced here: 670 us
  waiting for transfers between devices  284 us (42%)
  Pallas kernels  197 us (29%)
  starting transfers between devices  99.4 us (15%)
  local copies, waits for them, and re-layouts  48.8 us (7%)
  other arithmetic  25 us (4%)
  between operations  15.6 us (2%)
    ppermute x27, waiting for transfers between devices, z(): lax.ppermute(value, 'ctx', [(i, (i + k) % self.nz) for i in range(self.nz)])  144 us
    pallas_call x3, Pallas kernels, call(): pl.pallas_call(kernel, grid=(self.n // self.tile,), in_specs=in_specs, ou...  82.5 us
    ppermute x27, starting transfers between devices, z(): lax.ppermute(value, 'ctx', [(i, (i + k) % self.nz) for i in range(self.nz)])  73.4 us
    ppermute x6, waiting for transfers between devices, tp_others(): lax.ppermute(part, 'tp', [(i, (i + k) % n) for i in range(n)])  66.2 us
    unnamed x150, local copies, waits for them, and re-layouts  41.7 us
    pallas_call x5, Pallas kernels, row_call(): pl.pallas_call(kernel, grid_spec=pltpu.PrefetchScalarGridSpec(num_scalar_...  38.3 us
    ppermute x16, waiting for transfers between devices, x(): lax.ppermute(value, 'dp', [(i, (i + 2 * k) % self.ndp) for i in range(sel...  29.2 us
    ppermute x16, waiting for transfers between devices, core(): return lax.ppermute(value, 'dp', [(i, i ^ 1) for i in range(self.ndp)])  20.8 us
  transfers between devices with their start and end apart: 70, of which 29 were waited for; matrix products, arithmetic and copies ran while one was open for 4% of the time, Pallas kernels for 29%

profile of v6, /device:TPU:0, one launch (start us, length us, event | category | flops | bytes accessed | tf_op | source)
XLA Modules:
  0.0 669.8 jit_solution(5424562799441918670)
XLA Ops:
  79.1 12.8 %collective-permute-done.16 = bf16[512,256]{1,0:T(8,128)(2,1)S(1)} collective-permute-done((bf16[512,256]{1,0:T(8,128)(2,1)S(1)}, bf16[512,256]{1,0:T(8,128)(2,1)S(1)}, u32[]{:S(2)}, u32[]{:S(2)}) %collective-permute-start.16) | collective-permute-done | bytes 262176 | tf_op jit(solution)/shard_map/ppermute | solution.py:64
  96.5 9.1 %collective-permute-done.19.refs_1_ = bf16[128,1024]{1,0:T(8,128)(2,1)S(1)} collective-permute-done((bf16[128,1024]{1,0:T(8,128)(2,1)S(1)}, bf16[128,1024]{1,0:T(8,128)(2,1)S(1)}, u32[]{:S(2)}, u32[]{:S(2)}) %collective-permute-start.19) | collective-permute-done | bytes 262176 | tf_op jit(solution)/shard_map/ppermute | solution.py:64
  110.6 7.6 %collective-permute-done.20.refs_3_ = bf16[128,1024]{1,0:T(8,128)(2,1)S(1)} collective-permute-done((bf16[128,1024]{1,0:T(8,128)(2,1)S(1)}, bf16[128,1024]{1,0:T(8,128)(2,1)S(1)}, u32[]{:S(2)}, u32[]{:S(2)}) %collective-permute-start.20) | collective-permute-done | bytes 262176 | tf_op jit(solution)/shard_map/ppermute | solution.py:64
  119.0 18.9 %collective-permute-done.21.refs_2_ = bf16[128,1024]{1,0:T(8,128)(2,1)S(1)} collective-permute-done((bf16[128,1024]{1,0:T(8,128)(2,1)S(1)}, bf16[128,1024]{1,0:T(8,128)(2,1)S(1)}, u32[]{:S(2)}, u32[]{:S(2)}) %collective-permute-start.21) | collective-permute-done | bytes 262176 | tf_op jit(solution)/shard_map/ppermute | solution.py:64
  158.5 46.2 %collective-permute-done.27.refs_1_ = bf16[512,2048]{1,0:T(8,128)(2,1)S(1)} collective-permute-done((bf16[512,2048]{1,0:T(8,128)(2,1)S(1)}, bf16[512,2048]{1,0:T(8,128)(2,1)S(1)}, u32[]{:S(2)}, u32[]{:S(2)}) %collective-permute-start.27) | collective-permute-done | bytes 2097184 | tf_op jit(solution)/shard_map/ppermute | solution.py:136
  206.0 9.1 %shard_map.211 = (bf16[512,2048]{1,0:T(8,128)(2,1)}, bf16[2048,512]{1,0:T(8,128)(2,1)}, f32[512,2048]{1,0:T(8,128)}, f32[512,1]{1,0:T(8,128)}, f32[512,1]{1,0:T(8,128)}, /*index=5*/f32[512,1]{1,0:T(8,128)}) custom-call(s32[16]{0:T(128)} %stack.143.order_ref, bf16[512,2048]{1,0:T(8,128)(2,1)} %tok_ref.2, bf16[512,2048]{1,0:T(8,128)(2,1)} %copy-done.45, ...), custom_call_target="tpu_custom_call" | custom-call | flops 4600000000 | bytes 14000000 | tf_op jit(solution)/shard_map/pallas_call | solution.py:156
  215.1 45.4 %shard_map.212 = (bf16[2,1024,2560]{2,1,0:T(8,128)(2,1)}, bf16[512,2560]{1,0:T(8,128)(2,1)}, bf16[512,2560]{1,0:T(8,128)(2,1)}, bf16[512,2560]{1,0:T(8,128)(2,1)...) custom-call(bf16[512,2048]{1,0:T(8,128)(2,1)} %get-tuple-element.284.nt, ...), custom_call_target="tpu_custom_call" | custom-call | flops 1000 | bytes 1000 | tf_op jit(solution)/shard_map/pallas_call | solution.py:423
  265.7 7.8 %collective-permute-done.29.refs_1_ = bf16[512,2560]{1,0:T(8,128)(2,1)S(1)} collective-permute-done((bf16[512,2560]{1,0:T(8,128)(2,1)}, bf16[512,2560]{1,0:T(8,128)(2,1)S(1)}, u32[]{:S(2)}, u32[]{:S(2)}) %collective-permute-start.29) | collective-permute-done | bytes 2621472 | tf_op jit(solution)/shard_map/ppermute | solution.py:70
  281.8 12.8 %all-gather.3.cloned.1.call-done.up.down = bf16[2048,3072]{1,0:T(8,128)(2,1)} async-done(((bf16[128,3072]{1,0:T(8,128)(2,1)}), bf16[2048,3072]{1,0:T(8,128)(2,1)}) %all-gather.3.cloned.1.call-update) | async-done | bytes 12582928 | tf_op jit(solution)/shard_map/all_gather | solution.py:847
  294.6 18.6 %shard_map.214 = (bf16[512,1536]{1,0:T(8,128)(2,1)}, bf16[512,1536]{1,0:T(8,128)(2,1)}, bf16[512,2048]{1,0:T(8,128)(2,1)}) custom-call(bf16[512,2048]{1,0:T(8,128)(2,1)} %get-tuple-element.284.nt, bf16[512,2048]{1,0:T(8,128)(2,1)} %go_ref, bf16[2048,3072]{1,0:T(8,128)(2,1)} %all-gather.3.cloned.1.call-done.up.down, ...), custom_call_target="tpu_custom_call" | custom-call | flops 1000 | bytes 1000 | tf_op jit(solution)/shard_map/pallas_call | solution.py:423
  314.7 18.6 %shard_map.215 = (bf16[2,1024,1536]{2,1,0:T(8,128)(2,1)}, bf16[512,1536]{1,0:T(8,128)(2,1)}, bf16[512,1536]{1,0:T(8,128)(2,1)}, bf16[512,1536]{1,0:T(8,128)(2,1)...) custom-call(bf16[512,1536]{1,0:T(8,128)(2,1)} %get-tuple-element.291.act, ...), custom_call_target="tpu_custom_call" | custom-call | flops 1000 | bytes 1000 | tf_op jit(solution)/shard_map/pallas_call | solution.py:423
  344.7 16.7 %collective-permute-done.32.refs_1_ = bf16[512,2048]{1,0:T(8,128)(2,1)} collective-permute-done((bf16[512,2048]{1,0:T(8,128)(2,1)}, bf16[512,2048]{1,0:T(8,128)(2,1)}, u32[]{:S(2)}, u32[]{:S(2)}) %collective-permute-start.32) | collective-permute-done | bytes 2097184 | tf_op jit(solution)/shard_map/ppermute | solution.py:136
  361.3 9.3 %shard_map.217 = (bf16[512,2048]{1,0:T(8,128)(2,1)}, f32[512,2048]{1,0:T(8,128)}, f32[2,2048]{1,0:T(2,128)}) custom-call(s32[16]{0:T(128)} %stack.143.order_ref, f32[512,2048]{1,0:T(8,128)} %get-tuple-element.340.hid_ref, bf16[512,2048]{1,0:T(8,128)(2,1)} %go_ref, f32[512,1]{1,0:T(8,128)} %get-tuple-element.309.mean_ref, ...), custom_call_target="tpu_custom_call" | custom-call | flops 1000 | bytes 1000 | tf_op jit(solution)/shard_map/pallas_call | solution.py:156
  381.0 15.4 %collective-permute-done.36.refs_12_.refs_13_.refs_14_.refs_15_ = bf16[2,512,2560]{2,1,0:T(8,128)(2,1)} collective-permute-done((bf16[2,512,2560]{2,1,0:T(8,128)(2,1)}, bf16[2,512,2560]{2,1,0:T(8,128)(2,1)}, u32[]{:S(2)}, u32[]{:S(2)}) %collective-permute-start.36) | collective-permute-done | bytes 5242912 | tf_op jit(solution)/shard_map/ppermute | solution.py:67
  406.6 17.2 %collective-permute-start.43 = (bf16[2,128,2560]{2,1,0:T(8,128)(2,1)S(1)}, bf16[2,128,2560]{2,1,0:T(8,128)(2,1)S(1)}, u32[]{:S(2)}, u32[]{:S(2)}) collective-permute-start(bf16[2,128,2560]{2,1,0:T(8,128)(2,1)S(1)} %get-tuple-element.347), channel_id=1, source_target_pairs={{0,6},{2,0},{4,2},{6,4},{1,7},{3,1},{5,3},{7,5},{8,14},{10,8},{12,... | collective-permute-start | bytes 3932168 | tf_op jit(solution)/shard_map/ppermute | solution.py:64
  425.6 8.4 %shard_map.220 = (bf16[512,1024]{1,0:T(8,128)(2,1)S(1)}, f32[4,512,256]{2,1,0:T(8,128)S(1)}) custom-call(s32[1]{0:T(128)} %bitcast.27.z_ref, bf16[512,1024]{1,0:T(8,128)(2,1)S(1)} %copy-done.42, bf16[4,512,256]{2,1,0:T(8,128)(2,1)S(1)} %copy-done.19, bf16[512,1024]{1,0:T(8,128)(2,1)S(1)} %shard_map.218.d_ref, f32[8,128,512]{2,1,0:T(8,128)S(1)} %copy-done.31, ...), custom_call_target="tpu_custom_call" | custom-call | flops 1000 | bytes 1000 | tf_op jit(solution)/shard_map/pallas_call | solution.py:774
  444.0 19.5 %collective-permute-start.40 = (bf16[512,256]{1,0:T(8,128)(2,1)}, bf16[512,256]{1,0:T(8,128)(2,1)}, u32[]{:S(2)}, u32[]{:S(2)}) collective-permute-start(bf16[512,256]{1,0:T(8,128)(2,1)} %get-tuple-element.421), channel_id=1, source_target_pairs={{0,6},{2,0},{4,2},{6,4},{1,7},{3,1},{5,3},{7,5},{8,14},{10,8},{12,... | collective-permute-start | bytes 786440 | tf_op jit(solution)/shard_map/ppermute | solution.py:64
  472.6 10.0 %collective-permute-done.41 = bf16[512,256]{1,0:T(8,128)(2,1)} collective-permute-done((bf16[512,256]{1,0:T(8,128)(2,1)}, bf16[512,256]{1,0:T(8,128)(2,1)}, u32[]{:S(2)}, u32[]{:S(2)}) %collective-permute-start.41) | collective-permute-done | bytes 262176 | tf_op jit(solution)/shard_map/ppermute | solution.py:64
  528.1 9.6 %shard_map.229 = (f32[512,2048]{1,0:T(8,128)}, f32[2,2048]{1,0:T(2,128)}) custom-call(s32[16]{0:T(128)} %stack.143.order_ref, bf16[512,2048]{1,0:T(8,128)(2,1)} %tok_ref.2, f32[512,2048]{1,0:T(8,128)} %get-tuple-element.372.gh_ref, f32[512,1]{1,0:T(8,128)} %get-tuple-element.373.mean_ref, f32[512,1]{1,0:T(8,128)} %get-tuple-element.374.rate_ref, ...), custom_call_target="tpu_custom_call" | custom-call | flops 1000 | bytes 1000 | tf_op jit(solution)/shard_map/pallas_call | solution.py:156
  537.7 30.4 %collective-permute-done.52.refs_1_ = bf16[2,128,1536]{2,1,0:T(8,128)(2,1)} collective-permute-done((bf16[2,128,1536]{2,1,0:T(8,128)(2,1)}, bf16[2,128,1536]{2,1,0:T(8,128)(2,1)}, u32[]{:S(2)}, u32[]{:S(2)}) %collective-permute-start.52) | collective-permute-done | bytes 786464 | tf_op jit(solution)/shard_map/ppermute | solution.py:64
  582.1 8.5 %collective-permute-done.61 = bf16[2,128,1536]{2,1,0:T(8,128)(2,1)} collective-permute-done((bf16[2,128,1536]{2,1,0:T(8,128)(2,1)}, bf16[2,128,1536]{2,1,0:T(8,128)(2,1)}, u32[]{:S(2)}, u32[]{:S(2)}) %collective-permute-start.61) | collective-permute-done | bytes 786464 | tf_op jit(solution)/shard_map/ppermute | solution.py:64
  590.6 16.7 %collective-permute-done.60 = bf16[2,128,1536]{2,1,0:T(8,128)(2,1)S(1)} collective-permute-done((bf16[2,128,1536]{2,1,0:T(8,128)(2,1)}, bf16[2,128,1536]{2,1,0:T(8,128)(2,1)S(1)}, u32[]{:S(2)}, u32[]{:S(2)}) %collective-permute-start.60) | collective-permute-done | bytes 786464 | tf_op jit(solution)/shard_map/ppermute | solution.py:64
  607.3 11.8 %collective-permute-done.53 = bf16[1,128,2304]{2,1,0:T(8,128)(2,1)S(1)} collective-permute-done((bf16[1,128,2304]{2,1,0:T(8,128)(2,1)S(1)}, bf16[1,128,2304]{2,1,0:T(8,128)(2,1)S(1)}, u32[]{:S(2)}, u32[]{:S(2)}) %collective-permute-start.53) | collective-permute-done | bytes 589856 | tf_op jit(solution)/shard_map/ppermute | solution.py:64
  628.5 9.0 %collective-permute-done.59.refs_1_ = bf16[1,128,2304]{2,1,0:T(8,128)(2,1)S(1)} collective-permute-done((bf16[1,128,2304]{2,1,0:T(8,128)(2,1)S(1)}, bf16[1,128,2304]{2,1,0:T(8,128)(2,1)S(1)}, u32[]{:S(2)}, u32[]{:S(2)}) %collective-permute-start.59) | collective-permute-done | bytes 589856 | tf_op jit(solution)/shard_map/ppermute | solution.py:64
  (366 shorter events, 264.9 us)
Async XLA Ops:
  7.2 207.9 %all-gather.5.cloned.1.call-start = ((), (), s32[]{:S(2)}) async-start(), calls=%async_computation.1 | async-start | bytes 22282240 | tf_op jit(solution)/shard_map/all_gather | solution.py:847
  32.4 262.2 %all-gather.3.cloned.1.call-start = ((), (), s32[]{:S(2)}) async-start(), calls=%async_computation | async-start | bytes 13369344 | tf_op jit(solution)/shard_map/all_gather | solution.py:847
  91.9 54.0 %collective-permute-start.22 = (bf16[128,1024]{1,0:T(8,128)(2,1)S(1)}, bf16[128,1024]{1,0:T(8,128)(2,1)S(1)}, u32[]{:S(2)}, u32[]{:S(2)}) collective-permute-start(bf16[128,1024]{1,0:T(8,128)(2,1)S(1)} %copy-done.49), channel_id=1, source_target_pairs={{0,16},{8,24},{16,0},{24,8},{1,17},{9,25},{17,1},{25,9},{2,18},{10... | collective-permute-start | bytes 786440 | tf_op jit(solution)/shard_map/ppermute | solution.py:67
  105.6 33.1 %collective-permute-start.17 = (bf16[512,256]{1,0:T(8,128)(2,1)S(1)}, bf16[512,256]{1,0:T(8,128)(2,1)S(1)}, u32[]{:S(2)}, u32[]{:S(2)}) collective-permute-start(bf16[512,256]{1,0:T(8,128)(2,1)S(1)} %collective-permute-done.16), channel_id=1, source_target_pairs={{0,2},{2,4},{4,6},{6,0},{1,3},{3,5},{5,7},{7,1},{8,10},{10,12},{12... | collective-permute-start | bytes 786440 | tf_op jit(solution)/shard_map/ppermute | solution.py:64
  105.6 32.3 %collective-permute-start.21 = (bf16[128,1024]{1,0:T(8,128)(2,1)S(1)}, bf16[128,1024]{1,0:T(8,128)(2,1)S(1)}, u32[]{:S(2)}, u32[]{:S(2)}) collective-permute-start(bf16[128,1024]{1,0:T(8,128)(2,1)S(1)} %collective-permute-done.19.refs_1_), channel_id=1, source_target_pairs={{0,2},{2,4},{4,6},{6,0},{1,3},{3,5},{5,7},{7,1},{8,10},{10,12},{12... | collective-permute-start | bytes 786440 | tf_op jit(solution)/shard_map/ppermute | solution.py:64
  109.8 36.1 %collective-permute-start.23 = (bf16[128,1024]{1,0:T(8,128)(2,1)S(1)}, bf16[128,1024]{1,0:T(8,128)(2,1)S(1)}, u32[]{:S(2)}, u32[]{:S(2)}) collective-permute-start(bf16[128,1024]{1,0:T(8,128)(2,1)S(1)} %collective-permute-done.19.refs_1_), channel_id=1, source_target_pairs={{0,16},{8,24},{16,0},{24,8},{1,17},{9,25},{17,1},{25,9},{2,18},{10... | collective-permute-start | bytes 786440 | tf_op jit(solution)/shard_map/ppermute | solution.py:67
  157.0 47.7 %collective-permute-start.27 = (bf16[512,2048]{1,0:T(8,128)(2,1)S(1)}, bf16[512,2048]{1,0:T(8,128)(2,1)S(1)}, u32[]{:S(2)}, u32[]{:S(2)}) collective-permute-start(bf16[512,2048]{1,0:T(8,128)(2,1)S(1)} %shard_map.210.refs_0_), channel_id=1, source_target_pairs={{0,1},{1,0},{2,3},{3,2},{4,5},{5,4},{6,7},{7,6},{8,9},{9,8},{10,11... | collective-permute-start | bytes 6291464 | tf_op jit(solution)/shard_map/ppermute | solution.py:136
  261.0 33.6 %collective-permute-start.30 = (bf16[512,2560]{1,0:T(8,128)(2,1)}, bf16[512,2560]{1,0:T(8,128)(2,1)}, u32[]{:S(2)}, u32[]{:S(2)}) collective-permute-start(bf16[512,2560]{1,0:T(8,128)(2,1)} %get-tuple-element.282), channel_id=1, source_target_pairs={{0,8},{8,0},{16,24},{24,16},{1,9},{9,1},{17,25},{25,17},{2,10},{10... | collective-permute-start | bytes 7864328 | tf_op jit(solution)/shard_map/ppermute | solution.py:70
  261.1 33.5 %collective-permute-start.31 = (bf16[512,2560]{1,0:T(8,128)(2,1)}, bf16[512,2560]{1,0:T(8,128)(2,1)}, u32[]{:S(2)}, u32[]{:S(2)}) collective-permute-start(bf16[512,2560]{1,0:T(8,128)(2,1)} %get-tuple-element.283), channel_id=1, source_target_pairs={{0,8},{8,0},{16,24},{24,16},{1,9},{9,1},{17,25},{25,17},{2,10},{10... | collective-permute-start | bytes 7864328 | tf_op jit(solution)/shard_map/ppermute | solution.py:70
  281.0 115.3 %collective-permute-start.36 = (bf16[2,512,2560]{2,1,0:T(8,128)(2,1)}, bf16[2,512,2560]{2,1,0:T(8,128)(2,1)}, u32[]{:S(2)}, u32[]{:S(2)}) collective-permute-start(bf16[2,512,2560]{2,1,0:T(8,128)(2,1)} %shard_map.213), channel_id=1, source_target_pairs={{0,16},{8,24},{16,0},{24,8},{1,17},{9,25},{17,1},{25,9},{2,18},{10... | collective-permute-start | bytes 15728648 | tf_op jit(solution)/shard_map/ppermute | solution.py:67
  313.2 48.2 %collective-permute-start.32 = (bf16[512,2048]{1,0:T(8,128)(2,1)}, bf16[512,2048]{1,0:T(8,128)(2,1)}, u32[]{:S(2)}, u32[]{:S(2)}) collective-permute-start(bf16[512,2048]{1,0:T(8,128)(2,1)} %get-tuple-element.312.refs_0_), channel_id=1, source_target_pairs={{0,1},{1,0},{2,3},{3,2},{4,5},{5,4},{6,7},{7,6},{8,9},{9,8},{10,11... | collective-permute-start | bytes 6291464 | tf_op jit(solution)/shard_map/ppermute | solution.py:136
  370.7 92.9 %collective-permute-start.35 = (bf16[512,2048]{1,0:T(8,128)(2,1)}, bf16[512,2048]{1,0:T(8,128)(2,1)}, u32[]{:S(2)}, u32[]{:S(2)}) collective-permute-start(bf16[512,2048]{1,0:T(8,128)(2,1)} %get-tuple-element.341), channel_id=1, source_target_pairs={{0,1},{1,0},{2,3},{3,2},{4,5},{5,4},{6,7},{7,6},{8,9},{9,8},{10,11... | collective-permute-start | bytes 6291464 | tf_op jit(solution)/shard_map/ppermute | solution.py:136
  372.1 53.4 %collective-permute-start.38 = (bf16[512,1536]{1,0:T(8,128)(2,1)}, bf16[512,1536]{1,0:T(8,128)(2,1)S(1)}, u32[]{:S(2)}, u32[]{:S(2)}) collective-permute-start(bf16[512,1536]{1,0:T(8,128)(2,1)} %get-tuple-element.328), channel_id=1, source_target_pairs={{0,8},{8,0},{16,24},{24,16},{1,9},{9,1},{17,25},{25,17},{2,10},{10... | collective-permute-start | bytes 4718600 | tf_op jit(solution)/shard_map/ppermute | solution.py:70
  372.1 53.4 %collective-permute-start.37 = (bf16[512,1536]{1,0:T(8,128)(2,1)}, bf16[512,1536]{1,0:T(8,128)(2,1)S(1)}, u32[]{:S(2)}, u32[]{:S(2)}) collective-permute-start(bf16[512,1536]{1,0:T(8,128)(2,1)} %get-tuple-element.326), channel_id=1, source_target_pairs={{0,8},{8,0},{16,24},{24,16},{1,9},{9,1},{17,25},{25,17},{2,10},{10... | collective-permute-start | bytes 4718600 | tf_op jit(solution)/shard_map/ppermute | solution.py:70
  406.6 57.0 %collective-permute-start.43 = (bf16[2,128,2560]{2,1,0:T(8,128)(2,1)S(1)}, bf16[2,128,2560]{2,1,0:T(8,128)(2,1)S(1)}, u32[]{:S(2)}, u32[]{:S(2)}) collective-permute-start(bf16[2,128,2560]{2,1,0:T(8,128)(2,1)S(1)} %get-tuple-element.347), channel_id=1, source_target_pairs={{0,6},{2,0},{4,2},{6,4},{1,7},{3,1},{5,3},{7,5},{8,14},{10,8},{12,... | collective-permute-start | bytes 3932168 | tf_op jit(solution)/shard_map/ppermute | solution.py:64
  423.8 80.7 %collective-permute-start.47 = (bf16[2,512,1536]{2,1,0:T(8,128)(2,1)}, bf16[2,512,1536]{2,1,0:T(8,128)(2,1)}, u32[]{:S(2)}, u32[]{:S(2)}) collective-permute-start(bf16[2,512,1536]{2,1,0:T(8,128)(2,1)} %shard_map.216), channel_id=1, source_target_pairs={{0,16},{8,24},{16,0},{24,8},{1,17},{9,25},{17,1},{25,9},{2,18},{10... | collective-permute-start | bytes 9437192 | tf_op jit(solution)/shard_map/ppermute | solution.py:67
  442.4 67.8 %collective-permute-start.39 = (bf16[512,2048]{1,0:T(8,128)(2,1)}, bf16[512,2048]{1,0:T(8,128)(2,1)}, u32[]{:S(2)}, u32[]{:S(2)}) collective-permute-start(bf16[512,2048]{1,0:T(8,128)(2,1)} %shard_map.221.refs_0_), channel_id=1, source_target_pairs={{0,1},{1,0},{2,3},{3,2},{4,5},{5,4},{6,7},{7,6},{8,9},{9,8},{10,11... | collective-permute-start | bytes 6291464 | tf_op jit(solution)/shard_map/ppermute | solution.py:136
  490.0 81.5 %collective-permute-start.51 = (bf16[2,128,2560]{2,1,0:T(8,128)(2,1)}, bf16[2,128,2560]{2,1,0:T(8,128)(2,1)}, u32[]{:S(2)}, u32[]{:S(2)}) collective-permute-start(bf16[2,128,2560]{2,1,0:T(8,128)(2,1)} %copy-done.46), channel_id=1, source_target_pairs={{0,2},{2,4},{4,6},{6,0},{1,3},{3,5},{5,7},{7,1},{8,10},{10,12},{12... | collective-permute-start | bytes 3932168 | tf_op jit(solution)/shard_map/ppermute | solution.py:64
  510.3 64.5 %collective-permute-start.50 = (bf16[2,128,2560]{2,1,0:T(8,128)(2,1)}, bf16[2,128,2560]{2,1,0:T(8,128)(2,1)}, u32[]{:S(2)}, u32[]{:S(2)}) collective-permute-start(bf16[2,128,2560]{2,1,0:T(8,128)(2,1)} %shard_map.222), channel_id=1, source_target_pairs={{0,6},{2,0},{4,2},{6,4},{1,7},{3,1},{5,3},{7,5},{8,14},{10,8},{12,... | collective-permute-start | bytes 3932168 | tf_op jit(solution)/shard_map/ppermute | solution.py:64
  511.2 56.9 %collective-permute-start.52 = (bf16[2,128,1536]{2,1,0:T(8,128)(2,1)}, bf16[2,128,1536]{2,1,0:T(8,128)(2,1)}, u32[]{:S(2)}, u32[]{:S(2)}) collective-permute-start(bf16[2,128,1536]{2,1,0:T(8,128)(2,1)} %get-tuple-element.385), channel_id=1, source_target_pairs={{0,6},{2,0},{4,2},{6,4},{1,7},{3,1},{5,3},{7,5},{8,14},{10,8},{12,... | collective-permute-start | bytes 2359304 | tf_op jit(solution)/shard_map/ppermute | solution.py:64
  514.0 63.8 %collective-permute-start.48 = (bf16[512,2304]{1,0:T(8,128)(2,1)}, bf16[512,2304]{1,0:T(8,128)(2,1)S(1)}, u32[]{:S(2)}, u32[]{:S(2)}) collective-permute-start(bf16[512,2304]{1,0:T(8,128)(2,1)} %shard_map.230), channel_id=1, source_target_pairs={{0,8},{8,0},{16,24},{24,16},{1,9},{9,1},{17,25},{25,17},{2,10},{10... | collective-permute-start | bytes 7077896 | tf_op jit(solution)/shard_map/ppermute | solution.py:70
  518.0 59.7 %collective-permute-start.49 = (bf16[1,512,2304]{2,1,0:T(8,128)(2,1)}, bf16[1,512,2304]{2,1,0:T(8,128)(2,1)}, u32[]{:S(2)}, u32[]{:S(2)}) collective-permute-start(bf16[1,512,2304]{2,1,0:T(8,128)(2,1)} %shard_map.227), channel_id=1, source_target_pairs={{0,16},{8,24},{16,0},{24,8},{1,17},{9,25},{17,1},{25,9},{2,18},{10... | collective-permute-start | bytes 7077896 | tf_op jit(solution)/shard_map/ppermute | solution.py:67
  571.5 35.7 %collective-permute-start.60 = (bf16[2,128,1536]{2,1,0:T(8,128)(2,1)}, bf16[2,128,1536]{2,1,0:T(8,128)(2,1)S(1)}, u32[]{:S(2)}, u32[]{:S(2)}) collective-permute-start(bf16[2,128,1536]{2,1,0:T(8,128)(2,1)} %shard_map.231), channel_id=1, source_target_pairs={{0,6},{2,0},{4,2},{6,4},{1,7},{3,1},{5,3},{7,5},{8,14},{10,8},{12,... | collective-permute-start | bytes 2359304 | tf_op jit(solution)/shard_map/ppermute | solution.py:64
  580.9 38.2 %collective-permute-start.53 = (bf16[1,128,2304]{2,1,0:T(8,128)(2,1)S(1)}, bf16[1,128,2304]{2,1,0:T(8,128)(2,1)S(1)}, u32[]{:S(2)}, u32[]{:S(2)}) collective-permute-start(bf16[1,128,2304]{2,1,0:T(8,128)(2,1)S(1)} %get-tuple-element.394), channel_id=1, source_target_pairs={{0,2},{2,4},{4,6},{6,0},{1,3},{3,5},{5,7},{7,1},{8,10},{10,12},{12... | collective-permute-start | bytes 1769480 | tf_op jit(solution)/shard_map/ppermute | solution.py:64
  (125 other events, 1400.8 us)
Sparse Core Ops, SparseCore 0:
  32.5 157.1 all-gather.4
  192.0 102.5 all-gather.2
